TPU v7x, 256 devices: a whole 4x4x8 slice. The times are simulated.
256 devices in a mesh: head: 16 (over y_lo, z), query: 16 (over y_hi, x, core).
Axes of the slice: x: 4, y: 4 (y_hi: 2, y_lo: 2; y = y_hi * 2 + y_lo), z: 8, core: 2. Of those that a mesh axis runs over, the one named last changes fastest.
Arguments:
- queries: bfloat16 [16384, 32, 128], P(('query', 'head')), may hold values from -100 to 100
- keys: bfloat16 [16384, 4, 128], P(('query', 'head')), may hold values from -4 to 4
- values: bfloat16 [16384, 4, 128], P(('query', 'head')), may hold values from -6 to 6
- attention_out: bfloat16 [16384, 32, 128], P(('query', 'head')), may hold values from -3 to 3
- out_grad: bfloat16 [16384, 32, 128], P(('query', 'head')), may hold values from -6 to 6
- span_order: int32 [16, 2], replicated, may hold values from 0 to 31, as said below
- doc_lengths: int32 [64], replicated, may hold values from 1 to 512, 16384 in all
Outputs:
- query_grad: bfloat16 [16384, 32, 128], P(('query', 'head'))
- key_grad: bfloat16 [16384, 4, 128], P(('query', 'head'))
- value_grad: bfloat16 [16384, 4, 128], P(('query', 'head'))
Inputs may be any that keep to these rules, and one draw needn't show every extreme that they name: `span_order`: every number from 0 to 31 appears exactly once; the two numbers of a row sum to 31, in either order. `doc_lengths`: the lengths sum to 16384.
All inputs are finite; a program needn't handle non-finite values.
Results may differ from a plain program's by a relative error of at most 0.0058.
Values may be sent and summed in bfloat16 or wider, within the bound.
No kernel may reach another device: no remote copies, remote signals or barrier semaphores. Data moves between devices by JAX's collectives and lax.ppermute only.
A program may use at most 128 MiB of HBM per device.

v0:
```python
import jax
import jax.numpy as jnp
from jax import lax
from jax.sharding import PartitionSpec as P

key_block = 512
masked = -1e30


def positions(span_order, doc_lengths, rows_each):
    span_rows = rows_each // 2
    within = jnp.arange(span_rows, dtype=jnp.int32)
    pos_all = (span_order[:, :, None] * span_rows + within[None, None, :]).reshape(-1)
    doc_ends = jnp.cumsum(doc_lengths)[:-1]
    doc_all = jnp.sum((pos_all[:, None] >= doc_ends[None, :]).astype(jnp.int32), axis=1)
    return (pos_all, doc_all)


def visible(pos_query, doc_query, pos_key, doc_key):
    return (pos_key[None, :] <= pos_query[:, None]) & (doc_key[None, :] == doc_query[:, None])


def skipping(pos_query, doc_query, pos_key, doc_key, compute, totals):
    maybe = jnp.any(
        (pos_query >= jnp.min(pos_key))
        & (doc_query >= jnp.min(doc_key))
        & (doc_query <= jnp.max(doc_key))
    )
    return lax.cond(maybe, compute, lambda running: running, totals)


def tile_scores(query_tile, key_tile, allowed):
    factor = query_tile.shape[-1] ** (-0.5)
    scores = (
        jnp.einsum("rkgd,ckd->kgrc", query_tile, key_tile, preferred_element_type=jnp.float32)
        * factor
    )
    return jnp.where(allowed, scores, masked)


def tile_grads(query_tile, grad_tile, key_tile, value_tile, allowed, log_rows, delta_rows):
    scores = tile_scores(query_tile, key_tile, allowed)
    probability = jnp.where(allowed, jnp.exp(scores - log_rows[..., None]), 0.0)
    grad_prob = jnp.einsum(
        "rkgd,ckd->kgrc", grad_tile, value_tile, preferred_element_type=jnp.float32
    )
    grad_score = (probability * (grad_prob - delta_rows[..., None])).astype(jnp.bfloat16)
    return (probability, grad_score)


def blockwise(totals, pieces, update):
    length = pieces[0].shape[0]

    def advance(number, running):
        row_start = number * key_block
        sliced = tuple(
            (lax.dynamic_slice_in_dim(member, row_start, key_block, 0) for member in pieces)
        )
        return update(running, sliced, row_start)

    return lax.fori_loop(0, length // key_block, advance, totals)


def shards(queries, keys, values, attention_out, out_grad, span_order, doc_lengths):
    head_count = lax.axis_size("head")
    head_copies = max(head_count // keys.shape[1], 1)
    keys_wide = jnp.repeat(keys, head_copies, axis=1)
    values_wide = jnp.repeat(values, head_copies, axis=1)
    delta_tokens = jnp.sum(
        attention_out.astype(jnp.float32) * out_grad.astype(jnp.float32), axis=-1
    )
    query_here, grad_here, key_here, value_here = (
        lax.all_to_all(queries, "head", split_axis=1, concat_axis=0, tiled=True),
        lax.all_to_all(out_grad, "head", split_axis=1, concat_axis=0, tiled=True),
        lax.all_to_all(keys_wide, "head", split_axis=1, concat_axis=0, tiled=True),
        lax.all_to_all(values_wide, "head", split_axis=1, concat_axis=0, tiled=True),
    )
    delta_here = lax.all_to_all(delta_tokens, "head", split_axis=1, concat_axis=0, tiled=True)
    rows_each, local_heads, head_dim = query_here.shape
    kv_here = key_here.shape[1]
    group_here = local_heads // kv_here
    query_here = query_here.reshape(rows_each, kv_here, group_here, head_dim)
    grad_here = grad_here.reshape(rows_each, kv_here, group_here, head_dim)
    delta = jnp.transpose(delta_here.reshape(rows_each, kv_here, group_here), (1, 2, 0))
    factor = head_dim ** (-0.5)
    pos_all, doc_all = positions(span_order, doc_lengths, rows_each)
    row_first = lax.axis_index("query") * rows_each
    pos_query = lax.dynamic_slice_in_dim(pos_all, row_first, rows_each)
    doc_query = lax.dynamic_slice_in_dim(doc_all, row_first, rows_each)
    stat_shape = (kv_here, group_here, rows_each)

    def key_place(offset, length):
        return (
            lax.dynamic_slice_in_dim(pos_all, offset, length),
            lax.dynamic_slice_in_dim(doc_all, offset, length),
        )

    start_max = jnp.full(stat_shape, masked, jnp.float32)
    start_sum = jnp.zeros(stat_shape, jnp.float32)

    def max_update(totals, pieces, offset):
        key_piece = pieces[0]
        pos_key, doc_key = key_place(offset, key_piece.shape[0])

        def compute(running):
            row_max, row_sum = running
            allowed = visible(pos_query, doc_query, pos_key, doc_key)
            scores = tile_scores(query_here, key_piece, allowed)
            new_max = jnp.maximum(row_max, jnp.max(scores, axis=-1))
            exp_scores = jnp.where(allowed, jnp.exp(scores - new_max[..., None]), 0.0)
            return (new_max, row_sum * jnp.exp(row_max - new_max) + jnp.sum(exp_scores, axis=-1))

        return skipping(pos_query, doc_query, pos_key, doc_key, compute, totals)

    row_max, row_sum = blockwise(
        (start_max, start_sum), (lax.all_gather(key_here, "query", axis=0, tiled=True),), max_update
    )
    log_sum = row_max + jnp.log(row_sum)
    query_zero = jnp.zeros((rows_each, kv_here, group_here, head_dim), jnp.float32)

    def query_update(totals, pieces, offset):
        key_piece, value_piece = (pieces[0], pieces[1])
        pos_key, doc_key = key_place(offset, key_piece.shape[0])

        def compute(running):
            allowed = visible(pos_query, doc_query, pos_key, doc_key)
            probability, grad_score = tile_grads(
                query_here, grad_here, key_piece, value_piece, allowed, log_sum, delta
            )
            return (
                running
                + jnp.einsum(
                    "kgrc,ckd->rkgd", grad_score, key_piece, preferred_element_type=jnp.float32
                )
                * factor
            )

        return skipping(pos_query, doc_query, pos_key, doc_key, compute, totals)

    query_acc = blockwise(
        query_zero,
        (
            lax.all_gather(key_here, "query", axis=0, tiled=True),
            lax.all_gather(value_here, "query", axis=0, tiled=True),
        ),
        query_update,
    )
    log_all, delta_all = (
        lax.all_gather(log_sum, "query", axis=2, tiled=True),
        lax.all_gather(delta, "query", axis=2, tiled=True),
    )

    def key_update(totals, pieces, offset):
        query_piece, grad_piece = pieces
        length = query_piece.shape[0]
        pos_piece, doc_piece = key_place(offset, length)
        log_piece = lax.dynamic_slice_in_dim(log_all, offset, length, 2)
        delta_piece = lax.dynamic_slice_in_dim(delta_all, offset, length, 2)

        def compute(running):
            key_acc, value_acc = running
            allowed = visible(pos_piece, doc_piece, pos_query, doc_query)
            probability, grad_score = tile_grads(
                query_piece, grad_piece, key_here, value_here, allowed, log_piece, delta_piece
            )
            key_acc = (
                key_acc
                + jnp.einsum(
                    "kgrc,rkgd->ckd", grad_score, query_piece, preferred_element_type=jnp.float32
                )
                * factor
            )
            value_acc = value_acc + jnp.einsum(
                "kgrc,rkgd->ckd",
                probability.astype(jnp.bfloat16),
                grad_piece,
                preferred_element_type=jnp.float32,
            )
            return (key_acc, value_acc)

        return skipping(pos_piece, doc_piece, pos_query, doc_query, compute, totals)

    key_zero = jnp.zeros((rows_each, kv_here, head_dim), jnp.float32)
    key_acc, value_acc = blockwise(
        (key_zero, key_zero),
        (
            lax.all_gather(query_here, "query", axis=0, tiled=True),
            lax.all_gather(grad_here, "query", axis=0, tiled=True),
        ),
        key_update,
    )
    query_low = query_acc.reshape(rows_each, local_heads, head_dim).astype(jnp.bfloat16)
    query_rows, key_rows, value_rows = (
        lax.all_to_all(query_low, "head", split_axis=0, concat_axis=1, tiled=True),
        lax.all_to_all(
            key_acc.astype(jnp.bfloat16), "head", split_axis=0, concat_axis=1, tiled=True
        ),
        lax.all_to_all(
            value_acc.astype(jnp.bfloat16), "head", split_axis=0, concat_axis=1, tiled=True
        ),
    )
    row_count = key_rows.shape[0]
    key_grad = (
        key_rows.astype(jnp.float32)
        .reshape(row_count, -1, head_copies, head_dim)
        .sum(axis=2)
        .astype(jnp.bfloat16)
    )
    value_grad = (
        value_rows.astype(jnp.float32)
        .reshape(row_count, -1, head_copies, head_dim)
        .sum(axis=2)
        .astype(jnp.bfloat16)
    )
    return (query_rows, key_grad, value_grad)


def solution(mesh):
    return jax.shard_map(
        shards,
        mesh=mesh,
        in_specs=(
            P(("query", "head"), None, None),
            P(("query", "head"), None, None),
            P(("query", "head"), None, None),
            P(("query", "head"), None, None),
            P(("query", "head"), None, None),
            P(),
            P(),
        ),
        out_specs=(
            P(("query", "head"), None, None),
            P(("query", "head"), None, None),
            P(("query", "head"), None, None),
        ),
        check_vma=False,
    )
```

profile of v0, /device:TPU:1, one launch (start us, length us, event | category | flops | bytes accessed | tf_op | source)
XLA Modules:
  0.0 979.7 jit_solution(7660886381065516041)
XLA Ops:
  8.2 18.8 %all_to_all.136 = bf16[64,16,128]{2,0,1:T(8,128)(2,1)} all-to-all(bf16[64,16,128]{2,0,1:T(8,128)(2,1)S(1)} %bitcast.282), channel_id=1, replica_groups=mesh['head'=16,'query'=16] {'head'}, dimensions={1} | all-to-all | bytes 524288 | tf_op jit(solution)/shard_map/all_to_all | solution.py:75
  28.0 13.2 %all_to_all.137 = bf16[64,16,128]{2,0,1:T(8,128)(2,1)} all-to-all(bf16[64,16,128]{2,0,1:T(8,128)(2,1)S(1)} %bitcast.283), channel_id=1, replica_groups=mesh['head'=16,'query'=16] {'head'}, dimensions={1} | all-to-all | bytes 524288 | tf_op jit(solution)/shard_map/all_to_all | solution.py:76
  42.6 19.0 %all_to_all.138 = bf16[64,32,128]{2,0,1:T(8,128)(2,1)S(1)} all-to-all(bf16[64,32,128]{2,0,1:T(8,128)(2,1)S(1)} %copy.79), channel_id=1, replica_groups=mesh['head'=16,'query'=16] {'head'}, dimensions={1} | all-to-all | bytes 1048576 | tf_op jit(solution)/shard_map/all_to_all | solution.py:73
  97.4 27.5 %all_gather.24 = f32[1,2,16384]{2,1,0:T(2,128)S(1)} all-gather(f32[1,2,1024]{2,1,0:T(2,128)S(1)} %bitcast.290), channel_id=1, replica_groups=mesh['head'=16,'query'=16] {'query'}, dimensions={2}, use_global_device_ids=true | all-gather | bytes 139264 | tf_op jit(solution)/shard_map/all_gather | solution.py:150
  125.0 133.2 %while.47 = (s32[]{:T(128)}, f32[1,2,1024]{2,1,0:T(2,128)S(1)}, f32[1,2,1024]{2,1,0:T(2,128)S(1)}, s32[16384]{0:T(1024)S(1)}, s32[1024]{0:T(1024)S(1)}, /*index=...) while((s32[]{:T(128)}, f32[1,2,1024]{2,1,0:T(2,128)S(1)}, ...), condition=%wide.region_11.12_spmd, body=%wide.region_2.11_spmd.sunk | while | flops 278408704 | bytes 10752837 | solution.py:61
  258.3 148.0 %while.48 = (s32[]{:T(128)}, f32[1024,1,2,128]{0,3,2,1:T(8,128)S(1)}, s32[16384]{0:T(1024)S(1)}, s32[1024]{0:T(1024)S(1)}, s32[16384]{0:T(1024)S(1)}, /*index=5*...) while((s32[]{:T(128)}, ...), condition=%wide.region_20.21_spmd, body=%wide.region_13.20_spmd.sunk | while | flops 814751232 | bytes 13023061 | solution.py:61
  411.1 32.0 %all_gather.22 = f32[1,2,16384]{2,1,0:T(2,128)S(1)} all-gather(f32[1,2,1024]{2,1,0:T(2,128)S(1)} %get-tuple-element.1481), channel_id=1, replica_groups=mesh['head'=16,'query'=16] {'query'}, dimensions={2}, use_global_device_ids=true | all-gather | bytes 139264 | tf_op jit(solution)/shard_map/all_gather | solution.py:149
  443.3 498.8 %while.49 = (s32[]{:T(128)}, f32[1024,1,128]{0,2,1:T(8,128)S(1)}, f32[1024,1,128]{0,2,1:T(8,128)S(1)}, s32[16384]{0:T(1024)S(1)}, s32[]{:T(128)}, /*index=5*/s32...) while((s32[]{:T(128)}, f32[1024,1,128]{0,2,1:T(8,128)S(1)}, ...), condition=%wide.region_28.29_spmd, body=%wide.region_24.28_spmd.sunk | while | flops 1088293888 | bytes 17877396 | solution.py:61
  446.5 12.4 %conditional.8 = ((f32[1024,1,128]{0,2,1:T(8,128)S(1)}, f32[1024,1,128]{0,2,1:T(8,128)S(1)})) conditional(s32[]{:T(128)} %convert_element_type.114, (f32[1024,1,128]{0,2,1:T(8,128)S(1)}, f32[1024,1,128]{0,2,1:T(8,128)S(1)}) %tuple.152, (bf16[16384,1,2,128]{3,0,2,1:T(8,128)(2,1)}, s32[]{:T(128)}, s32[1024]{0:T(1024)S(1)}, s32[512]{0:T(512)S(1)}, ...), branch_computations={%region_26.26_spmd, %region_27.27_spmd} | conditional | flops 1088290816 | bytes 17868828 | solution.py:29
  462.1 12.4 %conditional.8 = ((f32[1024,1,128]{0,2,1:T(8,128)S(1)}, f32[1024,1,128]{0,2,1:T(8,128)S(1)})) conditional(s32[]{:T(128)} %convert_element_type.114, (f32[1024,1,128]{0,2,1:T(8,128)S(1)}, f32[1024,1,128]{0,2,1:T(8,128)S(1)}) %tuple.152, (bf16[16384,1,2,128]{3,0,2,1:T(8,128)(2,1)}, s32[]{:T(128)}, s32[1024]{0:T(1024)S(1)}, s32[512]{0:T(512)S(1)}, ...), branch_computations={%region_26.26_spmd, %region_27.27_spmd} | conditional | flops 1088290816 | bytes 17868828 | solution.py:29
  477.7 12.4 %conditional.8 = ((f32[1024,1,128]{0,2,1:T(8,128)S(1)}, f32[1024,1,128]{0,2,1:T(8,128)S(1)})) conditional(s32[]{:T(128)} %convert_element_type.114, (f32[1024,1,128]{0,2,1:T(8,128)S(1)}, f32[1024,1,128]{0,2,1:T(8,128)S(1)}) %tuple.152, (bf16[16384,1,2,128]{3,0,2,1:T(8,128)(2,1)}, s32[]{:T(128)}, s32[1024]{0:T(1024)S(1)}, s32[512]{0:T(512)S(1)}, ...), branch_computations={%region_26.26_spmd, %region_27.27_spmd} | conditional | flops 1088290816 | bytes 17868828 | solution.py:29
  493.3 12.4 %conditional.8 = ((f32[1024,1,128]{0,2,1:T(8,128)S(1)}, f32[1024,1,128]{0,2,1:T(8,128)S(1)})) conditional(s32[]{:T(128)} %convert_element_type.114, (f32[1024,1,128]{0,2,1:T(8,128)S(1)}, f32[1024,1,128]{0,2,1:T(8,128)S(1)}) %tuple.152, (bf16[16384,1,2,128]{3,0,2,1:T(8,128)(2,1)}, s32[]{:T(128)}, s32[1024]{0:T(1024)S(1)}, s32[512]{0:T(512)S(1)}, ...), branch_computations={%region_26.26_spmd, %region_27.27_spmd} | conditional | flops 1088290816 | bytes 17868828 | solution.py:29
  524.5 12.4 %conditional.8 = ((f32[1024,1,128]{0,2,1:T(8,128)S(1)}, f32[1024,1,128]{0,2,1:T(8,128)S(1)})) conditional(s32[]{:T(128)} %convert_element_type.114, (f32[1024,1,128]{0,2,1:T(8,128)S(1)}, f32[1024,1,128]{0,2,1:T(8,128)S(1)}) %tuple.152, (bf16[16384,1,2,128]{3,0,2,1:T(8,128)(2,1)}, s32[]{:T(128)}, s32[1024]{0:T(1024)S(1)}, s32[512]{0:T(512)S(1)}, ...), branch_computations={%region_26.26_spmd, %region_27.27_spmd} | conditional | flops 1088290816 | bytes 17868828 | solution.py:29
  540.1 12.4 %conditional.8 = ((f32[1024,1,128]{0,2,1:T(8,128)S(1)}, f32[1024,1,128]{0,2,1:T(8,128)S(1)})) conditional(s32[]{:T(128)} %convert_element_type.114, (f32[1024,1,128]{0,2,1:T(8,128)S(1)}, f32[1024,1,128]{0,2,1:T(8,128)S(1)}) %tuple.152, (bf16[16384,1,2,128]{3,0,2,1:T(8,128)(2,1)}, s32[]{:T(128)}, s32[1024]{0:T(1024)S(1)}, s32[512]{0:T(512)S(1)}, ...), branch_computations={%region_26.26_spmd, %region_27.27_spmd} | conditional | flops 1088290816 | bytes 17868828 | solution.py:29
  555.7 12.4 %conditional.8 = ((f32[1024,1,128]{0,2,1:T(8,128)S(1)}, f32[1024,1,128]{0,2,1:T(8,128)S(1)})) conditional(s32[]{:T(128)} %convert_element_type.114, (f32[1024,1,128]{0,2,1:T(8,128)S(1)}, f32[1024,1,128]{0,2,1:T(8,128)S(1)}) %tuple.152, (bf16[16384,1,2,128]{3,0,2,1:T(8,128)(2,1)}, s32[]{:T(128)}, s32[1024]{0:T(1024)S(1)}, s32[512]{0:T(512)S(1)}, ...), branch_computations={%region_26.26_spmd, %region_27.27_spmd} | conditional | flops 1088290816 | bytes 17868828 | solution.py:29
  571.2 12.4 %conditional.8 = ((f32[1024,1,128]{0,2,1:T(8,128)S(1)}, f32[1024,1,128]{0,2,1:T(8,128)S(1)})) conditional(s32[]{:T(128)} %convert_element_type.114, (f32[1024,1,128]{0,2,1:T(8,128)S(1)}, f32[1024,1,128]{0,2,1:T(8,128)S(1)}) %tuple.152, (bf16[16384,1,2,128]{3,0,2,1:T(8,128)(2,1)}, s32[]{:T(128)}, s32[1024]{0:T(1024)S(1)}, s32[512]{0:T(512)S(1)}, ...), branch_computations={%region_26.26_spmd, %region_27.27_spmd} | conditional | flops 1088290816 | bytes 17868828 | solution.py:29
  602.4 12.4 %conditional.8 = ((f32[1024,1,128]{0,2,1:T(8,128)S(1)}, f32[1024,1,128]{0,2,1:T(8,128)S(1)})) conditional(s32[]{:T(128)} %convert_element_type.114, (f32[1024,1,128]{0,2,1:T(8,128)S(1)}, f32[1024,1,128]{0,2,1:T(8,128)S(1)}) %tuple.152, (bf16[16384,1,2,128]{3,0,2,1:T(8,128)(2,1)}, s32[]{:T(128)}, s32[1024]{0:T(1024)S(1)}, s32[512]{0:T(512)S(1)}, ...), branch_computations={%region_26.26_spmd, %region_27.27_spmd} | conditional | flops 1088290816 | bytes 17868828 | solution.py:29
  633.6 12.4 %conditional.8 = ((f32[1024,1,128]{0,2,1:T(8,128)S(1)}, f32[1024,1,128]{0,2,1:T(8,128)S(1)})) conditional(s32[]{:T(128)} %convert_element_type.114, (f32[1024,1,128]{0,2,1:T(8,128)S(1)}, f32[1024,1,128]{0,2,1:T(8,128)S(1)}) %tuple.152, (bf16[16384,1,2,128]{3,0,2,1:T(8,128)(2,1)}, s32[]{:T(128)}, s32[1024]{0:T(1024)S(1)}, s32[512]{0:T(512)S(1)}, ...), branch_computations={%region_26.26_spmd, %region_27.27_spmd} | conditional | flops 1088290816 | bytes 17868828 | solution.py:29
  649.2 12.4 %conditional.8 = ((f32[1024,1,128]{0,2,1:T(8,128)S(1)}, f32[1024,1,128]{0,2,1:T(8,128)S(1)})) conditional(s32[]{:T(128)} %convert_element_type.114, (f32[1024,1,128]{0,2,1:T(8,128)S(1)}, f32[1024,1,128]{0,2,1:T(8,128)S(1)}) %tuple.152, (bf16[16384,1,2,128]{3,0,2,1:T(8,128)(2,1)}, s32[]{:T(128)}, s32[1024]{0:T(1024)S(1)}, s32[512]{0:T(512)S(1)}, ...), branch_computations={%region_26.26_spmd, %region_27.27_spmd} | conditional | flops 1088290816 | bytes 17868828 | solution.py:29
  664.8 12.4 %conditional.8 = ((f32[1024,1,128]{0,2,1:T(8,128)S(1)}, f32[1024,1,128]{0,2,1:T(8,128)S(1)})) conditional(s32[]{:T(128)} %convert_element_type.114, (f32[1024,1,128]{0,2,1:T(8,128)S(1)}, f32[1024,1,128]{0,2,1:T(8,128)S(1)}) %tuple.152, (bf16[16384,1,2,128]{3,0,2,1:T(8,128)(2,1)}, s32[]{:T(128)}, s32[1024]{0:T(1024)S(1)}, s32[512]{0:T(512)S(1)}, ...), branch_computations={%region_26.26_spmd, %region_27.27_spmd} | conditional | flops 1088290816 | bytes 17868828 | solution.py:29
  680.4 12.4 %conditional.8 = ((f32[1024,1,128]{0,2,1:T(8,128)S(1)}, f32[1024,1,128]{0,2,1:T(8,128)S(1)})) conditional(s32[]{:T(128)} %convert_element_type.114, (f32[1024,1,128]{0,2,1:T(8,128)S(1)}, f32[1024,1,128]{0,2,1:T(8,128)S(1)}) %tuple.152, (bf16[16384,1,2,128]{3,0,2,1:T(8,128)(2,1)}, s32[]{:T(128)}, s32[1024]{0:T(1024)S(1)}, s32[512]{0:T(512)S(1)}, ...), branch_computations={%region_26.26_spmd, %region_27.27_spmd} | conditional | flops 1088290816 | bytes 17868828 | solution.py:29
  711.5 12.4 %conditional.8 = ((f32[1024,1,128]{0,2,1:T(8,128)S(1)}, f32[1024,1,128]{0,2,1:T(8,128)S(1)})) conditional(s32[]{:T(128)} %convert_element_type.114, (f32[1024,1,128]{0,2,1:T(8,128)S(1)}, f32[1024,1,128]{0,2,1:T(8,128)S(1)}) %tuple.152, (bf16[16384,1,2,128]{3,0,2,1:T(8,128)(2,1)}, s32[]{:T(128)}, s32[1024]{0:T(1024)S(1)}, s32[512]{0:T(512)S(1)}, ...), branch_computations={%region_26.26_spmd, %region_27.27_spmd} | conditional | flops 1088290816 | bytes 17868828 | solution.py:29
  727.1 12.4 %conditional.8 = ((f32[1024,1,128]{0,2,1:T(8,128)S(1)}, f32[1024,1,128]{0,2,1:T(8,128)S(1)})) conditional(s32[]{:T(128)} %convert_element_type.114, (f32[1024,1,128]{0,2,1:T(8,128)S(1)}, f32[1024,1,128]{0,2,1:T(8,128)S(1)}) %tuple.152, (bf16[16384,1,2,128]{3,0,2,1:T(8,128)(2,1)}, s32[]{:T(128)}, s32[1024]{0:T(1024)S(1)}, s32[512]{0:T(512)S(1)}, ...), branch_computations={%region_26.26_spmd, %region_27.27_spmd} | conditional | flops 1088290816 | bytes 17868828 | solution.py:29
  742.7 12.4 %conditional.8 = ((f32[1024,1,128]{0,2,1:T(8,128)S(1)}, f32[1024,1,128]{0,2,1:T(8,128)S(1)})) conditional(s32[]{:T(128)} %convert_element_type.114, (f32[1024,1,128]{0,2,1:T(8,128)S(1)}, f32[1024,1,128]{0,2,1:T(8,128)S(1)}) %tuple.152, (bf16[16384,1,2,128]{3,0,2,1:T(8,128)(2,1)}, s32[]{:T(128)}, s32[1024]{0:T(1024)S(1)}, s32[512]{0:T(512)S(1)}, ...), branch_computations={%region_26.26_spmd, %region_27.27_spmd} | conditional | flops 1088290816 | bytes 17868828 | solution.py:29
  758.3 12.4 %conditional.8 = ((f32[1024,1,128]{0,2,1:T(8,128)S(1)}, f32[1024,1,128]{0,2,1:T(8,128)S(1)})) conditional(s32[]{:T(128)} %convert_element_type.114, (f32[1024,1,128]{0,2,1:T(8,128)S(1)}, f32[1024,1,128]{0,2,1:T(8,128)S(1)}) %tuple.152, (bf16[16384,1,2,128]{3,0,2,1:T(8,128)(2,1)}, s32[]{:T(128)}, s32[1024]{0:T(1024)S(1)}, s32[512]{0:T(512)S(1)}, ...), branch_computations={%region_26.26_spmd, %region_27.27_spmd} | conditional | flops 1088290816 | bytes 17868828 | solution.py:29
  789.5 12.4 %conditional.8 = ((f32[1024,1,128]{0,2,1:T(8,128)S(1)}, f32[1024,1,128]{0,2,1:T(8,128)S(1)})) conditional(s32[]{:T(128)} %convert_element_type.114, (f32[1024,1,128]{0,2,1:T(8,128)S(1)}, f32[1024,1,128]{0,2,1:T(8,128)S(1)}) %tuple.152, (bf16[16384,1,2,128]{3,0,2,1:T(8,128)(2,1)}, s32[]{:T(128)}, s32[1024]{0:T(1024)S(1)}, s32[512]{0:T(512)S(1)}, ...), branch_computations={%region_26.26_spmd, %region_27.27_spmd} | conditional | flops 1088290816 | bytes 17868828 | solution.py:29
  820.6 12.4 %conditional.8 = ((f32[1024,1,128]{0,2,1:T(8,128)S(1)}, f32[1024,1,128]{0,2,1:T(8,128)S(1)})) conditional(s32[]{:T(128)} %convert_element_type.114, (f32[1024,1,128]{0,2,1:T(8,128)S(1)}, f32[1024,1,128]{0,2,1:T(8,128)S(1)}) %tuple.152, (bf16[16384,1,2,128]{3,0,2,1:T(8,128)(2,1)}, s32[]{:T(128)}, s32[1024]{0:T(1024)S(1)}, s32[512]{0:T(512)S(1)}, ...), branch_computations={%region_26.26_spmd, %region_27.27_spmd} | conditional | flops 1088290816 | bytes 17868828 | solution.py:29
  836.2 12.4 %conditional.8 = ((f32[1024,1,128]{0,2,1:T(8,128)S(1)}, f32[1024,1,128]{0,2,1:T(8,128)S(1)})) conditional(s32[]{:T(128)} %convert_element_type.114, (f32[1024,1,128]{0,2,1:T(8,128)S(1)}, f32[1024,1,128]{0,2,1:T(8,128)S(1)}) %tuple.152, (bf16[16384,1,2,128]{3,0,2,1:T(8,128)(2,1)}, s32[]{:T(128)}, s32[1024]{0:T(1024)S(1)}, s32[512]{0:T(512)S(1)}, ...), branch_computations={%region_26.26_spmd, %region_27.27_spmd} | conditional | flops 1088290816 | bytes 17868828 | solution.py:29
  851.8 12.4 %conditional.8 = ((f32[1024,1,128]{0,2,1:T(8,128)S(1)}, f32[1024,1,128]{0,2,1:T(8,128)S(1)})) conditional(s32[]{:T(128)} %convert_element_type.114, (f32[1024,1,128]{0,2,1:T(8,128)S(1)}, f32[1024,1,128]{0,2,1:T(8,128)S(1)}) %tuple.152, (bf16[16384,1,2,128]{3,0,2,1:T(8,128)(2,1)}, s32[]{:T(128)}, s32[1024]{0:T(1024)S(1)}, s32[512]{0:T(512)S(1)}, ...), branch_computations={%region_26.26_spmd, %region_27.27_spmd} | conditional | flops 1088290816 | bytes 17868828 | solution.py:29
  867.4 12.4 %conditional.8 = ((f32[1024,1,128]{0,2,1:T(8,128)S(1)}, f32[1024,1,128]{0,2,1:T(8,128)S(1)})) conditional(s32[]{:T(128)} %convert_element_type.114, (f32[1024,1,128]{0,2,1:T(8,128)S(1)}, f32[1024,1,128]{0,2,1:T(8,128)S(1)}) %tuple.152, (bf16[16384,1,2,128]{3,0,2,1:T(8,128)(2,1)}, s32[]{:T(128)}, s32[1024]{0:T(1024)S(1)}, s32[512]{0:T(512)S(1)}, ...), branch_computations={%region_26.26_spmd, %region_27.27_spmd} | conditional | flops 1088290816 | bytes 17868828 | solution.py:29
  898.6 12.4 %conditional.8 = ((f32[1024,1,128]{0,2,1:T(8,128)S(1)}, f32[1024,1,128]{0,2,1:T(8,128)S(1)})) conditional(s32[]{:T(128)} %convert_element_type.114, (f32[1024,1,128]{0,2,1:T(8,128)S(1)}, f32[1024,1,128]{0,2,1:T(8,128)S(1)}) %tuple.152, (bf16[16384,1,2,128]{3,0,2,1:T(8,128)(2,1)}, s32[]{:T(128)}, s32[1024]{0:T(1024)S(1)}, s32[512]{0:T(512)S(1)}, ...), branch_computations={%region_26.26_spmd, %region_27.27_spmd} | conditional | flops 1088290816 | bytes 17868828 | solution.py:29
  929.8 12.4 %conditional.8 = ((f32[1024,1,128]{0,2,1:T(8,128)S(1)}, f32[1024,1,128]{0,2,1:T(8,128)S(1)})) conditional(s32[]{:T(128)} %convert_element_type.114, (f32[1024,1,128]{0,2,1:T(8,128)S(1)}, f32[1024,1,128]{0,2,1:T(8,128)S(1)}) %tuple.152, (bf16[16384,1,2,128]{3,0,2,1:T(8,128)(2,1)}, s32[]{:T(128)}, s32[1024]{0:T(1024)S(1)}, s32[512]{0:T(512)S(1)}, ...), branch_computations={%region_26.26_spmd, %region_27.27_spmd} | conditional | flops 1088290816 | bytes 17868828 | solution.py:29
  (511 shorter events, 924.6 us)
Async XLA Ops:
  7.2 55.3 %copy-start.2 = (bf16[64,32,128]{2,1,0:T(8,128)(2,1)S(1)}, bf16[64,32,128]{2,1,0:T(8,128)(2,1)}, u32[]{:S(2)}) copy-start(bf16[64,32,128]{2,1,0:T(8,128)(2,1)} %param.23) | copy-start | bytes 1572868
  7.2 62.4 %copy-start.5 = (bf16[64,32,128]{2,1,0:T(8,128)(2,1)S(1)}, bf16[64,32,128]{2,1,0:T(8,128)(2,1)}, u32[]{:S(2)}) copy-start(bf16[64,32,128]{2,1,0:T(8,128)(2,1)} %param.22) | copy-start | bytes 1572868
  7.2 117.8 %all-gather.5.cloned.1.call-start = ((), (), s32[]{:S(2)}) async-start(), calls=%async_computation.8 | async-start | bytes 4456448 | tf_op jit(solution)/shard_map/all_gather | solution.py:143
  27.0 231.2 %all-gather.7.cloned.1.call-start = ((), (), s32[]{:S(2)}) async-start(), calls=%async_computation.9 | async-start | bytes 4456448 | tf_op jit(solution)/shard_map/all_gather | solution.py:144
  41.3 48.5 %copy-start.6 = (s32[16,2]{0,1:T(2,128)S(1)}, s32[16,2]{0,1:T(2,128)}, u32[]{:S(2)}) copy-start(s32[16,2]{0,1:T(2,128)} %param.24) | copy-start | bytes 388
  41.3 48.7 %copy-start.7 = (s32[64]{0:T(128)S(1)}, s32[64]{0:T(128)}, u32[]{:S(2)}) copy-start(s32[64]{0:T(128)} %param.25) | copy-start | bytes 772
  41.3 401.9 %all-gather.9.cloned.1.call-start = ((), (), s32[]{:S(2)}) async-start(), calls=%async_computation.10 | async-start | bytes 8912896 | tf_op jit(solution)/shard_map/all_gather | solution.py:187
  62.5 62.5 %copy-start = (bf16[16,64,2,128]{3,1,0,2:T(8,128)(2,1)S(1)}, bf16[16,64,2,128]{3,1,0,2:T(8,128)(2,1)}, u32[]{:S(2)}) copy-start(bf16[16,64,2,128]{3,1,0,2:T(8,128)(2,1)} %copy.80) | copy-start | bytes 1572868
  63.6 19.0 %all-to-all-start.3 = ((bf16[64,32,128]{2,0,1:T(8,128)(2,1)}), bf16[64,32,128]{2,0,1:T(8,128)(2,1)S(1)}, u32[]{:S(2)}, u32[]{:S(2)}) async-start(bf16[64,32,128]{2,0,1:T(8,128)(2,1)} %copy.82), calls=%async_computation.3 | async-start | bytes 1048576 | tf_op jit(solution)/shard_map/all_to_all | solution.py:74
  82.6 13.5 %all-to-all-start.4 = ((f32[16,1,128]{2,1,0:T(1,128)}), f32[16,1,128]{2,1,0:T(1,128)S(1)}, u32[]{:S(2)}, u32[]{:S(2)}) async-start(f32[16,1,128]{2,1,0:T(1,128)} %reshape.213), calls=%async_computation.4 | async-start | bytes 16384 | tf_op jit(solution)/shard_map/all_to_all | solution.py:78
  88.8 354.4 %all-gather.11.cloned.1.call-start = ((), (), s32[]{:S(2)}) async-start(), calls=%async_computation.11 | async-start | bytes 8912896 | tf_op jit(solution)/shard_map/all_gather | solution.py:188
  125.0 133.4 %copy-start.3 = (bf16[16,64,2,128]{3,1,0,2:T(8,128)(2,1)S(1)}, bf16[16,64,2,128]{3,1,0,2:T(8,128)(2,1)}, u32[]{:S(2)}) copy-start(bf16[16,64,2,128]{3,1,0,2:T(8,128)(2,1)} %copy.83) | copy-start | bytes 1572868
  406.4 36.9 %copy-start.1 = (bf16[64,16,128]{2,0,1:T(8,128)(2,1)S(1)}, bf16[64,16,128]{2,0,1:T(8,128)(2,1)}, u32[]{:S(2)}) copy-start(bf16[64,16,128]{2,0,1:T(8,128)(2,1)} %all_to_all.136) | copy-start | bytes 786436
  406.4 36.9 %copy-start.4 = (bf16[64,16,128]{2,0,1:T(8,128)(2,1)S(1)}, bf16[64,16,128]{2,0,1:T(8,128)(2,1)}, u32[]{:S(2)}) copy-start(bf16[64,16,128]{2,0,1:T(8,128)(2,1)} %all_to_all.137) | copy-start | bytes 786436
  407.6 536.8 %all-to-all-start.5 = ((bf16[1024,2,128]{2,1,0:T(2,128)(2,1)}), bf16[1024,2,128]{2,1,0:T(2,128)(2,1)S(1)}, u32[]{:S(2)}, u32[]{:S(2)}) async-start(bf16[1024,2,128]{2,1,0:T(2,128)(2,1)} %bitcast.64), calls=%async_computation.5 | async-start | bytes 1048576 | tf_op jit(solution)/shard_map/all_to_all | solution.py:194
  944.4 15.9 %all-to-all-start.6 = ((bf16[16,2,4096]{2,1,0:T(2,128)(2,1)}), bf16[16,2,4096]{2,1,0:T(2,128)(2,1)S(1)}, u32[]{:S(2)}, u32[]{:S(2)}) async-start(bf16[16,2,4096]{2,1,0:T(2,128)(2,1)} %reshape.215), calls=%async_computation.6 | async-start | bytes 524288 | tf_op jit(solution)/shard_map/all_to_all | solution.py:195
  960.3 11.8 %all-to-all-start.7 = ((bf16[16,2,4096]{2,1,0:T(2,128)(2,1)}), bf16[16,2,4096]{2,1,0:T(2,128)(2,1)S(1)}, u32[]{:S(2)}, u32[]{:S(2)}) async-start(bf16[16,2,4096]{2,1,0:T(2,128)(2,1)} %reshape.217), calls=%async_computation.7 | async-start | bytes 524288 | tf_op jit(solution)/shard_map/all_to_all | solution.py:198
Sparse Core Ops, SparseCore 0:
  27.2 65.1 all-gather.4
  95.0 62.2 all-gather.6
  160.7 76.6 all-gather.8
  240.0 75.7 all-gather.10
where the time goes:
time: 986 us; the launch traced here: 980 us
  matrix products  408 us (41%)
  other arithmetic  310 us (31%)
  blocking collectives  111 us (11%)
  loops' own time  66.4 us (7%)
  starting transfers between devices  28.2 us (3%)
  waiting for transfers between devices  27.8 us (3%)
  local copies, waits for them, and re-layouts  14.9 us (2%)
  between operations  14.2 us (1%)
    reduce_or x96, other arithmetic, skipping(): jnp.any((pos_query >= jnp.min(pos_key)) & (doc_query >= jnp.min(doc_key))...  235 us
    dot_general x32, matrix products, compute(): jnp.einsum('kgrc,rkgd->ckd', grad_score, query_piece, preferred_element_t...  143 us
    dot_general x38, matrix products, tile_scores(): jnp.einsum('rkgd,ckd->kgrc', query_tile, key_tile, preferred_element_type...  132 us
    dot_general x32, matrix products, compute(): jnp.einsum('kgrc,rkgd->ckd', probability.astype(jnp.bfloat16), grad_piece...  120 us
    another operation x3, loops' own time, blockwise(): return lax.fori_loop(0, length // key_block, advance, totals)  64 us
    reduce_min x64, other arithmetic, skipping(): jnp.min(doc_key)  47.9 us
    all_gather x1, blocking collectives, shards(): lax.all_gather(log_sum, 'query', axis=2, tiled=True)  32 us
    all_gather x1, blocking collectives, shards(): lax.all_gather(delta, 'query', axis=2, tiled=True)  27.5 us
  transfers between devices with their start and end apart: 9, of which 4 were waited for; matrix products, arithmetic and copies ran while one was open for 75% of the time, Pallas kernels for 0%

commit v1 on v0

v1 whole, which is shorter than its diff:
```python
import jax
import jax.numpy as jnp
from jax import lax
from jax.experimental import pallas as pl
from jax.experimental.pallas import tpu as pltpu
from jax.sharding import Mesh, PartitionSpec as P

span = 512
chunk = 64
group = 8
width = 128
kv_heads = 4
heads = 32
window = span + chunk
columns = chunk * group
row_axes = ("yh", "x", "c", "yl", "z")
plane_axes = ("yl", "yh", "x", "c")
all_axes = ("z", "yl", "yh", "x", "c")
masked = -1e30
log2e = 1.4426950408889634
factor = width ** -0.5


def place_spans(order_ref, place_ref):
    def put(p, carry):
        place_ref[order_ref[p % 16, p // 16]] = p
        return carry

    lax.fori_loop(0, 32, put, 0)


def expand_kernel(order_ref, meta_ref, pieces_ref, out_ref, place_ref):
    place_spans(order_ref, place_ref)
    z = meta_ref[2]

    def fill(p, carry):
        before = place_ref[jnp.maximum(order_ref[p % 16, p // 16] - 1, 0)]
        own = pieces_ref[p]
        prev = pieces_ref[before]
        for j in range(8):
            @pl.when(j > z)
            def _():
                out_ref[j, p] = own

            @pl.when(j <= z)
            def _():
                out_ref[j, p] = prev
        return carry

    lax.fori_loop(0, 32, fill, 0)


def reduce_kernel(order_ref, meta_ref, parts_ref, out_ref, place_ref, own_ref, prev_ref):
    place_spans(order_ref, place_ref)
    z = meta_ref[2]

    def add(p, carry):
        own = jnp.zeros((16, width), jnp.float32)
        prev = jnp.zeros((16, width), jnp.float32)
        for j in range(8):
            part = parts_ref[j, p].astype(jnp.float32)
            own = own + jnp.where(j > z, part, 0.0)
            prev = prev + jnp.where(j > z, 0.0, part)
        own_ref[p] = own
        prev_ref[p] = prev
        return carry

    lax.fori_loop(0, 32, add, 0)

    def merge(p, carry):
        here = order_ref[p % 16, p // 16]
        after = place_ref[jnp.minimum(here + 1, 31)]
        out_ref[p] = own_ref[p] + jnp.where(here < 31, prev_ref[after], 0.0)
        return carry

    lax.fori_loop(0, 32, merge, 0)


def attention_kernel(
    order_ref,
    lengths_ref,
    meta_ref,
    query_ref,
    grad_ref,
    out_ref,
    window_ref,
    own_ref,
    query_grad_ref,
    window_grad_ref,
    own_grad_ref,
    bias_ref,
    query_acc_ref,
):
    place = meta_ref[2]
    current = order_ref[meta_ref[0], meta_ref[1]]
    base = (current - 1) * span
    token = lax.shift_right_logical(
        lax.broadcasted_iota(jnp.int32, (1, columns), 1), 3
    )
    last = span + place * chunk + token

    def doc(i, carry):
        end, low = carry
        end = end + lengths_ref[i]
        return end, jnp.where(end <= last, jnp.maximum(low, end), low)

    first_end = jnp.int32(0) - base
    low_start = jnp.zeros((1, columns), jnp.int32) + first_end
    _, low = lax.fori_loop(0, 63, doc, (first_end, low_start))
    row = lax.broadcasted_iota(jnp.int32, (window, columns), 0)
    key_at = jnp.where(
        row >= span,
        row + place * chunk,
        jnp.where(lax.shift_right_logical(row, 6) >= place, row, row + span),
    )
    allowed = (key_at <= last) & (key_at >= low)
    bias_ref[...] = jnp.where(allowed, 0.0, masked)
    ones = jnp.ones((8, width), jnp.bfloat16)

    def nt(a, b):
        return lax.dot_general(
            a, b, (((1,), (1,)), ((), ())), preferred_element_type=jnp.float32
        )

    for h in range(kv_heads):
        cut = slice(h * group, (h + 1) * group)
        query = query_ref[...].astype(jnp.float32)[:, cut].reshape(columns, width)
        grad = grad_ref[...].astype(jnp.float32)[:, cut].reshape(columns, width)
        out = out_ref[...].astype(jnp.float32)[:, cut].reshape(columns, width)
        product = grad * out
        high = product.astype(jnp.bfloat16)
        rest = (product - high.astype(jnp.float32)).astype(jnp.bfloat16)
        delta = (nt(ones, high) + nt(ones, rest))[0:1]
        query = query.astype(jnp.bfloat16)
        grad = grad.astype(jnp.bfloat16)
        key = jnp.concatenate(
            [window_ref[:, h, 0].reshape(span, width), own_ref[h, 0]], axis=0
        )
        value = jnp.concatenate(
            [window_ref[:, h, 1].reshape(span, width), own_ref[h, 1]], axis=0
        )
        scores = nt(key, query) * (factor * log2e) + bias_ref[...]
        top = jnp.max(scores, axis=0, keepdims=True)
        exps = jnp.exp2(scores - top)
        total = jnp.sum(exps, axis=0, keepdims=True)
        probs = exps * (1.0 / total)
        grad_scores = (probs * (nt(value, grad) - delta)).astype(jnp.bfloat16)
        value_part = jnp.dot(
            probs.astype(jnp.bfloat16), grad, preferred_element_type=jnp.float32
        )
        key_part = (
            jnp.dot(grad_scores, query, preferred_element_type=jnp.float32) * factor
        )
        query_part = lax.dot_general(
            key, grad_scores, (((0,), (0,)), ((), ())), preferred_element_type=jnp.float32
        )
        query_acc_ref[:, cut] = (jnp.transpose(query_part) * factor).reshape(
            chunk, group, width
        )
        window_grad_ref[:, h, 0] = key_part[:span].astype(jnp.bfloat16).reshape(8, chunk, width)
        window_grad_ref[:, h, 1] = value_part[:span].astype(jnp.bfloat16).reshape(8, chunk, width)
        own_grad_ref[h, 0] = key_part[span:]
        own_grad_ref[h, 1] = value_part[span:]
    query_grad_ref[...] = query_acc_ref[...].astype(jnp.bfloat16)


vmem = pl.BlockSpec(memory_space=pltpu.VMEM)
smem = pl.BlockSpec(memory_space=pltpu.SMEM)


def shards(queries, keys, values, attention_out, out_grad, span_order, doc_lengths):
    query_index = (lax.axis_index("yh") * 4 + lax.axis_index("x")) * 2 + lax.axis_index("c")
    meta = jnp.stack([query_index, lax.axis_index("yl"), lax.axis_index("z")]).astype(jnp.int32)
    own = jnp.transpose(jnp.stack([keys, values], axis=2), (1, 2, 0, 3))
    pieces = lax.all_to_all(
        own.reshape(32, 16, width), plane_axes, split_axis=0, concat_axis=0, tiled=True
    )
    spread = pl.pallas_call(
        expand_kernel,
        out_shape=jax.ShapeDtypeStruct((8, 32, 16, width), jnp.bfloat16),
        in_specs=[smem, smem, vmem],
        out_specs=vmem,
        scratch_shapes=[pltpu.SMEM((32,), jnp.int32)],
    )(span_order, meta, pieces)
    around = lax.all_to_all(
        spread.reshape(256, 16, width), all_axes, split_axis=0, concat_axis=0, tiled=True
    )
    query_grad, window_grad, own_grad = pl.pallas_call(
        attention_kernel,
        out_shape=(
            jax.ShapeDtypeStruct((chunk, heads, width), jnp.bfloat16),
            jax.ShapeDtypeStruct((8, kv_heads, 2, chunk, width), jnp.bfloat16),
            jax.ShapeDtypeStruct((kv_heads, 2, chunk, width), jnp.float32),
        ),
        in_specs=[smem, smem, smem, vmem, vmem, vmem, vmem, vmem],
        out_specs=(vmem, vmem, vmem),
        scratch_shapes=[
            pltpu.VMEM((window, columns), jnp.float32),
            pltpu.VMEM((chunk, heads, width), jnp.float32),
        ],
    )(
        span_order,
        doc_lengths,
        meta,
        queries,
        out_grad,
        attention_out,
        around.reshape(8, kv_heads, 2, chunk, width),
        own,
    )
    parts = lax.all_to_all(
        window_grad.reshape(256, 16, width), all_axes, split_axis=0, concat_axis=0, tiled=True
    )
    sums = pl.pallas_call(
        reduce_kernel,
        out_shape=jax.ShapeDtypeStruct((32, 16, width), jnp.float32),
        in_specs=[smem, smem, vmem],
        out_specs=vmem,
        scratch_shapes=[
            pltpu.SMEM((32,), jnp.int32),
            pltpu.VMEM((32, 16, width), jnp.float32),
            pltpu.VMEM((32, 16, width), jnp.float32),
        ],
    )(span_order, meta, parts.reshape(8, 32, 16, width))
    back = lax.all_to_all(sums, plane_axes, split_axis=0, concat_axis=0, tiled=True)
    both = own_grad + back.reshape(kv_heads, 2, chunk, width)
    both = jnp.transpose(both, (1, 2, 0, 3)).astype(jnp.bfloat16)
    return query_grad, both[0], both[1]


def solution(mesh):
    fine = Mesh(mesh.devices.reshape(2, 8, 2, 4, 2), ("yl", "z", "yh", "x", "c"))
    rows = P(row_axes, None, None)
    return jax.shard_map(
        shards,
        mesh=fine,
        in_specs=(rows, rows, rows, rows, rows, P(), P()),
        out_specs=(rows, rows, rows),
        check_vma=False,
    )
```

time: 986 us -> 135 us (0.14)
  matrix products: 408 us -> 0 us
  other arithmetic: 310 us -> 1.41 us
  loops' own time: 66.4 us -> 0 us
  waiting for transfers between devices: 27.8 us -> 5.65 us
  starting transfers between devices: 28.2 us -> 8.58 us
  Pallas kernels: 0 us -> 16.9 us
  blocking collectives: 111 us -> 96.6 us
  between operations: 14.2 us -> 0.68 us
  local copies, waits for them, and re-layouts: 14.9 us -> 4.28 us
    dot_general x105 -> x0, matrix products: 408 us -> none  [the longest x32 143 us: compute(): jnp.einsum('kgrc,rkgd->ckd', grad_score, query_piece, preferred_element_t...]
    reduce_or x96 -> x0, other arithmetic: 235 us -> none  [skipping(): jnp.any((pos_query >= jnp.min(pos_key)) & (doc_query >= jnp.min(doc_key))...]
    another operation x99 -> x0, loops' own time: 66.4 us -> none  [the longest x3 64 us: blockwise(): return lax.fori_loop(0, length // key_block, advance, totals)]
    all_gather x2 -> x0, blocking collectives: 59.5 us -> none  [the longest x1 32 us: shards(): lax.all_gather(log_sum, 'query', axis=2, tiled=True)]
    reduce_min x64 -> x0, other arithmetic: 47.9 us -> none  [skipping(): jnp.min(doc_key)]
    all_to_all x3, blocking collectives: 51.1 us -> 96.6 us  [the longest x1 42.7 us: shards(): lax.all_to_all(spread.reshape(256, 16, width), all_axes, split_axis=0, co...]
    all_to_all x5 -> x1, waiting for transfers between devices: 27.7 us -> 5.65 us  [shards(): lax.all_to_all(own.reshape(32, 16, width), plane_axes, split_axis=0, conc...]
    all_to_all x5 -> x1, starting transfers between devices: 28 us -> 8.58 us  [shards(): lax.all_to_all(own.reshape(32, 16, width), plane_axes, split_axis=0, conc...]
  transfers between devices with their start and end apart: 9 -> 1, of which waited for: 4 -> 1; matrix products, arithmetic and copies ran while one was open for 75% -> 1% of each run, Pallas kernels for 0% -> 0%
where the time goes in v1:
time: 135 us; the launch traced here: 134 us
  blocking collectives  96.6 us (72%)
  Pallas kernels  16.9 us (13%)
  starting transfers between devices  8.58 us (6%)
  waiting for transfers between devices  5.65 us (4%)
  local copies, waits for them, and re-layouts  4.28 us (3%)
  other arithmetic  1.41 us (1%)
    all_to_all x1, blocking collectives, shards(): lax.all_to_all(spread.reshape(256, 16, width), all_axes, split_axis=0, co...  42.7 us
    all_to_all x1, blocking collectives, shards(): lax.all_to_all(window_grad.reshape(256, 16, width), all_axes, split_axis=...  39.7 us
    all_to_all x1, blocking collectives, shards(): lax.all_to_all(sums, plane_axes, split_axis=0, concat_axis=0, tiled=True)  14.2 us
    all_to_all x1, starting transfers between devices, shards(): lax.all_to_all(own.reshape(32, 16, width), plane_axes, split_axis=0, conc...  8.58 us
    pallas_call x1, Pallas kernels, shards(): pl.pallas_call(attention_kernel, out_shape=(jax.ShapeDtypeStruct((chunk,...  7.99 us
    all_to_all x1, waiting for transfers between devices, shards(): lax.all_to_all(own.reshape(32, 16, width), plane_axes, split_axis=0, conc...  5.65 us
    pallas_call x1, Pallas kernels, shards(): pl.pallas_call(expand_kernel, out_shape=jax.ShapeDtypeStruct((8, 32, 16,...  5.15 us
    pallas_call x1, Pallas kernels, shards(): pl.pallas_call(reduce_kernel, out_shape=jax.ShapeDtypeStruct((32, 16, wid...  3.8 us
  transfers between devices with their start and end apart: 1, of which 1 were waited for; matrix products, arithmetic and copies ran while one was open for 1% of the time, Pallas kernels for 0%

profile of v1, /device:TPU:1, one launch (start us, length us, event | category | flops | bytes accessed | tf_op | source)
XLA Modules:
  0.0 134.1 jit_solution(6754206139939125999)
XLA Ops:
  0.6 0.9 copy_bitcast_fusion
  1.5 0.7 fusion.1
  2.3 8.6 %all-to-all-start = ((bf16[32,16,128]{2,1,0:T(8,128)(2,1)}), bf16[32,16,128]{2,1,0:T(8,128)(2,1)S(1)}, u32[]{:S(2)}, u32[]{:S(2)}) async-start(bf16[32,16,128]{2,1,0:T(8,128)(2,1)} %bitcast.6), calls=%async_computation | async-start | bytes 262144 | tf_op jit(solution)/shard_map/all_to_all | solution.py:175
  10.8 0.0 copy-start.2
  10.9 0.7 copy-done.2
  11.5 0.7 copy.13.order_ref
  12.2 0.7 pad_add_fusion.meta_ref
  12.9 5.6 %all-to-all-done.pieces_ref = bf16[32,16,128]{2,1,0:T(8,128)(2,1)S(1)} async-done(((bf16[32,16,128]{2,1,0:T(8,128)(2,1)}), bf16[32,16,128]{2,1,0:T(8,128)(2,1)S(1)}, u32[]{:S(2)}, u32[]{:S(2)}) %all-to-all-start) | async-done | bytes 131104 | tf_op jit(solution)/shard_map/all_to_all | solution.py:175
  18.5 0.0 copy-start
  18.5 0.7 copy-done
  19.2 5.2 %shard_map.94 = bf16[8,32,16,128]{3,2,1,0:T(8,128)(2,1)} custom-call(s32[16,2]{1,0:T(8,128)} %copy.13.order_ref, s32[3]{0:T(128)} %pad_add_fusion.meta_ref, bf16[32,16,128]{2,1,0:T(8,128)(2,1)} %copy-done), custom_call_target="tpu_custom_call" | custom-call | tf_op jit(solution)/shard_map/pallas_call | solution.py:178
  24.3 42.7 %all_to_all.20 = bf16[256,16,128]{2,1,0:T(8,128)(2,1)} all-to-all(bf16[256,16,128]{2,1,0:T(8,128)(2,1)} %bitcast.24), channel_id=1, replica_groups=mesh['yl'=2,'z'=8,'yh'=2,'x'=4,'c'=2] {'z','yl','yh','x','c'}, dimensions={0} | all-to-all | bytes 2097152 | tf_op jit(solution)/shard_map/all_to_all | solution.py:185
  67.0 8.0 %shard_map.95 = (bf16[64,32,128]{2,1,0:T(8,128)(2,1)}, bf16[8,4,2,64,128]{4,3,2,1,0:T(8,128)(2,1)}, f32[4,2,64,128]{3,2,1,0:T(8,128)}) custom-call(s32[16,2]{1,0:T(8,128)} %copy.13.order_ref, s32[64]{0:T(128)} %lengths_ref.1, s32[3]{0:T(128)} %pad_add_fusion.meta_ref, bf16[64,32,128]{2,1,0:T(8,128)(2,1)} %query_ref.1, bf16[64,32,128]{2,1,0:T(8,128)(2,1)} %grad_ref.1, ...), custom_call_target="tpu_custom_call" | custom-call | tf_op jit(solution)/shard_map/pallas_call | solution.py:188
  75.0 39.7 %all_to_all.21 = bf16[256,16,128]{2,1,0:T(8,128)(2,1)} all-to-all(bf16[256,16,128]{2,1,0:T(8,128)(2,1)} %bitcast.25), channel_id=1, replica_groups=mesh['yl'=2,'z'=8,'yh'=2,'x'=4,'c'=2] {'z','yl','yh','x','c'}, dimensions={0} | all-to-all | bytes 2097152 | tf_op jit(solution)/shard_map/all_to_all | solution.py:211
  114.7 3.8 %shard_map.96 = f32[32,16,128]{2,1,0:T(8,128)} custom-call(s32[16,2]{1,0:T(8,128)} %copy.13.order_ref, s32[3]{0:T(128)} %pad_add_fusion.meta_ref, bf16[8,32,16,128]{3,2,1,0:T(8,128)(2,1)} %bitcast.23), custom_call_target="tpu_custom_call" | custom-call | tf_op jit(solution)/shard_map/pallas_call | solution.py:214
  118.5 0.0 copy-start.1
  118.5 14.2 %all_to_all.22 = f32[32,16,128]{2,1,0:T(8,128)S(1)} all-to-all(f32[32,16,128]{2,1,0:T(8,128)} %shard_map.96), channel_id=1, replica_groups=mesh['yl'=2,'z'=8,'yh'=2,'x'=4,'c'=2] {'yl','yh','x','c'}, dimensions={0} | all-to-all | bytes 524288 | tf_op jit(solution)/shard_map/all_to_all | solution.py:225
  132.7 0.0 copy-done.1
  132.8 0.7 copy.16
  133.4 0.7 copy.15
  (2 shorter events, 0.0 us)
Async XLA Ops:
  2.3 16.3 %all-to-all-start = ((bf16[32,16,128]{2,1,0:T(8,128)(2,1)}), bf16[32,16,128]{2,1,0:T(8,128)(2,1)S(1)}, u32[]{:S(2)}, u32[]{:S(2)}) async-start(bf16[32,16,128]{2,1,0:T(8,128)(2,1)} %bitcast.6), calls=%async_computation | async-start | bytes 262144 | tf_op jit(solution)/shard_map/all_to_all | solution.py:175
  10.8 0.7 copy-start.2
  18.5 0.7 copy-start
  118.5 14.2 %copy-start.1 = (f32[4,2,64,128]{3,2,1,0:T(8,128)S(1)}, f32[4,2,64,128]{3,2,1,0:T(8,128)}, u32[]{:S(2)}) copy-start(f32[4,2,64,128]{3,2,1,0:T(8,128)} %get-tuple-element.7) | copy-start | bytes 786436

commit v2 on v1

v2 whole, which is shorter than its diff:
```python
import jax
import jax.numpy as jnp
from jax import lax
from jax.experimental import pallas as pl
from jax.experimental.pallas import tpu as pltpu
from jax.sharding import Mesh, PartitionSpec as P


span = 512
chunk = 64
group = 8
width = 128
kv_heads = 4
share = 2
local_kv = kv_heads // share
local_heads = local_kv * group
piece = 16 // share
window = span + share * chunk
columns = chunk * group
row_axes = ("yh", "x", "c", "yl", "z")
plane_axes = ("yl", "yh", "x", "c")
all_axes = ("z", "yl", "yh", "x", "c")
masked = -1e30
log2e = 1.4426950408889634
factor = width ** -0.5


def nt(a, b):
    return lax.dot_general(
        a, b, (((1,), (1,)), ((), ())), preferred_element_type=jnp.float32
    )


def place_spans(order_ref, place_ref):
    for p in range(32):
        place_ref[order_ref[p % 16, p // 16]] = p


def later(j, z):
    return j // share > lax.div(z, share)


def expand_kernel(order_ref, meta_ref, pieces_ref, out_ref, place_ref, prev_ref):
    place_spans(order_ref, place_ref)
    z = meta_ref[2]
    for p in range(32):
        before = place_ref[jnp.maximum(order_ref[p % 16, p // 16] - 1, 0)]
        prev_ref[p] = pieces_ref[before]
    for j in range(8):
        @pl.when(later(j, z))
        def _():
            out_ref[j] = pieces_ref[:, j % share]

        @pl.when(jnp.logical_not(later(j, z)))
        def _():
            out_ref[j] = prev_ref[:, j % share]


def reduce_kernel(order_ref, meta_ref, parts_ref, out_ref, place_ref, own_ref, prev_ref):
    place_spans(order_ref, place_ref)
    z = meta_ref[2]
    for e in range(share):
        own = jnp.zeros((32, piece, width), jnp.float32)
        prev = jnp.zeros((32, piece, width), jnp.float32)
        for j in range(e, 8, share):
            part = parts_ref[j].astype(jnp.float32)
            own = own + jnp.where(later(j, z), part, 0.0)
            prev = prev + jnp.where(later(j, z), 0.0, part)
        own_ref[:, e] = own
        prev_ref[:, e] = prev
    for p in range(32):
        here = order_ref[p % 16, p // 16]
        after = place_ref[jnp.minimum(here + 1, 31)]
        total = own_ref[p] + jnp.where(here < 31, prev_ref[after], 0.0)
        out_ref[p] = total.astype(out_ref.dtype)


def delta_kernel(grad_ref, out_ref, delta_ref):
    ones = jnp.ones((8, width), jnp.bfloat16)
    for h in range(kv_heads):
        cut = slice(h * group, (h + 1) * group)
        grad = grad_ref[...].astype(jnp.float32)[:, cut].reshape(columns, width)
        out = out_ref[...].astype(jnp.float32)[:, cut].reshape(columns, width)
        product = grad * out
        high = product.astype(jnp.bfloat16)
        rest = (product - high.astype(jnp.float32)).astype(jnp.bfloat16)
        delta_ref[h : h + 1] = (nt(ones, high) + nt(ones, rest))[0:1]


def attention_kernel(*refs):
    order_ref, lengths_ref, meta_ref = refs[:3]
    query_refs = refs[3 : 3 + share]
    grad_refs = refs[3 + share : 3 + 2 * share]
    delta_refs = refs[3 + 2 * share : 3 + 3 * share]
    own_refs = refs[3 + 3 * share : 3 + 4 * share]
    window_ref = refs[3 + 4 * share]
    results = refs[4 + 4 * share :]
    query_grad_refs = results[:share]
    own_grad_refs = results[share : 2 * share]
    window_grad_ref, bias_ref, key_acc_ref, value_acc_ref, query_acc_ref = results[2 * share :]
    place = meta_ref[2]
    current = order_ref[meta_ref[0], meta_ref[1]]
    base = (current - 1) * span
    token = lax.shift_right_logical(
        lax.broadcasted_iota(jnp.int32, (1, columns), 1), 3
    )
    lasts = [span + (place ^ b) * chunk + token for b in range(share)]

    def doc(i, carry):
        end, lows = carry
        end = end + lengths_ref[i]
        return end, tuple(
            jnp.where(end <= last, jnp.maximum(low, end), low)
            for low, last in zip(lows, lasts)
        )

    first_end = jnp.int32(0) - base
    low_start = jnp.zeros((1, columns), jnp.int32) + first_end
    _, lows = lax.fori_loop(0, 63, doc, (first_end, (low_start,) * share))
    row = lax.broadcasted_iota(jnp.int32, (window, columns), 0)
    stretch = lax.shift_right_logical(row, 6)
    key_at = jnp.where(
        lax.div(stretch, share) >= lax.div(place, share), row, row + span
    )
    for b in range(share):
        key_at = jnp.where(
            stretch == 8 + b, row - b * chunk + (place ^ b) * chunk, key_at
        )
    for b in range(share):
        allowed = (key_at <= lasts[b]) & (key_at >= lows[b])
        bias_ref[...] = jnp.where(allowed, 0.0, masked)
        for h in range(local_kv):
            cut = slice(h * group, (h + 1) * group)
            query = query_refs[b][...].astype(jnp.float32)[:, cut].reshape(columns, width)
            grad = grad_refs[b][...].astype(jnp.float32)[:, cut].reshape(columns, width)
            query = query.astype(jnp.bfloat16)
            grad = grad.astype(jnp.bfloat16)
            delta = delta_refs[b][h : h + 1]
            key = jnp.concatenate(
                [window_ref[:, h, 0].reshape(span, width)] + [own[h, 0] for own in own_refs],
                axis=0,
            )
            value = jnp.concatenate(
                [window_ref[:, h, 1].reshape(span, width)] + [own[h, 1] for own in own_refs],
                axis=0,
            )
            scores = nt(key, query) * (factor * log2e) + bias_ref[...]
            top = jnp.max(scores, axis=0, keepdims=True)
            exps = jnp.exp2(scores - top)
            total = jnp.sum(exps, axis=0, keepdims=True)
            probs = exps * (1.0 / total)
            grad_scores = (probs * (nt(value, grad) - delta)).astype(jnp.bfloat16)
            value_part = jnp.dot(
                probs.astype(jnp.bfloat16), grad, preferred_element_type=jnp.float32
            )
            key_part = jnp.dot(grad_scores, query, preferred_element_type=jnp.float32)
            query_part = lax.dot_general(
                key, grad_scores, (((0,), (0,)), ((), ())), preferred_element_type=jnp.float32
            )
            query_acc_ref[:, cut] = (jnp.transpose(query_part) * factor).reshape(
                chunk, group, width
            )
            if b > 0:
                key_part = key_part + key_acc_ref[h]
                value_part = value_part + value_acc_ref[h]
            if b < share - 1:
                key_acc_ref[h] = key_part
                value_acc_ref[h] = value_part
            else:
                key_part = key_part * factor
                window_grad_ref[:, h, 0] = key_part[:span].astype(jnp.bfloat16).reshape(8, chunk, width)
                window_grad_ref[:, h, 1] = value_part[:span].astype(jnp.bfloat16).reshape(8, chunk, width)
                for k in range(share):
                    at = slice(span + k * chunk, span + (k + 1) * chunk)
                    kind = own_grad_refs[k].dtype
                    own_grad_refs[k][h, 0] = key_part[at].astype(kind)
                    own_grad_refs[k][h, 1] = value_part[at].astype(kind)
        query_grad_refs[b][...] = query_acc_ref[...].astype(jnp.bfloat16)


vmem = pl.BlockSpec(memory_space=pltpu.VMEM)
smem = pl.BlockSpec(memory_space=pltpu.SMEM)
low = jnp.bfloat16


def trade(array, b):
    return lax.ppermute(array, "z", [(i, i ^ b) for i in range(8)])


def route(array, axes):
    return lax.all_to_all(array, axes, split_axis=0, concat_axis=0, tiled=True)


def shards(queries, keys, values, attention_out, out_grad, span_order, doc_lengths):
    z = lax.axis_index("z")
    mine = lax.rem(z, share)
    query_index = (lax.axis_index("yh") * 4 + lax.axis_index("x")) * 2 + lax.axis_index("c")
    meta = jnp.stack([query_index, lax.axis_index("yl"), z]).astype(jnp.int32)
    own = jnp.transpose(jnp.stack([keys, values], axis=2), (1, 2, 0, 3))
    own = own.reshape(share, 32, piece, width)
    pieces = route(jnp.transpose(own, (1, 0, 2, 3)), plane_axes)
    own = own.reshape(share, local_kv, 2, chunk, width)
    delta = pl.pallas_call(
        delta_kernel,
        out_shape=jax.ShapeDtypeStruct((kv_heads, columns), jnp.float32),
        in_specs=[vmem, vmem],
        out_specs=vmem,
    )(out_grad, attention_out).reshape(share, local_kv, columns)

    def gathered(array, axis, count):
        parts = []
        for b in range(share):
            part = lax.dynamic_slice_in_dim(array, (mine ^ b) * count, count, axis)
            parts.append(trade(part, b) if b else part)
        return parts

    query_parts = gathered(queries, 1, local_heads)
    grad_parts = gathered(out_grad, 1, local_heads)
    delta_parts = [d.reshape(local_kv, columns) for d in gathered(delta, 0, 1)]
    own_parts = [o.reshape(local_kv, 2, chunk, width) for o in gathered(own, 0, 1)]

    spread = pl.pallas_call(
        expand_kernel,
        out_shape=jax.ShapeDtypeStruct((8, 32, piece, width), low),
        in_specs=[smem, smem, vmem],
        out_specs=vmem,
        scratch_shapes=[
            pltpu.SMEM((32,), jnp.int32),
            pltpu.VMEM((32, share, piece, width), low),
        ],
    )(span_order, meta, pieces)
    around = route(spread.reshape(256, piece, width), all_axes)
    results = pl.pallas_call(
        attention_kernel,
        out_shape=tuple(
            [jax.ShapeDtypeStruct((chunk, local_heads, width), low)] * share
            + [jax.ShapeDtypeStruct((local_kv, 2, chunk, width), jnp.float32)]
            + [jax.ShapeDtypeStruct((local_kv, 2, chunk, width), low)] * (share - 1)
            + [jax.ShapeDtypeStruct((8, local_kv, 2, chunk, width), low)]
        ),
        in_specs=[smem] * 3 + [vmem] * (4 * share + 1),
        out_specs=tuple([vmem] * (2 * share + 1)),
        scratch_shapes=[
            pltpu.VMEM((window, columns), jnp.float32),
            pltpu.VMEM((local_kv, window, width), jnp.float32),
            pltpu.VMEM((local_kv, window, width), jnp.float32),
            pltpu.VMEM((chunk, local_heads, width), jnp.float32),
        ],
    )(
        span_order,
        doc_lengths,
        meta,
        *query_parts,
        *grad_parts,
        *delta_parts,
        *own_parts,
        around.reshape(8, local_kv, 2, chunk, width),
    )
    query_grads = list(results[:share])
    own_grads = list(results[share : 2 * share])
    parts = route(results[-1].reshape(256, piece, width), all_axes)
    for b in range(1, share):
        query_grads[b] = trade(query_grads[b], b)
        own_grads[b] = trade(own_grads[b], b)
    sums = pl.pallas_call(
        reduce_kernel,
        out_shape=jax.ShapeDtypeStruct((32, share, piece, width), low),
        in_specs=[smem, smem, vmem],
        out_specs=vmem,
        scratch_shapes=[
            pltpu.SMEM((32,), jnp.int32),
            pltpu.VMEM((32, share, piece, width), jnp.float32),
            pltpu.VMEM((32, share, piece, width), jnp.float32),
        ],
    )(span_order, meta, parts.reshape(8, 32, piece, width))
    back = route(sums, plane_axes)
    back = jnp.transpose(back, (1, 0, 2, 3)).reshape(share, local_kv, 2, chunk, width)

    def arranged(members):
        columns_of = []
        for e in range(share):
            chosen = members[0]
            for b in range(1, share):
                chosen = jnp.where((mine ^ b) == e, members[b], chosen)
            columns_of.append(chosen)
        return columns_of

    query_grad = jnp.concatenate(arranged(query_grads), axis=1)
    both = jnp.stack(arranged([m.astype(jnp.float32) for m in own_grads])) + back
    both = both.reshape(kv_heads, 2, chunk, width)
    both = jnp.transpose(both, (1, 2, 0, 3)).astype(low)
    return query_grad, both[0], both[1]


def solution(mesh):
    fine = Mesh(mesh.devices.reshape(2, 8, 2, 4, 2), ("yl", "z", "yh", "x", "c"))
    rows = P(row_axes, None, None)
    return jax.shard_map(
        shards,
        mesh=fine,
        in_specs=(rows, rows, rows, rows, rows, P(), P()),
        out_specs=(rows, rows, rows),
        check_vma=False,
    )
```

time: 135 us -> 117 us (0.87)
  blocking collectives: 96.6 us -> 0 us
  waiting for transfers between devices: 5.65 us -> 47.4 us
  starting transfers between devices: 8.58 us -> 42.6 us
  local copies, waits for them, and re-layouts: 4.28 us -> 10.2 us
  Pallas kernels: 16.9 us -> 14.1 us
    all_to_all x3 -> x0, blocking collectives: 96.6 us -> none  [the longest x1 42.7 us: shards(): lax.all_to_all(spread.reshape(256, 16, width), all_axes, split_axis=0, co...]
    all_to_all x1 -> x4, starting transfers between devices: 8.58 us -> 37.6 us  [route(): return lax.all_to_all(array, axes, split_axis=0, concat_axis=0, tiled=True)]
    ppermute x0 -> x6, waiting for transfers between devices: none -> 26.8 us  [trade(): return lax.ppermute(array, 'z', [(i, i ^ b) for i in range(8)])]
    all_to_all x1 -> x4, waiting for transfers between devices: 5.65 us -> 20.6 us  [route(): return lax.all_to_all(array, axes, split_axis=0, concat_axis=0, tiled=True)]
    ppermute x0 -> x6, starting transfers between devices: none -> 5.01 us  [trade(): return lax.ppermute(array, 'z', [(i, i ^ b) for i in range(8)])]
    pallas_call x3 -> x4, Pallas kernels: 16.9 us -> 14.1 us  [the longest x1 7.99 us: shards(): pl.pallas_call(attention_kernel, out_shape=tuple([jax.ShapeDtypeStruct((c...]
    dynamic_slice x0 -> x4, local copies, waits for them, and re-layouts: none -> 2.74 us  [gathered(): part = lax.dynamic_slice_in_dim(array, (mine ^ b) * count, count, axis)]
    unnamed x9 -> x31, local copies, waits for them, and re-layouts: 3.38 us -> 5.11 us
  transfers between devices with their start and end apart: 1 -> 10, of which waited for: 1 -> 5; matrix products, arithmetic and copies ran while one was open for 1% -> 5% of each run, Pallas kernels for 0% -> 4%
where the time goes in v2:
time: 117 us
  waiting for transfers between devices  47.4 us (41%)
  starting transfers between devices  42.6 us (36%)
  Pallas kernels  14.1 us (12%)
  local copies, waits for them, and re-layouts  10.2 us (9%)
  other arithmetic  1.57 us (1%)
    all_to_all x4, starting transfers between devices, route(): return lax.all_to_all(array, axes, split_axis=0, concat_axis=0, tiled=True)  37.6 us
    ppermute x6, waiting for transfers between devices, trade(): return lax.ppermute(array, 'z', [(i, i ^ b) for i in range(8)])  26.8 us
    all_to_all x4, waiting for transfers between devices, route(): return lax.all_to_all(array, axes, split_axis=0, concat_axis=0, tiled=True)  20.6 us
    pallas_call x1, Pallas kernels, shards(): pl.pallas_call(attention_kernel, out_shape=tuple([jax.ShapeDtypeStruct((c...  7.99 us
    unnamed x31, local copies, waits for them, and re-layouts  5.11 us
    ppermute x6, starting transfers between devices, trade(): return lax.ppermute(array, 'z', [(i, i ^ b) for i in range(8)])  5.01 us
    dynamic_slice x4, local copies, waits for them, and re-layouts, gathered(): part = lax.dynamic_slice_in_dim(array, (mine ^ b) * count, count, axis)  2.74 us
  transfers between devices with their start and end apart: 10, of which 5 were waited for; matrix products, arithmetic and copies ran while one was open for 5% of the time, Pallas kernels for 4%

profile of v2, /device:TPU:1, one launch (start us, length us, event | category | flops | bytes accessed | tf_op | source)
XLA Modules:
  0.0 116.7 jit_solution(297364827093114541)
XLA Ops:
  0.6 0.9 copy_bitcast_fusion.1
  1.5 0.7 copy.27
  2.2 8.6 %all-to-all-start = ((bf16[32,2,8,128]{3,2,1,0:T(8,128)(2,1)}), bf16[32,2,8,128]{3,2,1,0:T(8,128)(2,1)S(1)}, u32[]{:S(2)}, u32[]{:S(2)}) async-start(bf16[32,2,8,128]{3,2,1,0:T(8,128)(2,1)} %bitcast.40), calls=%async_computation | async-start | bytes 262144 | tf_op jit(solution)/shard_map/all_to_all | solution.py:191
  10.8 0.7 copy-done.11
  11.5 0.7 copy.19.order_ref.refs_0_
  12.2 0.6 pad_add_fusion.meta_ref.refs_2_
  12.8 5.7 %all-to-all-done.pieces_ref = bf16[32,2,8,128]{3,2,1,0:T(8,128)(2,1)S(1)} async-done(((bf16[32,2,8,128]{3,2,1,0:T(8,128)(2,1)}), bf16[32,2,8,128]{3,2,1,0:T(8,128)(2,1)S(1)}, u32[]{:S(2)}, u32[]{:S(2)}) %all-to-all-start) | async-done | bytes 131104 | tf_op jit(solution)/shard_map/all_to_all | solution.py:191
  18.5 0.6 copy-done.4
  19.1 1.9 %shard_map.95 = bf16[8,32,8,128]{3,2,1,0:T(8,128)(2,1)} custom-call(s32[16,2]{1,0:T(8,128)} %copy.19.order_ref.refs_0_, s32[3]{0:T(128)} %pad_add_fusion.meta_ref.refs_2_, bf16[32,2,8,128]{3,2,1,0:T(8,128)(2,1)} %copy-done.4), custom_call_target="tpu_custom_call" | custom-call | tf_op jit(solution)/shard_map/pallas_call | solution.py:222
  21.1 10.8 %all-to-all-start.1 = ((bf16[256,8,128]{2,1,0:T(8,128)(2,1)}), bf16[256,8,128]{2,1,0:T(8,128)(2,1)S(1)}, u32[]{:S(2)}, u32[]{:S(2)}) async-start(bf16[256,8,128]{2,1,0:T(8,128)(2,1)} %bitcast.42), calls=%async_computation.1 | async-start | bytes 1048576 | tf_op jit(solution)/shard_map/all_to_all | solution.py:191
  31.9 0.7 constant_dynamic-slice_fusion.2
  32.6 1.5 %collective-permute-start.1 = (bf16[64,16,128]{2,1,0:T(8,128)(2,1)S(1)}, bf16[64,16,128]{2,1,0:T(8,128)(2,1)S(1)}, u32[]{:S(2)}, u32[]{:S(2)}) collective-permute-start(bf16[64,16,128]{2,1,0:T(8,128)(2,1)S(1)} %get-tuple-element.18), channel_id=1, source_target_pairs={{0,16},{16,0},{32,48},{48,32},{64,80},{80,64},{96,112},{112,96},{1... | collective-permute-start | bytes 786440 | tf_op jit(solution)/shard_map/ppermute | solution.py:187
  34.1 0.8 constant_dynamic-slice_fusion.4
  35.2 0.6 constant_dynamic-slice_fusion
  35.9 1.1 collective-permute-start.3
  37.0 2.2 %shard_map.94 = f32[4,512]{1,0:T(4,128)} custom-call(bf16[64,32,128]{2,1,0:T(8,128)(2,1)} %grad_ref.1, bf16[64,32,128]{2,1,0:T(8,128)(2,1)} %out_ref.1), custom_call_target="tpu_custom_call" | custom-call | tf_op jit(solution)/shard_map/pallas_call | solution.py:203
  39.2 0.7 reshape.42
  39.9 0.6 constant_dynamic-slice_fusion.1
  40.9 15.4 %collective-permute-done.2 = f32[1,2,512]{2,1,0:T(2,128)S(1)} collective-permute-done((f32[1,2,512]{2,1,0:T(2,128)S(1)}, f32[1,2,512]{2,1,0:T(2,128)S(1)}, u32[]{:S(2)}, u32[]{:S(2)}) %collective-permute-start.2) | collective-permute-done | bytes 4128 | tf_op jit(solution)/shard_map/ppermute | solution.py:187
  56.3 0.5 copy-done.10
  57.3 8.0 %shard_map.96 = (bf16[64,16,128]{2,1,0:T(8,128)(2,1)}, bf16[64,16,128]{2,1,0:T(8,128)(2,1)}, f32[2,2,64,128]{3,2,1,0:T(8,128)}, bf16[2,2,64,128]{3,2,1,0:T(8,128)(2,1)}, bf16[8,2,2,64,128]{4,3,2,1,0:T(8,128)(2,1)}) custom-call(s32[16,2]{1,0:T(8,128)} %copy.19.order_ref.refs_0_, s32[64]{0:T(128)} %refs_1_.1, s32[3]{0:T(128)} %pad_add_fusion.meta_ref.refs_2_, ...), custom_call_target="tpu_custom_call" | custom-call | tf_op jit(solution)/shard_map/pallas_call | solution.py:233
  65.3 13.4 %all-to-all-start.2 = ((bf16[256,8,128]{2,1,0:T(8,128)(2,1)}), bf16[256,8,128]{2,1,0:T(8,128)(2,1)S(1)}, u32[]{:S(2)}, u32[]{:S(2)}) async-start(bf16[256,8,128]{2,1,0:T(8,128)(2,1)} %bitcast.48), calls=%async_computation.2 | async-start | bytes 1048576 | tf_op jit(solution)/shard_map/all_to_all | solution.py:191
  78.7 1.6 %collective-permute-start.5 = (bf16[2,2,64,128]{3,2,1,0:T(8,128)(2,1)S(1)}, bf16[2,2,64,128]{3,2,1,0:T(8,128)(2,1)S(1)}, u32[]{:S(2)}, u32[]{:S(2)}) collective-permute-start(bf16[2,2,64,128]{3,2,1,0:T(8,128)(2,1)S(1)} %copy-done.13), channel_id=1, source_target_pairs={{0,16},{16,0},{32,48},{48,32},{64,80},{80,64},{96,112},{112,96},{1... | collective-permute-start | bytes 196616 | tf_op jit(solution)/shard_map/ppermute | solution.py:187
  80.3 11.4 %collective-permute-done.5 = bf16[2,2,64,128]{3,2,1,0:T(8,128)(2,1)S(1)} collective-permute-done((bf16[2,2,64,128]{3,2,1,0:T(8,128)(2,1)S(1)}, bf16[2,2,64,128]{3,2,1,0:T(8,128)(2,1)S(1)}, u32[]{:S(2)}, u32[]{:S(2)}) %collective-permute-start.5) | collective-permute-done | bytes 65568 | tf_op jit(solution)/shard_map/ppermute | solution.py:187
  91.8 8.0 %all-to-all-done.2 = bf16[256,8,128]{2,1,0:T(8,128)(2,1)S(1)} async-done(((bf16[256,8,128]{2,1,0:T(8,128)(2,1)}), bf16[256,8,128]{2,1,0:T(8,128)(2,1)S(1)}, u32[]{:S(2)}, u32[]{:S(2)}) %all-to-all-start.2) | async-done | bytes 524320 | tf_op jit(solution)/shard_map/all_to_all | solution.py:191
  99.8 0.8 copy-done.2
  100.6 2.0 %shard_map.97 = bf16[32,2,8,128]{3,2,1,0:T(8,128)(2,1)} custom-call(s32[16,2]{1,0:T(8,128)} %copy.19.order_ref.refs_0_, s32[3]{0:T(128)} %pad_add_fusion.meta_ref.refs_2_, bf16[8,32,8,128]{3,2,1,0:T(8,128)(2,1)} %bitcast.43), custom_call_target="tpu_custom_call" | custom-call | tf_op jit(solution)/shard_map/pallas_call | solution.py:265
  102.6 4.9 %all-to-all-start.3 = ((bf16[32,2,8,128]{3,2,1,0:T(8,128)(2,1)}), bf16[32,2,8,128]{3,2,1,0:T(8,128)(2,1)S(1)}, u32[]{:S(2)}, u32[]{:S(2)}) async-start(bf16[32,2,8,128]{3,2,1,0:T(8,128)(2,1)} %shard_map.97), calls=%async_computation.3 | async-start | bytes 262144 | tf_op jit(solution)/shard_map/all_to_all | solution.py:191
  107.6 0.8 pad_maximum_fusion
  108.4 6.8 %all-to-all-done.3 = bf16[32,2,8,128]{3,2,1,0:T(8,128)(2,1)S(1)} async-done(((bf16[32,2,8,128]{3,2,1,0:T(8,128)(2,1)}), bf16[32,2,8,128]{3,2,1,0:T(8,128)(2,1)S(1)}, u32[]{:S(2)}, u32[]{:S(2)}) %all-to-all-start.3) | async-done | bytes 131104 | tf_op jit(solution)/shard_map/all_to_all | solution.py:191
  115.4 0.7 copy.22
  116.1 0.7 copy.23
  (40 shorter events, 1.5 us)
Async XLA Ops:
  2.2 16.3 %all-to-all-start = ((bf16[32,2,8,128]{3,2,1,0:T(8,128)(2,1)}), bf16[32,2,8,128]{3,2,1,0:T(8,128)(2,1)S(1)}, u32[]{:S(2)}, u32[]{:S(2)}) async-start(bf16[32,2,8,128]{3,2,1,0:T(8,128)(2,1)} %bitcast.40), calls=%async_computation | async-start | bytes 262144 | tf_op jit(solution)/shard_map/all_to_all | solution.py:191
  10.8 0.7 copy-start.11
  18.5 0.6 copy-start.4
  21.1 10.8 %copy-start.1 = (bf16[64,32,128]{2,1,0:T(8,128)(2,1)S(1)}, bf16[64,32,128]{2,1,0:T(8,128)(2,1)}, u32[]{:S(2)}) copy-start(bf16[64,32,128]{2,1,0:T(8,128)(2,1)} %grad_ref.1) | copy-start | bytes 1572868
  21.1 35.3 %all-to-all-start.1 = ((bf16[256,8,128]{2,1,0:T(8,128)(2,1)}), bf16[256,8,128]{2,1,0:T(8,128)(2,1)S(1)}, u32[]{:S(2)}, u32[]{:S(2)}) async-start(bf16[256,8,128]{2,1,0:T(8,128)(2,1)} %bitcast.42), calls=%async_computation.1 | async-start | bytes 1048576 | tf_op jit(solution)/shard_map/all_to_all | solution.py:191
  31.9 2.2 %copy-start.3 = (bf16[64,32,128]{2,1,0:T(8,128)(2,1)S(1)}, bf16[64,32,128]{2,1,0:T(8,128)(2,1)}, u32[]{:S(2)}) copy-start(bf16[64,32,128]{2,1,0:T(8,128)(2,1)} %param.7) | copy-start | bytes 1572868
  32.6 23.7 %collective-permute-start.1 = (bf16[64,16,128]{2,1,0:T(8,128)(2,1)S(1)}, bf16[64,16,128]{2,1,0:T(8,128)(2,1)S(1)}, u32[]{:S(2)}, u32[]{:S(2)}) collective-permute-start(bf16[64,16,128]{2,1,0:T(8,128)(2,1)S(1)} %get-tuple-element.18), channel_id=1, source_target_pairs={{0,16},{16,0},{32,48},{48,32},{64,80},{80,64},{96,112},{112,96},{1... | collective-permute-start | bytes 786440 | tf_op jit(solution)/shard_map/ppermute | solution.py:187
  34.9 21.4 %collective-permute-start = (bf16[64,16,128]{2,1,0:T(8,128)(2,1)S(1)}, bf16[64,16,128]{2,1,0:T(8,128)(2,1)S(1)}, u32[]{:S(2)}, u32[]{:S(2)}) collective-permute-start(bf16[64,16,128]{2,1,0:T(8,128)(2,1)S(1)} %get-tuple-element.20), channel_id=1, source_target_pairs={{0,16},{16,0},{32,48},{48,32},{64,80},{80,64},{96,112},{112,96},{1... | collective-permute-start | bytes 786440 | tf_op jit(solution)/shard_map/ppermute | solution.py:187
  35.9 20.4 %collective-permute-start.3 = (bf16[1,2,2,64,128]{4,3,2,1,0:T(8,128)(2,1)S(1)}, bf16[1,2,2,64,128]{4,3,2,1,0:T(8,128)(2,1)S(1)}, u32[]{:S(2)}, u32[]{:S(2)}) collective-permute-start(bf16[1,2,2,64,128]{4,3,2,1,0:T(8,128)(2,1)S(1)} %get-tuple-element.26), channel_id=1, source_target_pairs={{0,16},{16,0},{32,48},{48,32},{64,80},{80,64},{96,112},{112,96},{1... | collective-permute-start | bytes 196616 | tf_op jit(solution)/shard_map/ppermute | solution.py:187
  40.5 15.8 %collective-permute-start.2 = (f32[1,2,512]{2,1,0:T(2,128)S(1)}, f32[1,2,512]{2,1,0:T(2,128)S(1)}, u32[]{:S(2)}, u32[]{:S(2)}) collective-permute-start(f32[1,2,512]{2,1,0:T(2,128)S(1)} %get-tuple-element.28), channel_id=1, source_target_pairs={{0,16},{16,0},{32,48},{48,32},{64,80},{80,64},{96,112},{112,96},{1... | collective-permute-start | bytes 12296 | tf_op jit(solution)/shard_map/ppermute | solution.py:187
  56.3 0.6 copy-start.10
  56.3 0.6 copy-start.9
  56.3 0.7 copy-start.6
  56.3 0.8 copy-start.7
  56.3 0.9 copy-start
  65.3 13.4 %copy-start.13 = (bf16[2,2,64,128]{3,2,1,0:T(8,128)(2,1)S(1)}, bf16[2,2,64,128]{3,2,1,0:T(8,128)(2,1)}, u32[]{:S(2)}) copy-start(bf16[2,2,64,128]{3,2,1,0:T(8,128)(2,1)} %get-tuple-element.10) | copy-start | bytes 196612
  65.3 15.0 %copy-start.12 = (bf16[64,16,128]{2,1,0:T(8,128)(2,1)S(1)}, bf16[64,16,128]{2,1,0:T(8,128)(2,1)}, u32[]{:S(2)}) copy-start(bf16[64,16,128]{2,1,0:T(8,128)(2,1)} %get-tuple-element.8) | copy-start | bytes 786436
  65.3 26.5 %copy-start.8 = (f32[2,2,64,128]{3,2,1,0:T(8,128)S(1)}, f32[2,2,64,128]{3,2,1,0:T(8,128)}, u32[]{:S(2)}) copy-start(f32[2,2,64,128]{3,2,1,0:T(8,128)} %get-tuple-element.11) | copy-start | bytes 393220
  65.3 34.5 %all-to-all-start.2 = ((bf16[256,8,128]{2,1,0:T(8,128)(2,1)}), bf16[256,8,128]{2,1,0:T(8,128)(2,1)S(1)}, u32[]{:S(2)}, u32[]{:S(2)}) async-start(bf16[256,8,128]{2,1,0:T(8,128)(2,1)} %bitcast.48), calls=%async_computation.2 | async-start | bytes 1048576 | tf_op jit(solution)/shard_map/all_to_all | solution.py:191
  78.7 13.1 %collective-permute-start.5 = (bf16[2,2,64,128]{3,2,1,0:T(8,128)(2,1)S(1)}, bf16[2,2,64,128]{3,2,1,0:T(8,128)(2,1)S(1)}, u32[]{:S(2)}, u32[]{:S(2)}) collective-permute-start(bf16[2,2,64,128]{3,2,1,0:T(8,128)(2,1)S(1)} %copy-done.13), channel_id=1, source_target_pairs={{0,16},{16,0},{32,48},{48,32},{64,80},{80,64},{96,112},{112,96},{1... | collective-permute-start | bytes 196616 | tf_op jit(solution)/shard_map/ppermute | solution.py:187
  80.2 27.3 %collective-permute-start.4 = (bf16[64,16,128]{2,1,0:T(8,128)(2,1)S(1)}, bf16[64,16,128]{2,1,0:T(8,128)(2,1)S(1)}, u32[]{:S(2)}, u32[]{:S(2)}) collective-permute-start(bf16[64,16,128]{2,1,0:T(8,128)(2,1)S(1)} %copy-done.12), channel_id=1, source_target_pairs={{0,16},{16,0},{32,48},{48,32},{64,80},{80,64},{96,112},{112,96},{1... | collective-permute-start | bytes 786440 | tf_op jit(solution)/shard_map/ppermute | solution.py:187
  99.8 0.8 copy-start.2
  102.6 4.9 %copy-start.5 = (bf16[64,16,128]{2,1,0:T(8,128)(2,1)S(1)}, bf16[64,16,128]{2,1,0:T(8,128)(2,1)}, u32[]{:S(2)}) copy-start(bf16[64,16,128]{2,1,0:T(8,128)(2,1)} %get-tuple-element.9) | copy-start | bytes 786436
  102.6 12.7 %all-to-all-start.3 = ((bf16[32,2,8,128]{3,2,1,0:T(8,128)(2,1)}), bf16[32,2,8,128]{3,2,1,0:T(8,128)(2,1)S(1)}, u32[]{:S(2)}, u32[]{:S(2)}) async-start(bf16[32,2,8,128]{3,2,1,0:T(8,128)(2,1)} %shard_map.97), calls=%async_computation.3 | async-start | bytes 262144 | tf_op jit(solution)/shard_map/all_to_all | solution.py:191

commit v3 on v2

v3 whole, which is shorter than its diff:
```python
import jax
import jax.numpy as jnp
from jax import lax
from jax.experimental import pallas as pl
from jax.experimental.pallas import tpu as pltpu
from jax.sharding import Mesh, PartitionSpec as P


span = 512
chunk = 64
group = 8
width = 128
kv_heads = 4
heads = 32
share = 2
local_kv = kv_heads // share
piece = 16 // share
window = span + share * chunk
columns = chunk * group
row_axes = ("yh", "x", "c", "yl", "z")
plane_axes = ("yl", "yh", "x", "c")
all_axes = ("yl", "yh", "x", "c", "z")
masked = -1e30
log2e = 1.4426950408889634
factor = width ** -0.5


def nt(a, b):
    return lax.dot_general(
        a, b, (((1,), (1,)), ((), ())), preferred_element_type=jnp.float32
    )


def place_spans(order_ref, place_ref):
    for p in range(32):
        place_ref[order_ref[p % 16, p // 16]] = p


def later(j, z):
    return j // share > lax.div(z, share)


def expand_kernel(order_ref, meta_ref, pieces_ref, out_ref, place_ref, prev_ref):
    place_spans(order_ref, place_ref)
    z = meta_ref[2]
    for p in range(32):
        before = place_ref[jnp.maximum(order_ref[p % 16, p // 16] - 1, 0)]
        prev_ref[p] = pieces_ref[before]
    for j in range(8):
        @pl.when(later(j, z))
        def _():
            out_ref[:, j] = pieces_ref[:, j % share]

        @pl.when(jnp.logical_not(later(j, z)))
        def _():
            out_ref[:, j] = prev_ref[:, j % share]


def reduce_kernel(order_ref, meta_ref, parts_ref, out_ref, place_ref, own_ref, prev_ref):
    place_spans(order_ref, place_ref)
    z = meta_ref[2]
    for e in range(share):
        own = jnp.zeros((32, piece, width), jnp.float32)
        prev = jnp.zeros((32, piece, width), jnp.float32)
        for j in range(e, 8, share):
            part = parts_ref[:, j].astype(jnp.float32)
            own = own + jnp.where(later(j, z), part, 0.0)
            prev = prev + jnp.where(later(j, z), 0.0, part)
        own_ref[:, e] = own
        prev_ref[:, e] = prev
    for p in range(32):
        here = order_ref[p % 16, p // 16]
        after = place_ref[jnp.minimum(here + 1, 31)]
        total = own_ref[p] + jnp.where(here < 31, prev_ref[after], 0.0)
        out_ref[p] = total.astype(out_ref.dtype)


def delta_kernel(grad_ref, out_ref, delta_ref):
    ones = jnp.ones((8, width), jnp.bfloat16)
    for h in range(kv_heads):
        cut = slice(h * group, (h + 1) * group)
        grad = grad_ref[...].astype(jnp.float32)[:, cut].reshape(columns, width)
        out = out_ref[...].astype(jnp.float32)[:, cut].reshape(columns, width)
        product = grad * out
        high = product.astype(jnp.bfloat16)
        rest = (product - high.astype(jnp.float32)).astype(jnp.bfloat16)
        delta_ref[h : h + 1] = (nt(ones, high) + nt(ones, rest))[0:1]


def attention_kernel(*refs):
    order_ref, lengths_ref, meta_ref = refs[:3]
    message_refs = refs[3 : 3 + share]
    delta_refs = refs[3 + share : 3 + 2 * share]
    window_ref = refs[3 + 2 * share]
    results = refs[4 + 2 * share :]
    result_refs = results[:share]
    own_grad_ref, window_grad_ref, bias_ref, key_acc_ref, value_acc_ref = results[share:]
    place = meta_ref[2]
    current = order_ref[meta_ref[0], meta_ref[1]]
    base = (current - 1) * span
    token = lax.shift_right_logical(
        lax.broadcasted_iota(jnp.int32, (1, columns), 1), 3
    )
    lasts = [span + (place ^ b) * chunk + token for b in range(share)]

    def doc(i, carry):
        end, lows = carry
        end = end + lengths_ref[i]
        return end, tuple(
            jnp.where(end <= last, jnp.maximum(low, end), low)
            for low, last in zip(lows, lasts)
        )

    first_end = jnp.int32(0) - base
    low_start = jnp.zeros((1, columns), jnp.int32) + first_end
    _, lows = lax.fori_loop(0, 63, doc, (first_end, (low_start,) * share))
    row = lax.broadcasted_iota(jnp.int32, (window, columns), 0)
    stretch = lax.shift_right_logical(row, 6)
    source = lax.div(row, piece) & 7
    inside = lax.div(row, 8 * piece) * piece + (row & (piece - 1))
    key_at = source * chunk + inside
    key_at = jnp.where(
        lax.div(source, share) >= lax.div(place, share), key_at, key_at + span
    )
    for b in range(share):
        key_at = jnp.where(
            stretch == 8 + b, row - b * chunk + (place ^ b) * chunk, key_at
        )

    def own_rows(b, h, kind):
        start = local_kv * 2 * columns + (h * 2 + kind) * chunk
        return message_refs[b][start : start + chunk]

    for b in range(share):
        allowed = (key_at <= lasts[b]) & (key_at >= lows[b])
        bias_ref[...] = jnp.where(allowed, 0.0, masked)
        for h in range(local_kv):
            query = message_refs[b][h * columns : (h + 1) * columns]
            grad = message_refs[b][(local_kv + h) * columns : (local_kv + h + 1) * columns]
            delta = delta_refs[b][h : h + 1]
            key = jnp.concatenate(
                [window_ref[h, 0]]
                + [own_rows(k, h, 0) for k in range(share)],
                axis=0,
            )
            value = jnp.concatenate(
                [window_ref[h, 1]]
                + [own_rows(k, h, 1) for k in range(share)],
                axis=0,
            )
            scores = nt(key, query) * (factor * log2e) + bias_ref[...]
            top = jnp.max(scores, axis=0, keepdims=True)
            exps = jnp.exp2(scores - top)
            total = jnp.sum(exps, axis=0, keepdims=True)
            probs = exps * (1.0 / total)
            grad_scores = (probs * (nt(value, grad) - delta)).astype(low)
            value_part = jnp.dot(
                probs.astype(low), grad, preferred_element_type=jnp.float32
            )
            key_part = jnp.dot(grad_scores, query, preferred_element_type=jnp.float32)
            query_part = lax.dot_general(
                key, grad_scores, (((0,), (0,)), ((), ())), preferred_element_type=jnp.float32
            )
            result_refs[b][h * columns : (h + 1) * columns] = (
                jnp.transpose(query_part) * factor
            ).astype(low)
            if b > 0:
                key_part = key_part + key_acc_ref[h]
                value_part = value_part + value_acc_ref[h]
            if b < share - 1:
                key_acc_ref[h] = key_part
                value_acc_ref[h] = value_part
            else:
                key_part = key_part * factor
                window_grad_ref[h, 0] = key_part[:span].astype(low)
                window_grad_ref[h, 1] = value_part[:span].astype(low)
                for k in range(share):
                    at = slice(span + k * chunk, span + (k + 1) * chunk)
                    for kind, part in enumerate((key_part, value_part)):
                        start = (h * 2 + kind) * chunk
                        if k == 0:
                            own_grad_ref[start : start + chunk] = part[at]
                        else:
                            start = start + local_kv * columns
                            result_refs[k][start : start + chunk] = part[at].astype(low)


vmem = pl.BlockSpec(memory_space=pltpu.VMEM)
smem = pl.BlockSpec(memory_space=pltpu.SMEM)
low = jnp.bfloat16


def trade(array, b):
    return lax.ppermute(array, "z", [(i, i ^ b) for i in range(8)])


def route(array, axes):
    return lax.all_to_all(array, axes, split_axis=0, concat_axis=0, tiled=True)


def shards(queries, keys, values, attention_out, out_grad, span_order, doc_lengths):
    z = lax.axis_index("z")
    mine = lax.rem(z, share)
    query_index = (lax.axis_index("yh") * 4 + lax.axis_index("x")) * 2 + lax.axis_index("c")
    meta = jnp.stack([query_index, lax.axis_index("yl"), z]).astype(jnp.int32)
    own = jnp.stack([jnp.transpose(keys, (1, 0, 2)), jnp.transpose(values, (1, 0, 2))], axis=1)
    own = own.reshape(share, 32, piece, width)
    pieces = route(jnp.transpose(own, (1, 0, 2, 3)), plane_axes)
    delta = pl.pallas_call(
        delta_kernel,
        out_shape=jax.ShapeDtypeStruct((kv_heads, columns), jnp.float32),
        in_specs=[vmem, vmem],
        out_specs=vmem,
    )(out_grad, attention_out).reshape(share, local_kv, columns)

    def per_share(array):
        array = array.reshape(chunk, share, local_kv, group, width)
        return jnp.transpose(array, (1, 2, 0, 3, 4)).reshape(share, local_kv * columns, width)

    whole = jnp.concatenate(
        [per_share(queries), per_share(out_grad), own.reshape(share, -1, width)], axis=1
    )
    messages = []
    deltas = []
    for b in range(share):
        message = lax.dynamic_index_in_dim(whole, mine ^ b, 0, keepdims=False)
        part = lax.dynamic_index_in_dim(delta, mine ^ b, 0, keepdims=False)
        messages.append(trade(message, b) if b else message)
        deltas.append(trade(part, b) if b else part)

    spread = pl.pallas_call(
        expand_kernel,
        out_shape=jax.ShapeDtypeStruct((32, 8, piece, width), low),
        in_specs=[smem, smem, vmem],
        out_specs=vmem,
        scratch_shapes=[
            pltpu.SMEM((32,), jnp.int32),
            pltpu.VMEM((32, share, piece, width), low),
        ],
    )(span_order, meta, pieces)
    around = route(spread.reshape(256, piece, width), all_axes)
    back_rows = local_kv * (columns + 2 * chunk)
    results = pl.pallas_call(
        attention_kernel,
        out_shape=tuple(
            [jax.ShapeDtypeStruct((local_kv * columns, width), low)]
            + [jax.ShapeDtypeStruct((back_rows, width), low)] * (share - 1)
            + [jax.ShapeDtypeStruct((local_kv * 2 * chunk, width), jnp.float32)]
            + [jax.ShapeDtypeStruct((local_kv, 2, span, width), low)]
        ),
        in_specs=[smem] * 3 + [vmem] * (2 * share + 1),
        out_specs=tuple([vmem] * (share + 2)),
        scratch_shapes=[
            pltpu.VMEM((window, columns), jnp.float32),
            pltpu.VMEM((local_kv, window, width), jnp.float32),
            pltpu.VMEM((local_kv, window, width), jnp.float32),
        ],
    )(
        span_order,
        doc_lengths,
        meta,
        *messages,
        *deltas,
        around.reshape(local_kv, 2, span, width),
    )
    parts = route(results[-1].reshape(256, piece, width), all_axes)
    query_grads = [results[0]]
    own_grads = [results[share]]
    for b in range(1, share):
        got = trade(results[b], b)
        query_grads.append(got[: local_kv * columns])
        own_grads.append(got[local_kv * columns :])
    sums = pl.pallas_call(
        reduce_kernel,
        out_shape=jax.ShapeDtypeStruct((32, share, piece, width), low),
        in_specs=[smem, smem, vmem],
        out_specs=vmem,
        scratch_shapes=[
            pltpu.SMEM((32,), jnp.int32),
            pltpu.VMEM((32, share, piece, width), jnp.float32),
            pltpu.VMEM((32, share, piece, width), jnp.float32),
        ],
    )(span_order, meta, parts.reshape(32, 8, piece, width))
    back = route(sums, plane_axes)

    def arranged(members):
        found = []
        for e in range(share):
            chosen = members[0]
            for b in range(1, share):
                chosen = jnp.where((mine ^ b) == e, members[b], chosen)
            found.append(chosen)
        return jnp.stack(found)

    query_grad = arranged(query_grads).reshape(share, local_kv, chunk, group, width)
    query_grad = jnp.transpose(query_grad, (2, 0, 1, 3, 4)).reshape(chunk, heads, width)
    local = arranged([m.astype(jnp.float32) for m in own_grads])
    back, query_grad, local = lax.optimization_barrier((back, query_grad, local))
    back = jnp.transpose(back, (1, 0, 2, 3)).reshape(share, -1, width)
    both = (local + back).reshape(kv_heads, 2, chunk, width)
    both = jnp.transpose(both, (1, 2, 0, 3)).astype(low)
    return query_grad, both[0], both[1]


def solution(mesh):
    fine = Mesh(mesh.devices.reshape(2, 8, 2, 4, 2), ("yl", "z", "yh", "x", "c"))
    rows = P(row_axes, None, None)
    return jax.shard_map(
        shards,
        mesh=fine,
        in_specs=(rows, rows, rows, rows, rows, P(), P()),
        out_specs=(rows, rows, rows),
        check_vma=False,
    )
```

time: 117 us -> 118 us (level)
  waiting for transfers between devices: 47.4 us -> 49.9 us
  local copies, waits for them, and re-layouts: 10.2 us -> 8.89 us
    ppermute x6 -> x3, waiting for transfers between devices: 26.8 us -> 35.6 us  [trade(): return lax.ppermute(array, 'z', [(i, i ^ b) for i in range(8)])]
    all_to_all x4, waiting for transfers between devices: 20.6 us -> 14.3 us  [route(): return lax.all_to_all(array, axes, split_axis=0, concat_axis=0, tiled=True)]
    dynamic_slice x4 -> x0, local copies, waits for them, and re-layouts: 2.74 us -> none  [gathered(): part = lax.dynamic_slice_in_dim(array, (mine ^ b) * count, count, axis)]
    unnamed x31 -> x19, local copies, waits for them, and re-layouts: 5.11 us -> 3.12 us
    ppermute x6 -> x3, starting transfers between devices: 5.01 us -> 3.05 us  [trade(): return lax.ppermute(array, 'z', [(i, i ^ b) for i in range(8)])]
    all_to_all x4, starting transfers between devices: 37.6 us -> 39.2 us  [route(): return lax.all_to_all(array, axes, split_axis=0, concat_axis=0, tiled=True)]
    squeeze x0 -> x2, local copies, waits for them, and re-layouts: none -> 1.53 us  [the longest x1 0.94 us: shards(): message = lax.dynamic_index_in_dim(whole, mine ^ b, 0, keepdims=False)]
  transfers between devices with their start and end apart: 10 -> 7, of which waited for: 5 -> 5; matrix products, arithmetic and copies ran while one was open for 5% -> 5% of each run, Pallas kernels for 4% -> 2%
where the time goes in v3:
time: 118 us
  waiting for transfers between devices  49.9 us (42%)
  starting transfers between devices  42.3 us (36%)
  Pallas kernels  14.2 us (12%)
  local copies, waits for them, and re-layouts  8.89 us (8%)
  other arithmetic  1.81 us (2%)
    all_to_all x4, starting transfers between devices, route(): return lax.all_to_all(array, axes, split_axis=0, concat_axis=0, tiled=True)  39.2 us
    ppermute x3, waiting for transfers between devices, trade(): return lax.ppermute(array, 'z', [(i, i ^ b) for i in range(8)])  35.6 us
    all_to_all x4, waiting for transfers between devices, route(): return lax.all_to_all(array, axes, split_axis=0, concat_axis=0, tiled=True)  14.3 us
    pallas_call x1, Pallas kernels, shards(): pl.pallas_call(attention_kernel, out_shape=tuple([jax.ShapeDtypeStruct((l...  8.03 us
    unnamed x19, local copies, waits for them, and re-layouts  3.12 us
    ppermute x3, starting transfers between devices, trade(): return lax.ppermute(array, 'z', [(i, i ^ b) for i in range(8)])  3.05 us
  transfers between devices with their start and end apart: 7, of which 5 were waited for; matrix products, arithmetic and copies ran while one was open for 5% of the time, Pallas kernels for 2%

profile of v3, /device:TPU:1, one launch (start us, length us, event | category | flops | bytes accessed | tf_op | source)
XLA Modules:
  0.0 118.0 jit_solution(5186582361871560340)
XLA Ops:
  0.7 1.0 copy_bitcast_fusion.2
  1.7 0.7 copy.34
  2.3 8.7 %all-to-all-start = ((bf16[32,2,8,128]{3,2,1,0:T(8,128)(2,1)}), bf16[32,2,8,128]{3,2,1,0:T(8,128)(2,1)S(1)}, u32[]{:S(2)}, u32[]{:S(2)}) async-start(bf16[32,2,8,128]{3,2,1,0:T(8,128)(2,1)} %bitcast.59), calls=%async_computation | async-start | bytes 262144 | tf_op jit(solution)/shard_map/all_to_all | solution.py:198
  11.1 0.1 copy.17
  11.3 0.7 copy.24.order_ref.refs_0_
  12.0 0.6 pad_add_fusion.meta_ref.refs_2_
  12.6 6.1 %all-to-all-done.pieces_ref = bf16[32,2,8,128]{3,2,1,0:T(8,128)(2,1)S(1)} async-done(((bf16[32,2,8,128]{3,2,1,0:T(8,128)(2,1)}), bf16[32,2,8,128]{3,2,1,0:T(8,128)(2,1)S(1)}, u32[]{:S(2)}, u32[]{:S(2)}) %all-to-all-start) | async-done | bytes 131104 | tf_op jit(solution)/shard_map/all_to_all | solution.py:198
  18.7 0.7 copy-done.5
  19.4 2.0 %shard_map.95 = bf16[32,8,8,128]{3,2,1,0:T(8,128)(2,1)} custom-call(s32[16,2]{1,0:T(8,128)} %copy.24.order_ref.refs_0_, s32[3]{0:T(128)} %pad_add_fusion.meta_ref.refs_2_, bf16[32,2,8,128]{3,2,1,0:T(8,128)(2,1)} %copy-done.5), custom_call_target="tpu_custom_call" | custom-call | tf_op jit(solution)/shard_map/pallas_call | solution.py:231
  21.3 10.8 %all-to-all-start.1 = ((bf16[256,8,128]{2,1,0:T(8,128)(2,1)}), bf16[256,8,128]{2,1,0:T(8,128)(2,1)S(1)}, u32[]{:S(2)}, u32[]{:S(2)}) async-start(bf16[256,8,128]{2,1,0:T(8,128)(2,1)} %bitcast.62), calls=%async_computation.1 | async-start | bytes 1048576 | tf_op jit(solution)/shard_map/all_to_all | solution.py:198
  32.2 0.9 dynamic-slice_bitcast_fusion
  33.1 1.5 %collective-permute-start = (bf16[2304,128]{1,0:T(8,128)(2,1)S(1)}, bf16[2304,128]{1,0:T(8,128)(2,1)S(1)}, u32[]{:S(2)}, u32[]{:S(2)}) collective-permute-start(bf16[2304,128]{1,0:T(8,128)(2,1)S(1)} %get-tuple-element.17), channel_id=1, source_target_pairs={{0,16},{16,0},{32,48},{48,32},{64,80},{80,64},{96,112},{112,96},{1... | collective-permute-start | bytes 1769480 | tf_op jit(solution)/shard_map/ppermute | solution.py:194
  34.6 2.2 %shard_map.94 = f32[4,512]{1,0:T(4,128)} custom-call(bf16[64,32,128]{2,1,0:T(8,128)(2,1)} %grad_ref.1, bf16[64,32,128]{2,1,0:T(8,128)(2,1)} %out_ref.1), custom_call_target="tpu_custom_call" | custom-call | tf_op jit(solution)/shard_map/pallas_call | solution.py:209
  36.8 0.7 reshape.53
  37.6 0.6 dynamic-slice_bitcast_fusion.2
  38.2 18.4 %collective-permute-done.1.refs_6_ = f32[2,512]{1,0:T(2,128)S(1)} collective-permute-done((f32[2,512]{1,0:T(2,128)S(1)}, f32[2,512]{1,0:T(2,128)S(1)}, u32[]{:S(2)}, u32[]{:S(2)}) %collective-permute-start.1) | collective-permute-done | bytes 4128 | tf_op jit(solution)/shard_map/ppermute | solution.py:194
  56.6 0.6 copy-done.7
  57.1 0.2 copy-done.3
  57.4 0.2 copy-done
  57.5 8.0 %shard_map.96 = (bf16[1024,128]{1,0:T(8,128)(2,1)}, bf16[1280,128]{1,0:T(8,128)(2,1)}, f32[256,128]{1,0:T(8,128)}, bf16[2,2,512,128]{3,2,1,0:T(8,128)(2,1)}) custom-call(s32[16,2]{1,0:T(8,128)} %copy.24.order_ref.refs_0_, s32[64]{0:T(128)} %refs_1_.1, s32[3]{0:T(128)} %pad_add_fusion.meta_ref.refs_2_, bf16[2304,128]{1,0:T(8,128)(2,1)} %get-tuple-element.18.refs_3_, ...), custom_call_target="tpu_custom_call" | custom-call | tf_op jit(solution)/shard_map/pallas_call | solution.py:243
  65.6 13.4 %all-to-all-start.2 = ((bf16[256,8,128]{2,1,0:T(8,128)(2,1)}), bf16[256,8,128]{2,1,0:T(8,128)(2,1)S(1)}, u32[]{:S(2)}, u32[]{:S(2)}) async-start(bf16[256,8,128]{2,1,0:T(8,128)(2,1)} %bitcast.71), calls=%async_computation.2 | async-start | bytes 1048576 | tf_op jit(solution)/shard_map/all_to_all | solution.py:198
  79.0 1.6 %collective-permute-start.2 = (bf16[1280,128]{1,0:T(8,128)(2,1)}, bf16[1280,128]{1,0:T(8,128)(2,1)S(1)}, u32[]{:S(2)}, u32[]{:S(2)}) collective-permute-start(bf16[1280,128]{1,0:T(8,128)(2,1)} %get-tuple-element.11), channel_id=1, source_target_pairs={{0,16},{16,0},{32,48},{48,32},{64,80},{80,64},{96,112},{112,96},{1... | collective-permute-start | bytes 983048 | tf_op jit(solution)/shard_map/ppermute | solution.py:194
  80.5 17.2 %collective-permute-done.2 = bf16[1280,128]{1,0:T(8,128)(2,1)S(1)} collective-permute-done((bf16[1280,128]{1,0:T(8,128)(2,1)}, bf16[1280,128]{1,0:T(8,128)(2,1)S(1)}, u32[]{:S(2)}, u32[]{:S(2)}) %collective-permute-start.2) | collective-permute-done | bytes 327712 | tf_op jit(solution)/shard_map/ppermute | solution.py:194
  97.7 0.9 fusion.1
  98.7 1.5 %all-to-all-done.2 = bf16[256,8,128]{2,1,0:T(8,128)(2,1)S(1)} async-done(((bf16[256,8,128]{2,1,0:T(8,128)(2,1)}), bf16[256,8,128]{2,1,0:T(8,128)(2,1)S(1)}, u32[]{:S(2)}, u32[]{:S(2)}) %all-to-all-start.2) | async-done | bytes 524320 | tf_op jit(solution)/shard_map/all_to_all | solution.py:198
  100.2 0.8 copy-done.2
  101.0 2.0 %shard_map.97 = bf16[32,2,8,128]{3,2,1,0:T(8,128)(2,1)} custom-call(s32[16,2]{1,0:T(8,128)} %copy.24.order_ref.refs_0_, s32[3]{0:T(128)} %pad_add_fusion.meta_ref.refs_2_, bf16[32,8,8,128]{3,2,1,0:T(8,128)(2,1)} %bitcast.63), custom_call_target="tpu_custom_call" | custom-call | tf_op jit(solution)/shard_map/pallas_call | solution.py:273
  103.0 6.4 %all-to-all-start.3 = ((bf16[32,2,8,128]{3,2,1,0:T(8,128)(2,1)}), bf16[32,2,8,128]{3,2,1,0:T(8,128)(2,1)S(1)}, u32[]{:S(2)}, u32[]{:S(2)}) async-start(bf16[32,2,8,128]{3,2,1,0:T(8,128)(2,1)} %shard_map.97), calls=%async_computation.3 | async-start | bytes 262144 | tf_op jit(solution)/shard_map/all_to_all | solution.py:198
  109.5 0.9 copy.25
  110.4 6.7 %all-to-all-done.3 = bf16[32,2,8,128]{3,2,1,0:T(8,128)(2,1)S(1)} async-done(((bf16[32,2,8,128]{3,2,1,0:T(8,128)(2,1)}), bf16[32,2,8,128]{3,2,1,0:T(8,128)(2,1)S(1)}, u32[]{:S(2)}, u32[]{:S(2)}) %all-to-all-start.3) | async-done | bytes 131104 | tf_op jit(solution)/shard_map/all_to_all | solution.py:198
  117.1 0.1 copy.33
  117.3 0.7 slice_bitcast_fusion
  (23 shorter events, 0.4 us)
Async XLA Ops:
  0.6 10.4 %copy-start.4 = (bf16[64,32,128]{2,1,0:T(8,128)(2,1)S(1)}, bf16[64,32,128]{2,1,0:T(8,128)(2,1)}, u32[]{:S(2)}) copy-start(bf16[64,32,128]{2,1,0:T(8,128)(2,1)} %param.7) | copy-start | bytes 1572868
  0.6 10.5 %copy-start.1 = (bf16[64,32,128]{2,1,0:T(8,128)(2,1)S(1)}, bf16[64,32,128]{2,1,0:T(8,128)(2,1)}, u32[]{:S(2)}) copy-start(bf16[64,32,128]{2,1,0:T(8,128)(2,1)} %grad_ref.1) | copy-start | bytes 1572868
  2.3 9.0 %copy-start.8 = (s32[16,2]{0,1:T(2,128)S(1)}, s32[16,2]{0,1:T(2,128)}, u32[]{:S(2)}) copy-start(s32[16,2]{0,1:T(2,128)} %param.12) | copy-start | bytes 388
  2.3 16.4 %all-to-all-start = ((bf16[32,2,8,128]{3,2,1,0:T(8,128)(2,1)}), bf16[32,2,8,128]{3,2,1,0:T(8,128)(2,1)S(1)}, u32[]{:S(2)}, u32[]{:S(2)}) async-start(bf16[32,2,8,128]{3,2,1,0:T(8,128)(2,1)} %bitcast.59), calls=%async_computation | async-start | bytes 262144 | tf_op jit(solution)/shard_map/all_to_all | solution.py:198
  18.7 0.7 copy-start.5
  21.3 35.2 %all-to-all-start.1 = ((bf16[256,8,128]{2,1,0:T(8,128)(2,1)}), bf16[256,8,128]{2,1,0:T(8,128)(2,1)S(1)}, u32[]{:S(2)}, u32[]{:S(2)}) async-start(bf16[256,8,128]{2,1,0:T(8,128)(2,1)} %bitcast.62), calls=%async_computation.1 | async-start | bytes 1048576 | tf_op jit(solution)/shard_map/all_to_all | solution.py:198
  33.1 23.4 %collective-permute-start = (bf16[2304,128]{1,0:T(8,128)(2,1)S(1)}, bf16[2304,128]{1,0:T(8,128)(2,1)S(1)}, u32[]{:S(2)}, u32[]{:S(2)}) collective-permute-start(bf16[2304,128]{1,0:T(8,128)(2,1)S(1)} %get-tuple-element.17), channel_id=1, source_target_pairs={{0,16},{16,0},{32,48},{48,32},{64,80},{80,64},{96,112},{112,96},{1... | collective-permute-start | bytes 1769480 | tf_op jit(solution)/shard_map/ppermute | solution.py:194
  38.1 18.4 %collective-permute-start.1 = (f32[2,512]{1,0:T(2,128)S(1)}, f32[2,512]{1,0:T(2,128)S(1)}, u32[]{:S(2)}, u32[]{:S(2)}) collective-permute-start(f32[2,512]{1,0:T(2,128)S(1)} %get-tuple-element.25), channel_id=1, source_target_pairs={{0,16},{16,0},{32,48},{48,32},{64,80},{80,64},{96,112},{112,96},{1... | collective-permute-start | bytes 12296 | tf_op jit(solution)/shard_map/ppermute | solution.py:194
  56.6 0.6 copy-start.7
  56.6 0.8 copy-start.3
  56.6 1.0 copy-start
  65.6 33.0 %copy-start.6 = (bf16[1024,128]{1,0:T(8,128)(2,1)S(1)}, bf16[1024,128]{1,0:T(8,128)(2,1)}, u32[]{:S(2)}) copy-start(bf16[1024,128]{1,0:T(8,128)(2,1)} %get-tuple-element.12) | copy-start | bytes 786436
  65.6 34.6 %all-to-all-start.2 = ((bf16[256,8,128]{2,1,0:T(8,128)(2,1)}), bf16[256,8,128]{2,1,0:T(8,128)(2,1)S(1)}, u32[]{:S(2)}, u32[]{:S(2)}) async-start(bf16[256,8,128]{2,1,0:T(8,128)(2,1)} %bitcast.71), calls=%async_computation.2 | async-start | bytes 1048576 | tf_op jit(solution)/shard_map/all_to_all | solution.py:198
  79.0 18.7 %collective-permute-start.2 = (bf16[1280,128]{1,0:T(8,128)(2,1)}, bf16[1280,128]{1,0:T(8,128)(2,1)S(1)}, u32[]{:S(2)}, u32[]{:S(2)}) collective-permute-start(bf16[1280,128]{1,0:T(8,128)(2,1)} %get-tuple-element.11), channel_id=1, source_target_pairs={{0,16},{16,0},{32,48},{48,32},{64,80},{80,64},{96,112},{112,96},{1... | collective-permute-start | bytes 983048 | tf_op jit(solution)/shard_map/ppermute | solution.py:194
  100.2 0.8 copy-start.2
  103.0 14.1 %all-to-all-start.3 = ((bf16[32,2,8,128]{3,2,1,0:T(8,128)(2,1)}), bf16[32,2,8,128]{3,2,1,0:T(8,128)(2,1)S(1)}, u32[]{:S(2)}, u32[]{:S(2)}) async-start(bf16[32,2,8,128]{3,2,1,0:T(8,128)(2,1)} %shard_map.97), calls=%async_computation.3 | async-start | bytes 262144 | tf_op jit(solution)/shard_map/all_to_all | solution.py:198

commit v4 on v3

--- a/solution.py
+++ b/solution.py
@@ -186,6 +186,12 @@
 
 
 vmem = pl.BlockSpec(memory_space=pltpu.VMEM)
+
+
+def near(array):
+    return pltpu.with_memory_space_constraint(array, pltpu.VMEM)
+
+
 smem = pl.BlockSpec(memory_space=pltpu.SMEM)
 low = jnp.bfloat16
 
@@ -230,23 +236,23 @@
 
     spread = pl.pallas_call(
         expand_kernel,
-        out_shape=jax.ShapeDtypeStruct((32, 8, piece, width), low),
+        out_shape=pltpu.VMEM((32, 8, piece, width), low),
         in_specs=[smem, smem, vmem],
         out_specs=vmem,
         scratch_shapes=[
             pltpu.SMEM((32,), jnp.int32),
             pltpu.VMEM((32, share, piece, width), low),
         ],
-    )(span_order, meta, pieces)
+    )(span_order, meta, near(pieces))
     around = route(spread.reshape(256, piece, width), all_axes)
     back_rows = local_kv * (columns + 2 * chunk)
     results = pl.pallas_call(
         attention_kernel,
         out_shape=tuple(
-            [jax.ShapeDtypeStruct((local_kv * columns, width), low)]
-            + [jax.ShapeDtypeStruct((back_rows, width), low)] * (share - 1)
-            + [jax.ShapeDtypeStruct((local_kv * 2 * chunk, width), jnp.float32)]
-            + [jax.ShapeDtypeStruct((local_kv, 2, span, width), low)]
+            [pltpu.VMEM((local_kv * columns, width), low)]
+            + [pltpu.VMEM((back_rows, width), low)] * (share - 1)
+            + [pltpu.VMEM((local_kv * 2 * chunk, width), jnp.float32)]
+            + [pltpu.VMEM((local_kv, 2, span, width), low)]
         ),
         in_specs=[smem] * 3 + [vmem] * (2 * share + 1),
         out_specs=tuple([vmem] * (share + 2)),
@@ -259,9 +265,9 @@
         span_order,
         doc_lengths,
         meta,
-        *messages,
+        *[near(m) for m in messages],
         *deltas,
-        around.reshape(local_kv, 2, span, width),
+        near(around.reshape(local_kv, 2, span, width)),
     )
     parts = route(results[-1].reshape(256, piece, width), all_axes)
     query_grads = [results[0]]
@@ -272,7 +278,7 @@
         own_grads.append(got[local_kv * columns :])
     sums = pl.pallas_call(
         reduce_kernel,
-        out_shape=jax.ShapeDtypeStruct((32, share, piece, width), low),
+        out_shape=pltpu.VMEM((32, share, piece, width), low),
         in_specs=[smem, smem, vmem],
         out_specs=vmem,
         scratch_shapes=[
@@ -280,7 +286,7 @@
             pltpu.VMEM((32, share, piece, width), jnp.float32),
             pltpu.VMEM((32, share, piece, width), jnp.float32),
         ],
-    )(span_order, meta, parts.reshape(32, 8, piece, width))
+    )(span_order, meta, near(parts.reshape(32, 8, piece, width)))
     back = route(sums, plane_axes)
 
     def arranged(members):

time: 118 us -> 115 us (0.975)
  local copies, waits for them, and re-layouts: 8.89 us -> 6.99 us
    unnamed x19 -> x11, local copies, waits for them, and re-layouts: 3.12 us -> 1.28 us
  transfers between devices with their start and end apart: 7 -> 7, of which waited for: 5 -> 5; matrix products, arithmetic and copies ran while one was open for 5% -> 4% of each run, Pallas kernels for 2% -> 2%
where the time goes in v4:
time: 115 us; the launch traced here: 114 us
  waiting for transfers between devices  50.8 us (44%)
  starting transfers between devices  41.5 us (36%)
  Pallas kernels  13.1 us (11%)
  local copies, waits for them, and re-layouts  6.99 us (6%)
    all_to_all x4, starting transfers between devices, route(): return lax.all_to_all(array, axes, split_axis=0, concat_axis=0, tiled=True)  38.3 us
    ppermute x3, waiting for transfers between devices, trade(): return lax.ppermute(array, 'z', [(i, i ^ b) for i in range(8)])  36.3 us
    all_to_all x4, waiting for transfers between devices, route(): return lax.all_to_all(array, axes, split_axis=0, concat_axis=0, tiled=True)  14.5 us
    pallas_call x1, Pallas kernels, shards(): pl.pallas_call(attention_kernel, out_shape=tuple([pltpu.VMEM((local_kv *...  7.24 us
    ppermute x3, starting transfers between devices, trade(): return lax.ppermute(array, 'z', [(i, i ^ b) for i in range(8)])  3.15 us
  transfers between devices with their start and end apart: 7, of which 5 were waited for; matrix products, arithmetic and copies ran while one was open for 4% of the time, Pallas kernels for 2%

profile of v4, /device:TPU:1, one launch (start us, length us, event | category | flops | bytes accessed | tf_op | source)
XLA Modules:
  0.0 114.1 jit_solution(5901675143771627535)
XLA Ops:
  0.6 0.0 copy-start
  0.7 1.0 copy_bitcast_fusion.2
  1.7 0.7 copy.34
  2.3 8.7 %all-to-all-start = ((bf16[32,2,8,128]{3,2,1,0:T(8,128)(2,1)}), bf16[32,2,8,128]{3,2,1,0:T(8,128)(2,1)S(1)}, u32[]{:S(2)}, u32[]{:S(2)}) async-start(bf16[32,2,8,128]{3,2,1,0:T(8,128)(2,1)} %bitcast.59), calls=%async_computation | async-start | bytes 262144 | tf_op jit(solution)/shard_map/all_to_all | solution.py:204
  11.1 0.1 copy.17
  11.2 0.9 copy.18
  12.1 0.7 copy.24.order_ref.refs_0_
  12.7 0.6 pad_add_fusion.meta_ref.refs_2_
  13.4 5.4 %all-to-all-done.pieces_ref = bf16[32,2,8,128]{3,2,1,0:T(8,128)(2,1)S(1)} async-done(((bf16[32,2,8,128]{3,2,1,0:T(8,128)(2,1)}), bf16[32,2,8,128]{3,2,1,0:T(8,128)(2,1)S(1)}, u32[]{:S(2)}, u32[]{:S(2)}) %all-to-all-start) | async-done | bytes 131104 | tf_op jit(solution)/shard_map/all_to_all | solution.py:204
  18.7 1.9 %shard_map.95 = bf16[32,8,8,128]{3,2,1,0:T(8,128)(2,1)} custom-call(s32[16,2]{1,0:T(8,128)} %copy.24.order_ref.refs_0_, s32[3]{0:T(128)} %pad_add_fusion.meta_ref.refs_2_, bf16[32,2,8,128]{3,2,1,0:T(8,128)(2,1)S(1)} %all-to-all-done.pieces_ref), custom_call_target="tpu_custom_call" | custom-call | tf_op jit(solution)/shard_map/pallas_call | solution.py:237
  20.6 10.8 %all-to-all-start.1 = ((bf16[256,8,128]{2,1,0:T(8,128)(2,1)}), bf16[256,8,128]{2,1,0:T(8,128)(2,1)S(1)}, u32[]{:S(2)}, u32[]{:S(2)}) async-start(bf16[256,8,128]{2,1,0:T(8,128)(2,1)} %bitcast.20), calls=%async_computation.1 | async-start | bytes 1048576 | tf_op jit(solution)/shard_map/all_to_all | solution.py:204
  31.4 0.1 pad_maximum_fusion
  31.5 0.1 dynamic-slice_bitcast_fusion
  31.6 1.6 %collective-permute-start = (bf16[2304,128]{1,0:T(8,128)(2,1)S(1)}, bf16[2304,128]{1,0:T(8,128)(2,1)S(1)}, u32[]{:S(2)}, u32[]{:S(2)}) collective-permute-start(bf16[2304,128]{1,0:T(8,128)(2,1)S(1)} %get-tuple-element.17), channel_id=1, source_target_pairs={{0,16},{16,0},{32,48},{48,32},{64,80},{80,64},{96,112},{112,96},{1... | collective-permute-start | bytes 1769480 | tf_op jit(solution)/shard_map/ppermute | solution.py:200
  33.1 2.2 %shard_map.94 = f32[4,512]{1,0:T(4,128)} custom-call(bf16[64,32,128]{2,1,0:T(8,128)(2,1)} %grad_ref.1, bf16[64,32,128]{2,1,0:T(8,128)(2,1)} %out_ref.1), custom_call_target="tpu_custom_call" | custom-call | tf_op jit(solution)/shard_map/pallas_call | solution.py:215
  35.3 0.7 reshape.53
  36.0 0.6 dynamic-slice_bitcast_fusion.2
  36.6 0.0 collective-permute-start.1
  36.7 19.1 %collective-permute-done.1.refs_6_ = f32[2,512]{1,0:T(2,128)S(1)} collective-permute-done((f32[2,512]{1,0:T(2,128)S(1)}, f32[2,512]{1,0:T(2,128)S(1)}, u32[]{:S(2)}, u32[]{:S(2)}) %collective-permute-start.1) | collective-permute-done | bytes 4128 | tf_op jit(solution)/shard_map/ppermute | solution.py:200
  55.8 0.6 copy-done.3
  56.4 7.2 %shard_map.96 = (bf16[1024,128]{1,0:T(8,128)(2,1)S(1)}, bf16[1280,128]{1,0:T(8,128)(2,1)S(1)}, f32[256,128]{1,0:T(8,128)S(1)}, bf16[2,2,512,128]{3,2,1,0:T(8,128)(2,1)}) custom-call(s32[16,2]{1,0:T(8,128)} %copy.24.order_ref.refs_0_, s32[64]{0:T(128)} %refs_1_.1, s32[3]{0:T(128)} %pad_add_fusion.meta_ref.refs_2_, ...), custom_call_target="tpu_custom_call" | custom-call | tf_op jit(solution)/shard_map/pallas_call | solution.py:249
  63.6 13.4 %all-to-all-start.2 = ((bf16[256,8,128]{2,1,0:T(8,128)(2,1)}), bf16[256,8,128]{2,1,0:T(8,128)(2,1)S(1)}, u32[]{:S(2)}, u32[]{:S(2)}) async-start(bf16[256,8,128]{2,1,0:T(8,128)(2,1)} %bitcast.22), calls=%async_computation.2 | async-start | bytes 1048576 | tf_op jit(solution)/shard_map/all_to_all | solution.py:204
  77.0 1.6 %collective-permute-start.2 = (bf16[1280,128]{1,0:T(8,128)(2,1)S(1)}, bf16[1280,128]{1,0:T(8,128)(2,1)S(1)}, u32[]{:S(2)}, u32[]{:S(2)}) collective-permute-start(bf16[1280,128]{1,0:T(8,128)(2,1)S(1)} %get-tuple-element.11), channel_id=1, source_target_pairs={{0,16},{16,0},{32,48},{48,32},{64,80},{80,64},{96,112},{112,96},{1... | collective-permute-start | bytes 983048 | tf_op jit(solution)/shard_map/ppermute | solution.py:200
  78.6 17.2 %collective-permute-done.2 = bf16[1280,128]{1,0:T(8,128)(2,1)S(1)} collective-permute-done((bf16[1280,128]{1,0:T(8,128)(2,1)S(1)}, bf16[1280,128]{1,0:T(8,128)(2,1)S(1)}, u32[]{:S(2)}, u32[]{:S(2)}) %collective-permute-start.2) | collective-permute-done | bytes 327712 | tf_op jit(solution)/shard_map/ppermute | solution.py:200
  95.8 2.4 %all-to-all-done.2 = bf16[256,8,128]{2,1,0:T(8,128)(2,1)S(1)} async-done(((bf16[256,8,128]{2,1,0:T(8,128)(2,1)}), bf16[256,8,128]{2,1,0:T(8,128)(2,1)S(1)}, u32[]{:S(2)}, u32[]{:S(2)}) %all-to-all-start.2) | async-done | bytes 524320 | tf_op jit(solution)/shard_map/all_to_all | solution.py:204
  98.3 1.8 %shard_map.97 = bf16[32,2,8,128]{3,2,1,0:T(8,128)(2,1)} custom-call(s32[16,2]{1,0:T(8,128)} %copy.24.order_ref.refs_0_, s32[3]{0:T(128)} %pad_add_fusion.meta_ref.refs_2_, bf16[32,8,8,128]{3,2,1,0:T(8,128)(2,1)S(1)} %bitcast.61), custom_call_target="tpu_custom_call" | custom-call | tf_op jit(solution)/shard_map/pallas_call | solution.py:279
  100.0 5.5 %all-to-all-start.3 = ((bf16[32,2,8,128]{3,2,1,0:T(8,128)(2,1)}), bf16[32,2,8,128]{3,2,1,0:T(8,128)(2,1)S(1)}, u32[]{:S(2)}, u32[]{:S(2)}) async-start(bf16[32,2,8,128]{3,2,1,0:T(8,128)(2,1)} %shard_map.97), calls=%async_computation.3 | async-start | bytes 262144 | tf_op jit(solution)/shard_map/all_to_all | solution.py:204
  105.5 0.1 maximum_bitcast_fusion
  105.6 0.9 copy.25
  106.5 6.7 %all-to-all-done.3 = bf16[32,2,8,128]{3,2,1,0:T(8,128)(2,1)S(1)} async-done(((bf16[32,2,8,128]{3,2,1,0:T(8,128)(2,1)}), bf16[32,2,8,128]{3,2,1,0:T(8,128)(2,1)S(1)}, u32[]{:S(2)}, u32[]{:S(2)}) %all-to-all-start.3) | async-done | bytes 131104 | tf_op jit(solution)/shard_map/all_to_all | solution.py:204
  113.2 0.1 copy.33
  113.4 0.7 slice_bitcast_fusion
  (15 shorter events, 0.1 us)
Async XLA Ops:
  0.6 10.4 %copy-start.2 = (bf16[64,32,128]{2,1,0:T(8,128)(2,1)S(1)}, bf16[64,32,128]{2,1,0:T(8,128)(2,1)}, u32[]{:S(2)}) copy-start(bf16[64,32,128]{2,1,0:T(8,128)(2,1)} %param.7) | copy-start | bytes 1572868
  0.6 10.5 %copy-start = (bf16[64,32,128]{2,1,0:T(8,128)(2,1)S(1)}, bf16[64,32,128]{2,1,0:T(8,128)(2,1)}, u32[]{:S(2)}) copy-start(bf16[64,32,128]{2,1,0:T(8,128)(2,1)} %grad_ref.1) | copy-start | bytes 1572868
  2.3 9.7 %copy-start.4 = (s32[16,2]{0,1:T(2,128)S(1)}, s32[16,2]{0,1:T(2,128)}, u32[]{:S(2)}) copy-start(s32[16,2]{0,1:T(2,128)} %param.12) | copy-start | bytes 388
  2.3 16.4 %all-to-all-start = ((bf16[32,2,8,128]{3,2,1,0:T(8,128)(2,1)}), bf16[32,2,8,128]{3,2,1,0:T(8,128)(2,1)S(1)}, u32[]{:S(2)}, u32[]{:S(2)}) async-start(bf16[32,2,8,128]{3,2,1,0:T(8,128)(2,1)} %bitcast.59), calls=%async_computation | async-start | bytes 262144 | tf_op jit(solution)/shard_map/all_to_all | solution.py:204
  12.1 19.3 %copy-start.1 = (bf16[2,2,64,8,128]{4,3,2,1,0:T(8,128)(2,1)S(1)}, bf16[2,2,64,8,128]{4,3,2,1,0:T(8,128)(2,1)}, u32[]{:S(2)}) copy-start(bf16[2,2,64,8,128]{4,3,2,1,0:T(8,128)(2,1)} %copy.18) | copy-start | bytes 1572868
  20.6 35.2 %all-to-all-start.1 = ((bf16[256,8,128]{2,1,0:T(8,128)(2,1)}), bf16[256,8,128]{2,1,0:T(8,128)(2,1)S(1)}, u32[]{:S(2)}, u32[]{:S(2)}) async-start(bf16[256,8,128]{2,1,0:T(8,128)(2,1)} %bitcast.20), calls=%async_computation.1 | async-start | bytes 1048576 | tf_op jit(solution)/shard_map/all_to_all | solution.py:204
  31.6 24.2 %collective-permute-start = (bf16[2304,128]{1,0:T(8,128)(2,1)S(1)}, bf16[2304,128]{1,0:T(8,128)(2,1)S(1)}, u32[]{:S(2)}, u32[]{:S(2)}) collective-permute-start(bf16[2304,128]{1,0:T(8,128)(2,1)S(1)} %get-tuple-element.17), channel_id=1, source_target_pairs={{0,16},{16,0},{32,48},{48,32},{64,80},{80,64},{96,112},{112,96},{1... | collective-permute-start | bytes 1769480 | tf_op jit(solution)/shard_map/ppermute | solution.py:200
  36.6 19.1 %collective-permute-start.1 = (f32[2,512]{1,0:T(2,128)S(1)}, f32[2,512]{1,0:T(2,128)S(1)}, u32[]{:S(2)}, u32[]{:S(2)}) collective-permute-start(f32[2,512]{1,0:T(2,128)S(1)} %get-tuple-element.25), channel_id=1, source_target_pairs={{0,16},{16,0},{32,48},{48,32},{64,80},{80,64},{96,112},{112,96},{1... | collective-permute-start | bytes 12296 | tf_op jit(solution)/shard_map/ppermute | solution.py:200
  55.8 0.6 copy-start.3
  63.6 34.6 %all-to-all-start.2 = ((bf16[256,8,128]{2,1,0:T(8,128)(2,1)}), bf16[256,8,128]{2,1,0:T(8,128)(2,1)S(1)}, u32[]{:S(2)}, u32[]{:S(2)}) async-start(bf16[256,8,128]{2,1,0:T(8,128)(2,1)} %bitcast.22), calls=%async_computation.2 | async-start | bytes 1048576 | tf_op jit(solution)/shard_map/all_to_all | solution.py:204
  77.0 18.7 %collective-permute-start.2 = (bf16[1280,128]{1,0:T(8,128)(2,1)S(1)}, bf16[1280,128]{1,0:T(8,128)(2,1)S(1)}, u32[]{:S(2)}, u32[]{:S(2)}) collective-permute-start(bf16[1280,128]{1,0:T(8,128)(2,1)S(1)} %get-tuple-element.11), channel_id=1, source_target_pairs={{0,16},{16,0},{32,48},{48,32},{64,80},{80,64},{96,112},{112,96},{1... | collective-permute-start | bytes 983048 | tf_op jit(solution)/shard_map/ppermute | solution.py:200
  100.0 13.2 %all-to-all-start.3 = ((bf16[32,2,8,128]{3,2,1,0:T(8,128)(2,1)}), bf16[32,2,8,128]{3,2,1,0:T(8,128)(2,1)S(1)}, u32[]{:S(2)}, u32[]{:S(2)}) async-start(bf16[32,2,8,128]{3,2,1,0:T(8,128)(2,1)} %shard_map.97), calls=%async_computation.3 | async-start | bytes 262144 | tf_op jit(solution)/shard_map/all_to_all | solution.py:204

commit v5 on v4

--- a/solution.py
+++ b/solution.py
@@ -17,6 +17,7 @@
 piece = 16 // share
 window = span + share * chunk
 columns = chunk * group
+merged = 2
 row_axes = ("yh", "x", "c", "yl", "z")
 plane_axes = ("yl", "yh", "x", "c")
 all_axes = ("yl", "yh", "x", "c", "z")
@@ -31,48 +32,39 @@
     )
 
 
-def place_spans(order_ref, place_ref):
+def expand_kernel(table_ref, pieces_ref, out_ref, plan_ref, prev_ref):
+    pltpu.sync_copy(table_ref, plan_ref)
+    z = plan_ref[0, 64]
     for p in range(32):
-        place_ref[order_ref[p % 16, p // 16]] = p
-
-
-def later(j, z):
-    return j // share > lax.div(z, share)
-
-
-def expand_kernel(order_ref, meta_ref, pieces_ref, out_ref, place_ref, prev_ref):
-    place_spans(order_ref, place_ref)
-    z = meta_ref[2]
-    for p in range(32):
-        before = place_ref[jnp.maximum(order_ref[p % 16, p // 16] - 1, 0)]
-        prev_ref[p] = pieces_ref[before]
+        prev_ref[p] = pieces_ref[plan_ref[0, p]]
     for j in range(8):
-        @pl.when(later(j, z))
+        later = j // share > lax.div(z, share)
+
+        @pl.when(later)
         def _():
             out_ref[:, j] = pieces_ref[:, j % share]
 
-        @pl.when(jnp.logical_not(later(j, z)))
+        @pl.when(jnp.logical_not(later))
         def _():
             out_ref[:, j] = prev_ref[:, j % share]
 
 
-def reduce_kernel(order_ref, meta_ref, parts_ref, out_ref, place_ref, own_ref, prev_ref):
-    place_spans(order_ref, place_ref)
-    z = meta_ref[2]
+def reduce_kernel(table_ref, parts_ref, out_ref, plan_ref, own_ref, prev_ref):
+    pltpu.sync_copy(table_ref, plan_ref)
+    z = plan_ref[0, 64]
+    prev_ref[32] = jnp.zeros((share, piece, width), jnp.float32)
     for e in range(share):
         own = jnp.zeros((32, piece, width), jnp.float32)
         prev = jnp.zeros((32, piece, width), jnp.float32)
         for j in range(e, 8, share):
+            later = j // share > lax.div(z, share)
             part = parts_ref[:, j].astype(jnp.float32)
-            own = own + jnp.where(later(j, z), part, 0.0)
-            prev = prev + jnp.where(later(j, z), 0.0, part)
+            own = own + jnp.where(later, part, 0.0)
+            prev = prev + jnp.where(later, 0.0, part)
         own_ref[:, e] = own
-        prev_ref[:, e] = prev
+        prev_ref[:32, e] = prev
     for p in range(32):
-        here = order_ref[p % 16, p // 16]
-        after = place_ref[jnp.minimum(here + 1, 31)]
-        total = own_ref[p] + jnp.where(here < 31, prev_ref[after], 0.0)
-        out_ref[p] = total.astype(out_ref.dtype)
+        out_ref[p] = (own_ref[p] + prev_ref[plan_ref[0, 32 + p]]).astype(out_ref.dtype)
 
 
 def delta_kernel(grad_ref, out_ref, delta_ref):
@@ -88,33 +80,15 @@
 
 
 def attention_kernel(*refs):
-    order_ref, lengths_ref, meta_ref = refs[:3]
-    message_refs = refs[3 : 3 + share]
-    delta_refs = refs[3 + share : 3 + 2 * share]
-    window_ref = refs[3 + 2 * share]
-    results = refs[4 + 2 * share :]
+    info_ref = refs[0]
+    message_refs = refs[1 : 1 + share]
+    delta_refs = refs[1 + share : 1 + 2 * share]
+    window_ref = refs[1 + 2 * share]
+    results = refs[2 + 2 * share :]
     result_refs = results[:share]
     own_grad_ref, window_grad_ref, bias_ref, key_acc_ref, value_acc_ref = results[share:]
-    place = meta_ref[2]
-    current = order_ref[meta_ref[0], meta_ref[1]]
-    base = (current - 1) * span
-    token = lax.shift_right_logical(
-        lax.broadcasted_iota(jnp.int32, (1, columns), 1), 3
-    )
-    lasts = [span + (place ^ b) * chunk + token for b in range(share)]
-
-    def doc(i, carry):
-        end, lows = carry
-        end = end + lengths_ref[i]
-        return end, tuple(
-            jnp.where(end <= last, jnp.maximum(low, end), low)
-            for low, last in zip(lows, lasts)
-        )
-
-    first_end = jnp.int32(0) - base
-    low_start = jnp.zeros((1, columns), jnp.int32) + first_end
-    _, lows = lax.fori_loop(0, 63, doc, (first_end, (low_start,) * share))
-    row = lax.broadcasted_iota(jnp.int32, (window, columns), 0)
+    place = info_ref[share : share + 1, :width]
+    row = lax.broadcasted_iota(jnp.int32, (window, width), 0)
     stretch = lax.shift_right_logical(row, 6)
     source = lax.div(row, piece) & 7
     inside = lax.div(row, 8 * piece) * piece + (row & (piece - 1))
@@ -132,23 +106,34 @@
         return message_refs[b][start : start + chunk]
 
     for b in range(share):
-        allowed = (key_at <= lasts[b]) & (key_at >= lows[b])
-        bias_ref[...] = jnp.where(allowed, 0.0, masked)
-        for h in range(local_kv):
-            query = message_refs[b][h * columns : (h + 1) * columns]
-            grad = message_refs[b][(local_kv + h) * columns : (local_kv + h + 1) * columns]
-            delta = delta_refs[b][h : h + 1]
-            key = jnp.concatenate(
-                [window_ref[h, 0]]
-                + [own_rows(k, h, 0) for k in range(share)],
-                axis=0,
-            )
-            value = jnp.concatenate(
-                [window_ref[h, 1]]
-                + [own_rows(k, h, 1) for k in range(share)],
-                axis=0,
-            )
-            scores = nt(key, query) * (factor * log2e) + bias_ref[...]
+        for c in range(0, columns, width):
+            token = lax.shift_right_logical(
+                c + lax.broadcasted_iota(jnp.int32, (1, width), 1), 3
+            )
+            last = span + (place ^ b) * chunk + token
+            allowed = (key_at <= last) & (key_at >= info_ref[b : b + 1, c : c + width])
+            bias_ref[:, b * columns + c : b * columns + c + width] = jnp.where(
+                allowed, 0.0, masked
+            )
+    for h in range(local_kv):
+        key = jnp.concatenate(
+            [window_ref[h, 0]] + [own_rows(k, h, 0) for k in range(share)], axis=0
+        )
+        value = jnp.concatenate(
+            [window_ref[h, 1]] + [own_rows(k, h, 1) for k in range(share)], axis=0
+        )
+        for b in range(0, share, merged):
+            several = range(b, b + merged)
+            query = jnp.concatenate(
+                [message_refs[k][h * columns : (h + 1) * columns] for k in several], axis=0
+            )
+            start = (local_kv + h) * columns
+            grad = jnp.concatenate(
+                [message_refs[k][start : start + columns] for k in several], axis=0
+            )
+            delta = jnp.concatenate([delta_refs[k][h : h + 1] for k in several], axis=1)
+            bias = bias_ref[:, b * columns : (b + merged) * columns]
+            scores = nt(key, query) * (factor * log2e) + bias
             top = jnp.max(scores, axis=0, keepdims=True)
             exps = jnp.exp2(scores - top)
             total = jnp.sum(exps, axis=0, keepdims=True)
@@ -161,13 +146,15 @@
             query_part = lax.dot_general(
                 key, grad_scores, (((0,), (0,)), ((), ())), preferred_element_type=jnp.float32
             )
-            result_refs[b][h * columns : (h + 1) * columns] = (
-                jnp.transpose(query_part) * factor
-            ).astype(low)
+            query_part = (jnp.transpose(query_part) * factor).astype(low)
+            for k in several:
+                result_refs[k][h * columns : (h + 1) * columns] = query_part[
+                    (k - b) * columns : (k - b + 1) * columns
+                ]
             if b > 0:
                 key_part = key_part + key_acc_ref[h]
                 value_part = value_part + value_acc_ref[h]
-            if b < share - 1:
+            if b + merged < share:
                 key_acc_ref[h] = key_part
                 value_acc_ref[h] = value_part
             else:
@@ -188,6 +175,10 @@
 vmem = pl.BlockSpec(memory_space=pltpu.VMEM)
 
 
+def grant(mib):
+    return pltpu.CompilerParams(vmem_limit_bytes=mib * 2**20)
+
+
 def near(array):
     return pltpu.with_memory_space_constraint(array, pltpu.VMEM)
 
@@ -202,18 +193,43 @@
 
 def route(array, axes):
     return lax.all_to_all(array, axes, split_axis=0, concat_axis=0, tiled=True)
+
+
+def plan(span_order, z):
+    spans = jnp.transpose(span_order).reshape(32)
+    kind = lax.broadcasted_iota(jnp.int32, (4, 32, 32), 0)
+    other = lax.broadcasted_iota(jnp.int32, (4, 32, 32), 2)
+    wanted = spans[None, :, None] + jnp.where(kind == 0, -1, 1)
+    found = jnp.where(kind == 0, other, other - 32)
+    found = jnp.sum(jnp.where(spans[None, None, :] == wanted, found, 0), axis=2)
+    kind = lax.broadcasted_iota(jnp.int32, (4, 32), 0)
+    found = jnp.where(kind == 2, z, found + jnp.where(kind == 1, 32, 0))
+    return near(found.reshape(1, 128))
+
+
+def bounds(span_order, doc_lengths, query_index, half, z):
+    base = (span_order[query_index, half] - 1) * span
+    ends = jnp.cumsum(doc_lengths)
+    block = lax.broadcasted_iota(jnp.int32, (share, chunk, 64), 0)
+    token = lax.broadcasted_iota(jnp.int32, (share, chunk, 64), 1)
+    at = base + span + (z ^ block) * chunk + token
+    lows = jnp.max(jnp.where(ends[None, None, :] <= at, ends[None, None, :], 0), axis=2) - base
+    lows = jnp.broadcast_to(lows[:, :, None], (share, chunk, group)).reshape(share, columns)
+    places = jnp.broadcast_to(z, (1, columns)).astype(jnp.int32)
+    return near(jnp.concatenate([lows, places], axis=0))
 
 
 def shards(queries, keys, values, attention_out, out_grad, span_order, doc_lengths):
     z = lax.axis_index("z")
     mine = lax.rem(z, share)
     query_index = (lax.axis_index("yh") * 4 + lax.axis_index("x")) * 2 + lax.axis_index("c")
-    meta = jnp.stack([query_index, lax.axis_index("yl"), z]).astype(jnp.int32)
+    table = plan(span_order, z)
     own = jnp.stack([jnp.transpose(keys, (1, 0, 2)), jnp.transpose(values, (1, 0, 2))], axis=1)
     own = own.reshape(share, 32, piece, width)
     pieces = route(jnp.transpose(own, (1, 0, 2, 3)), plane_axes)
     delta = pl.pallas_call(
         delta_kernel,
+        compiler_params=grant(8),
         out_shape=jax.ShapeDtypeStruct((kv_heads, columns), jnp.float32),
         in_specs=[vmem, vmem],
         out_specs=vmem,
@@ -236,37 +252,37 @@
 
     spread = pl.pallas_call(
         expand_kernel,
+        compiler_params=grant(8),
         out_shape=pltpu.VMEM((32, 8, piece, width), low),
-        in_specs=[smem, smem, vmem],
+        in_specs=[vmem, vmem],
         out_specs=vmem,
         scratch_shapes=[
-            pltpu.SMEM((32,), jnp.int32),
+            pltpu.SMEM((1, 128), jnp.int32),
             pltpu.VMEM((32, share, piece, width), low),
         ],
-    )(span_order, meta, near(pieces))
+    )(table, near(pieces))
     around = route(spread.reshape(256, piece, width), all_axes)
     back_rows = local_kv * (columns + 2 * chunk)
     results = pl.pallas_call(
         attention_kernel,
+        compiler_params=grant(32),
         out_shape=tuple(
             [pltpu.VMEM((local_kv * columns, width), low)]
             + [pltpu.VMEM((back_rows, width), low)] * (share - 1)
             + [pltpu.VMEM((local_kv * 2 * chunk, width), jnp.float32)]
             + [pltpu.VMEM((local_kv, 2, span, width), low)]
         ),
-        in_specs=[smem] * 3 + [vmem] * (2 * share + 1),
+        in_specs=[vmem] * (2 * share + 2),
         out_specs=tuple([vmem] * (share + 2)),
         scratch_shapes=[
-            pltpu.VMEM((window, columns), jnp.float32),
+            pltpu.VMEM((window, share * columns), jnp.float32),
             pltpu.VMEM((local_kv, window, width), jnp.float32),
             pltpu.VMEM((local_kv, window, width), jnp.float32),
         ],
     )(
-        span_order,
-        doc_lengths,
-        meta,
+        bounds(span_order, doc_lengths, query_index, lax.axis_index("yl"), z),
         *[near(m) for m in messages],
-        *deltas,
+        *[near(d) for d in deltas],
         near(around.reshape(local_kv, 2, span, width)),
     )
     parts = route(results[-1].reshape(256, piece, width), all_axes)
@@ -278,15 +294,16 @@
         own_grads.append(got[local_kv * columns :])
     sums = pl.pallas_call(
         reduce_kernel,
+        compiler_params=grant(8),
         out_shape=pltpu.VMEM((32, share, piece, width), low),
-        in_specs=[smem, smem, vmem],
+        in_specs=[vmem, vmem],
         out_specs=vmem,
         scratch_shapes=[
-            pltpu.SMEM((32,), jnp.int32),
+            pltpu.SMEM((1, 128), jnp.int32),
             pltpu.VMEM((32, share, piece, width), jnp.float32),
-            pltpu.VMEM((32, share, piece, width), jnp.float32),
+            pltpu.VMEM((33, share, piece, width), jnp.float32),
         ],
-    )(span_order, meta, near(parts.reshape(32, 8, piece, width)))
+    )(table, near(parts.reshape(32, 8, piece, width)))
     back = route(sums, plane_axes)
 
     def arranged(members):

time: 115 us -> 111 us (0.965)
  Pallas kernels: 13.1 us -> 8.64 us
    pallas_call x4, Pallas kernels: 13.1 us -> 8.64 us  [the longest x1 5.26 us: shards(): pl.pallas_call(attention_kernel, compiler_params=grant(32), out_shape=tup...]
    unnamed x11 -> x12, local copies, waits for them, and re-layouts: 1.28 us -> 0.03 us
  transfers between devices with their start and end apart: 7 -> 7, of which waited for: 5 -> 5; matrix products, arithmetic and copies ran while one was open for 4% -> 4% of each run, Pallas kernels for 2% -> 0%
where the time goes in v5:
time: 111 us
  waiting for transfers between devices  51.7 us (47%)
  starting transfers between devices  41.7 us (38%)
  Pallas kernels  8.64 us (8%)
  local copies, waits for them, and re-layouts  6.32 us (6%)
  between operations  1.54 us (1%)
    all_to_all x4, starting transfers between devices, route(): return lax.all_to_all(array, axes, split_axis=0, concat_axis=0, tiled=True)  38.3 us
    ppermute x3, waiting for transfers between devices, trade(): return lax.ppermute(array, 'z', [(i, i ^ b) for i in range(8)])  36.4 us
    all_to_all x4, waiting for transfers between devices, route(): return lax.all_to_all(array, axes, split_axis=0, concat_axis=0, tiled=True)  15.3 us
    pallas_call x1, Pallas kernels, shards(): pl.pallas_call(attention_kernel, compiler_params=grant(32), out_shape=tup...  5.26 us
    ppermute x3, starting transfers between devices, trade(): return lax.ppermute(array, 'z', [(i, i ^ b) for i in range(8)])  3.35 us
  transfers between devices with their start and end apart: 7, of which 5 were waited for; matrix products, arithmetic and copies ran while one was open for 4% of the time, Pallas kernels for 0%

profile of v5, /device:TPU:1, one launch (start us, length us, event | category | flops | bytes accessed | tf_op | source)
XLA Modules:
  0.0 110.8 jit_solution(6167522567905047937)
XLA Ops:
  0.7 1.0 copy_bitcast_fusion.2
  1.7 0.7 copy.39
  2.3 8.7 %all-to-all-start = ((bf16[32,2,8,128]{3,2,1,0:T(8,128)(2,1)}), bf16[32,2,8,128]{3,2,1,0:T(8,128)(2,1)S(1)}, u32[]{:S(2)}, u32[]{:S(2)}) async-start(bf16[32,2,8,128]{3,2,1,0:T(8,128)(2,1)} %bitcast.59), calls=%async_computation | async-start | bytes 262144 | tf_op jit(solution)/shard_map/all_to_all | solution.py:195
  11.1 0.1 copy.25
  11.2 0.9 copy.26
  12.2 0.2 select_reduce_fusion.1
  12.5 0.1 select_n.85.table_ref
  12.6 6.1 %all-to-all-done.pieces_ref = bf16[32,2,8,128]{3,2,1,0:T(8,128)(2,1)S(1)} async-done(((bf16[32,2,8,128]{3,2,1,0:T(8,128)(2,1)}), bf16[32,2,8,128]{3,2,1,0:T(8,128)(2,1)S(1)}, u32[]{:S(2)}, u32[]{:S(2)}) %all-to-all-start) | async-done | bytes 131104 | tf_op jit(solution)/shard_map/all_to_all | solution.py:195
  18.7 1.5 %shard_map.95 = bf16[32,8,8,128]{3,2,1,0:T(8,128)(2,1)} custom-call(s32[1,128]{1,0:T(1,128)S(1)} %select_n.85.table_ref, bf16[32,2,8,128]{3,2,1,0:T(8,128)(2,1)S(1)} %all-to-all-done.pieces_ref), custom_call_target="tpu_custom_call" | custom-call | tf_op jit(solution)/shard_map/pallas_call | solution.py:253
  20.3 10.8 %all-to-all-start.1 = ((bf16[256,8,128]{2,1,0:T(8,128)(2,1)}), bf16[256,8,128]{2,1,0:T(8,128)(2,1)S(1)}, u32[]{:S(2)}, u32[]{:S(2)}) async-start(bf16[256,8,128]{2,1,0:T(8,128)(2,1)} %bitcast.20), calls=%async_computation.1 | async-start | bytes 1048576 | tf_op jit(solution)/shard_map/all_to_all | solution.py:195
  31.2 0.9 dynamic-slice_bitcast_fusion
  32.1 1.5 %collective-permute-start = (bf16[2304,128]{1,0:T(8,128)(2,1)}, bf16[2304,128]{1,0:T(8,128)(2,1)S(1)}, u32[]{:S(2)}, u32[]{:S(2)}) collective-permute-start(bf16[2304,128]{1,0:T(8,128)(2,1)} %get-tuple-element.17), channel_id=1, source_target_pairs={{0,16},{16,0},{32,48},{48,32},{64,80},{80,64},{96,112},{112,96},{1... | collective-permute-start | bytes 1769480 | tf_op jit(solution)/shard_map/ppermute | solution.py:191
  33.5 0.4 shard_map.94
  34.0 0.3 collective-permute-start.1
  34.3 0.1 copy.24
  34.4 0.1 reduce-window.8
  34.5 0.1 reduce
  34.6 0.6 dynamic_slice.17
  35.9 0.2 select_reduce_fusion
  36.1 0.1 reshape.122
  36.2 19.2 %collective-permute-done.1.refs_4_ = f32[2,512]{1,0:T(2,128)S(1)} collective-permute-done((f32[2,512]{1,0:T(2,128)S(1)}, f32[2,512]{1,0:T(2,128)S(1)}, u32[]{:S(2)}, u32[]{:S(2)}) %collective-permute-start.1) | collective-permute-done | bytes 4128 | tf_op jit(solution)/shard_map/ppermute | solution.py:191
  55.5 5.3 %shard_map.96 = (bf16[1024,128]{1,0:T(8,128)(2,1)S(1)}, bf16[1280,128]{1,0:T(8,128)(2,1)S(1)}, f32[256,128]{1,0:T(8,128)S(1)}, bf16[2,2,512,128]{3,2,1,0:T(8,128)(2,1)}) custom-call(s32[3,512]{1,0:T(4,128)S(1)} %concatenate.7.refs_0_, bf16[2304,128]{1,0:T(8,128)(2,1)S(1)} %get-tuple-element.18.refs_1_, bf16[2304,128]{1,0:T(8,128)(2,1)S(1)} %collective-permute-done.refs_2_, ...), custom_call_target="tpu_custom_call" | custom-call | tf_op jit(solution)/shard_map/pallas_call | solution.py:266
  60.7 13.4 %all-to-all-start.2 = ((bf16[256,8,128]{2,1,0:T(8,128)(2,1)}), bf16[256,8,128]{2,1,0:T(8,128)(2,1)S(1)}, u32[]{:S(2)}, u32[]{:S(2)}) async-start(bf16[256,8,128]{2,1,0:T(8,128)(2,1)} %bitcast.22), calls=%async_computation.2 | async-start | bytes 1048576 | tf_op jit(solution)/shard_map/all_to_all | solution.py:195
  74.1 1.6 %collective-permute-start.2 = (bf16[1280,128]{1,0:T(8,128)(2,1)S(1)}, bf16[1280,128]{1,0:T(8,128)(2,1)S(1)}, u32[]{:S(2)}, u32[]{:S(2)}) collective-permute-start(bf16[1280,128]{1,0:T(8,128)(2,1)S(1)} %get-tuple-element.11), channel_id=1, source_target_pairs={{0,16},{16,0},{32,48},{48,32},{64,80},{80,64},{96,112},{112,96},{1... | collective-permute-start | bytes 983048 | tf_op jit(solution)/shard_map/ppermute | solution.py:191
  75.7 17.2 %collective-permute-done.2 = bf16[1280,128]{1,0:T(8,128)(2,1)S(1)} collective-permute-done((bf16[1280,128]{1,0:T(8,128)(2,1)S(1)}, bf16[1280,128]{1,0:T(8,128)(2,1)S(1)}, u32[]{:S(2)}, u32[]{:S(2)}) %collective-permute-start.2) | collective-permute-done | bytes 327712 | tf_op jit(solution)/shard_map/ppermute | solution.py:191
  92.9 2.4 %all-to-all-done.2 = bf16[256,8,128]{2,1,0:T(8,128)(2,1)S(1)} async-done(((bf16[256,8,128]{2,1,0:T(8,128)(2,1)}), bf16[256,8,128]{2,1,0:T(8,128)(2,1)S(1)}, u32[]{:S(2)}, u32[]{:S(2)}) %all-to-all-start.2) | async-done | bytes 524320 | tf_op jit(solution)/shard_map/all_to_all | solution.py:195
  95.4 1.4 %shard_map.97 = bf16[32,2,8,128]{3,2,1,0:T(8,128)(2,1)} custom-call(s32[1,128]{1,0:T(1,128)S(1)} %select_n.85.table_ref, bf16[32,8,8,128]{3,2,1,0:T(8,128)(2,1)S(1)} %bitcast.62), custom_call_target="tpu_custom_call" | custom-call | tf_op jit(solution)/shard_map/pallas_call | solution.py:295
  96.8 5.5 %all-to-all-start.3 = ((bf16[32,2,8,128]{3,2,1,0:T(8,128)(2,1)}), bf16[32,2,8,128]{3,2,1,0:T(8,128)(2,1)S(1)}, u32[]{:S(2)}, u32[]{:S(2)}) async-start(bf16[32,2,8,128]{3,2,1,0:T(8,128)(2,1)} %shard_map.97), calls=%async_computation.3 | async-start | bytes 262144 | tf_op jit(solution)/shard_map/all_to_all | solution.py:195
  102.4 0.9 copy.30
  103.3 6.7 %all-to-all-done.3 = bf16[32,2,8,128]{3,2,1,0:T(8,128)(2,1)S(1)} async-done(((bf16[32,2,8,128]{3,2,1,0:T(8,128)(2,1)}), bf16[32,2,8,128]{3,2,1,0:T(8,128)(2,1)S(1)}, u32[]{:S(2)}, u32[]{:S(2)}) %all-to-all-start.3) | async-done | bytes 131104 | tf_op jit(solution)/shard_map/all_to_all | solution.py:195
  110.0 0.1 copy.38
  110.1 0.7 slice_bitcast_fusion
  (33 shorter events, 0.6 us)
Async XLA Ops:
  0.6 10.5 %copy-start.3 = (bf16[64,32,128]{2,1,0:T(8,128)(2,1)S(1)}, bf16[64,32,128]{2,1,0:T(8,128)(2,1)}, u32[]{:S(2)}) copy-start(bf16[64,32,128]{2,1,0:T(8,128)(2,1)} %param.7) | copy-start | bytes 1572868
  0.6 10.6 %copy-start = (bf16[64,32,128]{2,1,0:T(8,128)(2,1)S(1)}, bf16[64,32,128]{2,1,0:T(8,128)(2,1)}, u32[]{:S(2)}) copy-start(bf16[64,32,128]{2,1,0:T(8,128)(2,1)} %grad_ref.1) | copy-start | bytes 1572868
  2.3 9.8 %copy-start.5 = (s32[16,2]{0,1:T(2,128)S(1)}, s32[16,2]{0,1:T(2,128)}, u32[]{:S(2)}) copy-start(s32[16,2]{0,1:T(2,128)} %param.12) | copy-start | bytes 388
  2.3 16.4 %all-to-all-start = ((bf16[32,2,8,128]{3,2,1,0:T(8,128)(2,1)}), bf16[32,2,8,128]{3,2,1,0:T(8,128)(2,1)S(1)}, u32[]{:S(2)}, u32[]{:S(2)}) async-start(bf16[32,2,8,128]{3,2,1,0:T(8,128)(2,1)} %bitcast.59), calls=%async_computation | async-start | bytes 262144 | tf_op jit(solution)/shard_map/all_to_all | solution.py:195
  20.3 10.8 %copy-start.2 = (bf16[2,2,64,8,128]{4,3,2,1,0:T(8,128)(2,1)S(1)}, bf16[2,2,64,8,128]{4,3,2,1,0:T(8,128)(2,1)}, u32[]{:S(2)}) copy-start(bf16[2,2,64,8,128]{4,3,2,1,0:T(8,128)(2,1)} %copy.26) | copy-start | bytes 1572868
  20.3 35.2 %all-to-all-start.1 = ((bf16[256,8,128]{2,1,0:T(8,128)(2,1)}), bf16[256,8,128]{2,1,0:T(8,128)(2,1)S(1)}, u32[]{:S(2)}, u32[]{:S(2)}) async-start(bf16[256,8,128]{2,1,0:T(8,128)(2,1)} %bitcast.20), calls=%async_computation.1 | async-start | bytes 1048576 | tf_op jit(solution)/shard_map/all_to_all | solution.py:195
  31.1 2.4 %copy-start.1 = (bf16[64,32,128]{2,1,0:T(8,128)(2,1)S(1)}, bf16[64,32,128]{2,1,0:T(8,128)(2,1)}, u32[]{:S(2)}) copy-start(bf16[64,32,128]{2,1,0:T(8,128)(2,1)} %out_ref.1) | copy-start | bytes 1572868
  31.1 3.1 %copy-start.4 = (s32[64]{0:T(128)S(1)}, s32[64]{0:T(128)}, u32[]{:S(2)}) copy-start(s32[64]{0:T(128)} %param.13) | copy-start | bytes 772
  32.1 23.4 %collective-permute-start = (bf16[2304,128]{1,0:T(8,128)(2,1)}, bf16[2304,128]{1,0:T(8,128)(2,1)S(1)}, u32[]{:S(2)}, u32[]{:S(2)}) collective-permute-start(bf16[2304,128]{1,0:T(8,128)(2,1)} %get-tuple-element.17), channel_id=1, source_target_pairs={{0,16},{16,0},{32,48},{48,32},{64,80},{80,64},{96,112},{112,96},{1... | collective-permute-start | bytes 1769480 | tf_op jit(solution)/shard_map/ppermute | solution.py:191
  34.0 21.5 %collective-permute-start.1 = (f32[2,512]{1,0:T(2,128)S(1)}, f32[2,512]{1,0:T(2,128)S(1)}, u32[]{:S(2)}, u32[]{:S(2)}) collective-permute-start(f32[2,512]{1,0:T(2,128)S(1)} %get-tuple-element.25), channel_id=1, source_target_pairs={{0,16},{16,0},{32,48},{48,32},{64,80},{80,64},{96,112},{112,96},{1... | collective-permute-start | bytes 12296 | tf_op jit(solution)/shard_map/ppermute | solution.py:191
  60.7 34.6 %all-to-all-start.2 = ((bf16[256,8,128]{2,1,0:T(8,128)(2,1)}), bf16[256,8,128]{2,1,0:T(8,128)(2,1)S(1)}, u32[]{:S(2)}, u32[]{:S(2)}) async-start(bf16[256,8,128]{2,1,0:T(8,128)(2,1)} %bitcast.22), calls=%async_computation.2 | async-start | bytes 1048576 | tf_op jit(solution)/shard_map/all_to_all | solution.py:195
  74.1 18.7 %collective-permute-start.2 = (bf16[1280,128]{1,0:T(8,128)(2,1)S(1)}, bf16[1280,128]{1,0:T(8,128)(2,1)S(1)}, u32[]{:S(2)}, u32[]{:S(2)}) collective-permute-start(bf16[1280,128]{1,0:T(8,128)(2,1)S(1)} %get-tuple-element.11), channel_id=1, source_target_pairs={{0,16},{16,0},{32,48},{48,32},{64,80},{80,64},{96,112},{112,96},{1... | collective-permute-start | bytes 983048 | tf_op jit(solution)/shard_map/ppermute | solution.py:191
  96.8 13.2 %all-to-all-start.3 = ((bf16[32,2,8,128]{3,2,1,0:T(8,128)(2,1)}), bf16[32,2,8,128]{3,2,1,0:T(8,128)(2,1)S(1)}, u32[]{:S(2)}, u32[]{:S(2)}) async-start(bf16[32,2,8,128]{3,2,1,0:T(8,128)(2,1)} %shard_map.97), calls=%async_computation.3 | async-start | bytes 262144 | tf_op jit(solution)/shard_map/all_to_all | solution.py:195

commit v6 on v5

--- a/solution.py
+++ b/solution.py
@@ -32,37 +32,43 @@
     )
 
 
-def expand_kernel(table_ref, pieces_ref, out_ref, plan_ref, prev_ref):
-    pltpu.sync_copy(table_ref, plan_ref)
+def expand_kernel(table_ref, pieces_ref, out_ref, plan_ref, prev_ref, sem):
+    fetch = pltpu.make_async_copy(table_ref, plan_ref, sem)
+    fetch.start()
+    for j in range(share, 8):
+        out_ref[:, j] = pieces_ref[:, j % share]
+    fetch.wait()
     z = plan_ref[0, 64]
     for p in range(32):
         prev_ref[p] = pieces_ref[plan_ref[0, p]]
-    for j in range(8):
-        later = j // share > lax.div(z, share)
-
-        @pl.when(later)
+    for j in range(share):
+        out_ref[:, j] = prev_ref[:, j]
+    for j in range(share, 8, share):
+        @pl.when(j // share <= lax.div(z, share))
         def _():
-            out_ref[:, j] = pieces_ref[:, j % share]
-
-        @pl.when(jnp.logical_not(later))
-        def _():
-            out_ref[:, j] = prev_ref[:, j % share]
-
-
-def reduce_kernel(table_ref, parts_ref, out_ref, plan_ref, own_ref, prev_ref):
-    pltpu.sync_copy(table_ref, plan_ref)
-    z = plan_ref[0, 64]
+            for e in range(share):
+                out_ref[:, j + e] = prev_ref[:, e]
+
+
+def reduce_kernel(table_ref, parts_ref, out_ref, plan_ref, own_ref, prev_ref, sem):
+    fetch = pltpu.make_async_copy(table_ref, plan_ref, sem)
+    fetch.start()
+    z = jnp.max(jnp.broadcast_to(table_ref[0:1, 64:65], (piece, width)), axis=0, keepdims=True)
+    mask = [
+        jnp.broadcast_to(j // share > lax.div(z, share), (piece, width))[None]
+        for j in range(8)
+    ]
     prev_ref[32] = jnp.zeros((share, piece, width), jnp.float32)
     for e in range(share):
         own = jnp.zeros((32, piece, width), jnp.float32)
         prev = jnp.zeros((32, piece, width), jnp.float32)
         for j in range(e, 8, share):
-            later = j // share > lax.div(z, share)
             part = parts_ref[:, j].astype(jnp.float32)
-            own = own + jnp.where(later, part, 0.0)
-            prev = prev + jnp.where(later, 0.0, part)
+            own = own + jnp.where(mask[j], part, 0.0)
+            prev = prev + jnp.where(mask[j], 0.0, part)
         own_ref[:, e] = own
         prev_ref[:32, e] = prev
+    fetch.wait()
     for p in range(32):
         out_ref[p] = (own_ref[p] + prev_ref[plan_ref[0, 32 + p]]).astype(out_ref.dtype)
 
@@ -259,6 +265,7 @@
         scratch_shapes=[
             pltpu.SMEM((1, 128), jnp.int32),
             pltpu.VMEM((32, share, piece, width), low),
+            pltpu.SemaphoreType.DMA(()),
         ],
     )(table, near(pieces))
     around = route(spread.reshape(256, piece, width), all_axes)
@@ -302,6 +309,7 @@
             pltpu.SMEM((1, 128), jnp.int32),
             pltpu.VMEM((32, share, piece, width), jnp.float32),
             pltpu.VMEM((33, share, piece, width), jnp.float32),
+            pltpu.SemaphoreType.DMA(()),
         ],
     )(table, near(parts.reshape(32, 8, piece, width)))
     back = route(sums, plane_axes)

time: 111 us -> 111 us (level)
  no operation moved by 1% of the time
where the time goes in v6:
time: 111 us
  waiting for transfers between devices  51.7 us (47%)
  starting transfers between devices  41.7 us (38%)
  Pallas kernels  8.3 us (7%)
  local copies, waits for them, and re-layouts  6.32 us (6%)
  between operations  1.57 us (1%)
    all_to_all x4, starting transfers between devices, route(): return lax.all_to_all(array, axes, split_axis=0, concat_axis=0, tiled=True)  38.4 us
    ppermute x3, waiting for transfers between devices, trade(): return lax.ppermute(array, 'z', [(i, i ^ b) for i in range(8)])  36.4 us
    all_to_all x4, waiting for transfers between devices, route(): return lax.all_to_all(array, axes, split_axis=0, concat_axis=0, tiled=True)  15.3 us
    pallas_call x1, Pallas kernels, shards(): pl.pallas_call(attention_kernel, compiler_params=grant(32), out_shape=tup...  5.27 us
    ppermute x3, starting transfers between devices, trade(): return lax.ppermute(array, 'z', [(i, i ^ b) for i in range(8)])  3.35 us
  transfers between devices with their start and end apart: 7, of which 5 were waited for; matrix products, arithmetic and copies ran while one was open for 4% of the time, Pallas kernels for 0%

profile of v6, /device:TPU:1, one launch (start us, length us, event | category | flops | bytes accessed | tf_op | source)
XLA Modules:
  0.0 110.6 jit_solution(16014814071033414989)
XLA Ops:
  0.7 1.0 copy_bitcast_fusion.2
  1.7 0.7 copy.39
  2.3 8.7 %all-to-all-start = ((bf16[32,2,8,128]{3,2,1,0:T(8,128)(2,1)}), bf16[32,2,8,128]{3,2,1,0:T(8,128)(2,1)S(1)}, u32[]{:S(2)}, u32[]{:S(2)}) async-start(bf16[32,2,8,128]{3,2,1,0:T(8,128)(2,1)} %bitcast.59), calls=%async_computation | async-start | bytes 262144 | tf_op jit(solution)/shard_map/all_to_all | solution.py:201
  11.1 0.1 copy.25
  11.2 0.9 copy.26
  12.2 0.2 select_reduce_fusion.1
  12.5 0.1 select_n.85.table_ref
  12.6 6.1 %all-to-all-done.pieces_ref = bf16[32,2,8,128]{3,2,1,0:T(8,128)(2,1)S(1)} async-done(((bf16[32,2,8,128]{3,2,1,0:T(8,128)(2,1)}), bf16[32,2,8,128]{3,2,1,0:T(8,128)(2,1)S(1)}, u32[]{:S(2)}, u32[]{:S(2)}) %all-to-all-start) | async-done | bytes 131104 | tf_op jit(solution)/shard_map/all_to_all | solution.py:201
  18.7 1.4 %shard_map.95 = bf16[32,8,8,128]{3,2,1,0:T(8,128)(2,1)} custom-call(s32[1,128]{1,0:T(1,128)S(1)} %select_n.85.table_ref, bf16[32,2,8,128]{3,2,1,0:T(8,128)(2,1)S(1)} %all-to-all-done.pieces_ref), custom_call_target="tpu_custom_call" | custom-call | tf_op jit(solution)/shard_map/pallas_call | solution.py:259
  20.1 10.8 %all-to-all-start.1 = ((bf16[256,8,128]{2,1,0:T(8,128)(2,1)}), bf16[256,8,128]{2,1,0:T(8,128)(2,1)S(1)}, u32[]{:S(2)}, u32[]{:S(2)}) async-start(bf16[256,8,128]{2,1,0:T(8,128)(2,1)} %bitcast.20), calls=%async_computation.1 | async-start | bytes 1048576 | tf_op jit(solution)/shard_map/all_to_all | solution.py:201
  31.1 0.9 dynamic-slice_bitcast_fusion
  32.0 1.5 %collective-permute-start = (bf16[2304,128]{1,0:T(8,128)(2,1)}, bf16[2304,128]{1,0:T(8,128)(2,1)S(1)}, u32[]{:S(2)}, u32[]{:S(2)}) collective-permute-start(bf16[2304,128]{1,0:T(8,128)(2,1)} %get-tuple-element.17), channel_id=1, source_target_pairs={{0,16},{16,0},{32,48},{48,32},{64,80},{80,64},{96,112},{112,96},{1... | collective-permute-start | bytes 1769480 | tf_op jit(solution)/shard_map/ppermute | solution.py:197
  33.5 0.4 shard_map.94
  33.9 0.3 collective-permute-start.1
  34.2 0.1 copy.24
  34.3 0.1 reduce-window.8
  34.4 0.1 reduce
  34.5 0.6 dynamic_slice.17
  35.8 0.2 select_reduce_fusion
  36.0 0.1 reshape.122
  36.2 19.2 %collective-permute-done.1.refs_4_ = f32[2,512]{1,0:T(2,128)S(1)} collective-permute-done((f32[2,512]{1,0:T(2,128)S(1)}, f32[2,512]{1,0:T(2,128)S(1)}, u32[]{:S(2)}, u32[]{:S(2)}) %collective-permute-start.1) | collective-permute-done | bytes 4128 | tf_op jit(solution)/shard_map/ppermute | solution.py:197
  55.4 5.3 %shard_map.96 = (bf16[1024,128]{1,0:T(8,128)(2,1)S(1)}, bf16[1280,128]{1,0:T(8,128)(2,1)S(1)}, f32[256,128]{1,0:T(8,128)S(1)}, bf16[2,2,512,128]{3,2,1,0:T(8,128)(2,1)}) custom-call(s32[3,512]{1,0:T(4,128)S(1)} %concatenate.7.refs_0_, bf16[2304,128]{1,0:T(8,128)(2,1)S(1)} %get-tuple-element.18.refs_1_, bf16[2304,128]{1,0:T(8,128)(2,1)S(1)} %collective-permute-done.refs_2_, ...), custom_call_target="tpu_custom_call" | custom-call | tf_op jit(solution)/shard_map/pallas_call | solution.py:273
  60.7 13.4 %all-to-all-start.2 = ((bf16[256,8,128]{2,1,0:T(8,128)(2,1)}), bf16[256,8,128]{2,1,0:T(8,128)(2,1)S(1)}, u32[]{:S(2)}, u32[]{:S(2)}) async-start(bf16[256,8,128]{2,1,0:T(8,128)(2,1)} %bitcast.22), calls=%async_computation.2 | async-start | bytes 1048576 | tf_op jit(solution)/shard_map/all_to_all | solution.py:201
  74.0 1.6 %collective-permute-start.2 = (bf16[1280,128]{1,0:T(8,128)(2,1)S(1)}, bf16[1280,128]{1,0:T(8,128)(2,1)S(1)}, u32[]{:S(2)}, u32[]{:S(2)}) collective-permute-start(bf16[1280,128]{1,0:T(8,128)(2,1)S(1)} %get-tuple-element.11), channel_id=1, source_target_pairs={{0,16},{16,0},{32,48},{48,32},{64,80},{80,64},{96,112},{112,96},{1... | collective-permute-start | bytes 983048 | tf_op jit(solution)/shard_map/ppermute | solution.py:197
  75.6 17.2 %collective-permute-done.2 = bf16[1280,128]{1,0:T(8,128)(2,1)S(1)} collective-permute-done((bf16[1280,128]{1,0:T(8,128)(2,1)S(1)}, bf16[1280,128]{1,0:T(8,128)(2,1)S(1)}, u32[]{:S(2)}, u32[]{:S(2)}) %collective-permute-start.2) | collective-permute-done | bytes 327712 | tf_op jit(solution)/shard_map/ppermute | solution.py:197
  92.8 2.4 %all-to-all-done.2 = bf16[256,8,128]{2,1,0:T(8,128)(2,1)S(1)} async-done(((bf16[256,8,128]{2,1,0:T(8,128)(2,1)}), bf16[256,8,128]{2,1,0:T(8,128)(2,1)S(1)}, u32[]{:S(2)}, u32[]{:S(2)}) %all-to-all-start.2) | async-done | bytes 524320 | tf_op jit(solution)/shard_map/all_to_all | solution.py:201
  95.3 1.2 %shard_map.97 = bf16[32,2,8,128]{3,2,1,0:T(8,128)(2,1)} custom-call(s32[1,128]{1,0:T(1,128)S(1)} %select_n.85.table_ref, bf16[32,8,8,128]{3,2,1,0:T(8,128)(2,1)S(1)} %bitcast.62), custom_call_target="tpu_custom_call" | custom-call | tf_op jit(solution)/shard_map/pallas_call | solution.py:302
  96.5 5.5 %all-to-all-start.3 = ((bf16[32,2,8,128]{3,2,1,0:T(8,128)(2,1)}), bf16[32,2,8,128]{3,2,1,0:T(8,128)(2,1)S(1)}, u32[]{:S(2)}, u32[]{:S(2)}) async-start(bf16[32,2,8,128]{3,2,1,0:T(8,128)(2,1)} %shard_map.97), calls=%async_computation.3 | async-start | bytes 262144 | tf_op jit(solution)/shard_map/all_to_all | solution.py:201
  102.1 0.9 copy.30
  103.0 6.7 %all-to-all-done.3 = bf16[32,2,8,128]{3,2,1,0:T(8,128)(2,1)S(1)} async-done(((bf16[32,2,8,128]{3,2,1,0:T(8,128)(2,1)}), bf16[32,2,8,128]{3,2,1,0:T(8,128)(2,1)S(1)}, u32[]{:S(2)}, u32[]{:S(2)}) %all-to-all-start.3) | async-done | bytes 131104 | tf_op jit(solution)/shard_map/all_to_all | solution.py:201
  109.7 0.1 copy.38
  109.9 0.7 slice_bitcast_fusion
  (33 shorter events, 0.6 us)
Async XLA Ops:
  0.6 10.5 %copy-start.3 = (bf16[64,32,128]{2,1,0:T(8,128)(2,1)S(1)}, bf16[64,32,128]{2,1,0:T(8,128)(2,1)}, u32[]{:S(2)}) copy-start(bf16[64,32,128]{2,1,0:T(8,128)(2,1)} %param.7) | copy-start | bytes 1572868
  0.6 10.6 %copy-start = (bf16[64,32,128]{2,1,0:T(8,128)(2,1)S(1)}, bf16[64,32,128]{2,1,0:T(8,128)(2,1)}, u32[]{:S(2)}) copy-start(bf16[64,32,128]{2,1,0:T(8,128)(2,1)} %grad_ref.1) | copy-start | bytes 1572868
  2.3 9.8 %copy-start.5 = (s32[16,2]{0,1:T(2,128)S(1)}, s32[16,2]{0,1:T(2,128)}, u32[]{:S(2)}) copy-start(s32[16,2]{0,1:T(2,128)} %param.12) | copy-start | bytes 388
  2.3 16.4 %all-to-all-start = ((bf16[32,2,8,128]{3,2,1,0:T(8,128)(2,1)}), bf16[32,2,8,128]{3,2,1,0:T(8,128)(2,1)S(1)}, u32[]{:S(2)}, u32[]{:S(2)}) async-start(bf16[32,2,8,128]{3,2,1,0:T(8,128)(2,1)} %bitcast.59), calls=%async_computation | async-start | bytes 262144 | tf_op jit(solution)/shard_map/all_to_all | solution.py:201
  20.1 10.8 %copy-start.2 = (bf16[2,2,64,8,128]{4,3,2,1,0:T(8,128)(2,1)S(1)}, bf16[2,2,64,8,128]{4,3,2,1,0:T(8,128)(2,1)}, u32[]{:S(2)}) copy-start(bf16[2,2,64,8,128]{4,3,2,1,0:T(8,128)(2,1)} %copy.26) | copy-start | bytes 1572868
  20.1 35.2 %all-to-all-start.1 = ((bf16[256,8,128]{2,1,0:T(8,128)(2,1)}), bf16[256,8,128]{2,1,0:T(8,128)(2,1)S(1)}, u32[]{:S(2)}, u32[]{:S(2)}) async-start(bf16[256,8,128]{2,1,0:T(8,128)(2,1)} %bitcast.20), calls=%async_computation.1 | async-start | bytes 1048576 | tf_op jit(solution)/shard_map/all_to_all | solution.py:201
  31.0 2.4 %copy-start.1 = (bf16[64,32,128]{2,1,0:T(8,128)(2,1)S(1)}, bf16[64,32,128]{2,1,0:T(8,128)(2,1)}, u32[]{:S(2)}) copy-start(bf16[64,32,128]{2,1,0:T(8,128)(2,1)} %out_ref.1) | copy-start | bytes 1572868
  31.1 3.1 %copy-start.4 = (s32[64]{0:T(128)S(1)}, s32[64]{0:T(128)}, u32[]{:S(2)}) copy-start(s32[64]{0:T(128)} %param.13) | copy-start | bytes 772
  32.0 23.4 %collective-permute-start = (bf16[2304,128]{1,0:T(8,128)(2,1)}, bf16[2304,128]{1,0:T(8,128)(2,1)S(1)}, u32[]{:S(2)}, u32[]{:S(2)}) collective-permute-start(bf16[2304,128]{1,0:T(8,128)(2,1)} %get-tuple-element.17), channel_id=1, source_target_pairs={{0,16},{16,0},{32,48},{48,32},{64,80},{80,64},{96,112},{112,96},{1... | collective-permute-start | bytes 1769480 | tf_op jit(solution)/shard_map/ppermute | solution.py:197
  33.9 21.5 %collective-permute-start.1 = (f32[2,512]{1,0:T(2,128)S(1)}, f32[2,512]{1,0:T(2,128)S(1)}, u32[]{:S(2)}, u32[]{:S(2)}) collective-permute-start(f32[2,512]{1,0:T(2,128)S(1)} %get-tuple-element.25), channel_id=1, source_target_pairs={{0,16},{16,0},{32,48},{48,32},{64,80},{80,64},{96,112},{112,96},{1... | collective-permute-start | bytes 12296 | tf_op jit(solution)/shard_map/ppermute | solution.py:197
  60.7 34.6 %all-to-all-start.2 = ((bf16[256,8,128]{2,1,0:T(8,128)(2,1)}), bf16[256,8,128]{2,1,0:T(8,128)(2,1)S(1)}, u32[]{:S(2)}, u32[]{:S(2)}) async-start(bf16[256,8,128]{2,1,0:T(8,128)(2,1)} %bitcast.22), calls=%async_computation.2 | async-start | bytes 1048576 | tf_op jit(solution)/shard_map/all_to_all | solution.py:201
  74.0 18.7 %collective-permute-start.2 = (bf16[1280,128]{1,0:T(8,128)(2,1)S(1)}, bf16[1280,128]{1,0:T(8,128)(2,1)S(1)}, u32[]{:S(2)}, u32[]{:S(2)}) collective-permute-start(bf16[1280,128]{1,0:T(8,128)(2,1)S(1)} %get-tuple-element.11), channel_id=1, source_target_pairs={{0,16},{16,0},{32,48},{48,32},{64,80},{80,64},{96,112},{112,96},{1... | collective-permute-start | bytes 983048 | tf_op jit(solution)/shard_map/ppermute | solution.py:197
  96.5 13.2 %all-to-all-start.3 = ((bf16[32,2,8,128]{3,2,1,0:T(8,128)(2,1)}), bf16[32,2,8,128]{3,2,1,0:T(8,128)(2,1)S(1)}, u32[]{:S(2)}, u32[]{:S(2)}) async-start(bf16[32,2,8,128]{3,2,1,0:T(8,128)(2,1)} %shard_map.97), calls=%async_computation.3 | async-start | bytes 262144 | tf_op jit(solution)/shard_map/all_to_all | solution.py:201

commit v7 on v6

--- a/solution.py
+++ b/solution.py
@@ -96,11 +96,12 @@
     place = info_ref[share : share + 1, :width]
     row = lax.broadcasted_iota(jnp.int32, (window, width), 0)
     stretch = lax.shift_right_logical(row, 6)
-    source = lax.div(row, piece) & 7
-    inside = lax.div(row, 8 * piece) * piece + (row & (piece - 1))
+    shift = piece.bit_length() - 1
+    source = lax.shift_right_logical(row, shift) & 7
+    inside = lax.shift_right_logical(row, shift + 3) * piece + (row & (piece - 1))
     key_at = source * chunk + inside
     key_at = jnp.where(
-        lax.div(source, share) >= lax.div(place, share), key_at, key_at + span
+        (source | (share - 1)) >= place, key_at, key_at + span
     )
     for b in range(share):
         key_at = jnp.where(
@@ -117,7 +118,8 @@
                 c + lax.broadcasted_iota(jnp.int32, (1, width), 1), 3
             )
             last = span + (place ^ b) * chunk + token
-            allowed = (key_at <= last) & (key_at >= info_ref[b : b + 1, c : c + width])
+            first = info_ref[b : b + 1, c : c + width]
+            allowed = (key_at - first).astype(jnp.uint32) <= (last - first).astype(jnp.uint32)
             bias_ref[:, b * columns + c : b * columns + c + width] = jnp.where(
                 allowed, 0.0, masked
             )

time: 111 us -> 111 us (level)
  no operation moved by 1% of the time
where the time goes in v7:
time: 111 us; the launch traced here: 110 us
  waiting for transfers between devices  51.7 us (47%)
  starting transfers between devices  41.7 us (38%)
  Pallas kernels  8.23 us (7%)
  local copies, waits for them, and re-layouts  6.32 us (6%)
  between operations  1.57 us (1%)
    all_to_all x4, starting transfers between devices, route(): return lax.all_to_all(array, axes, split_axis=0, concat_axis=0, tiled=True)  38.4 us
    ppermute x3, waiting for transfers between devices, trade(): return lax.ppermute(array, 'z', [(i, i ^ b) for i in range(8)])  36.4 us
    all_to_all x4, waiting for transfers between devices, route(): return lax.all_to_all(array, axes, split_axis=0, concat_axis=0, tiled=True)  15.3 us
    pallas_call x1, Pallas kernels, shards(): pl.pallas_call(attention_kernel, compiler_params=grant(32), out_shape=tup...  5.2 us
    ppermute x3, starting transfers between devices, trade(): return lax.ppermute(array, 'z', [(i, i ^ b) for i in range(8)])  3.35 us
  transfers between devices with their start and end apart: 7, of which 5 were waited for; matrix products, arithmetic and copies ran while one was open for 4% of the time, Pallas kernels for 0%

profile of v7, /device:TPU:1, one launch (start us, length us, event | category | flops | bytes accessed | tf_op | source)
XLA Modules:
  0.0 110.5 jit_solution(4025491613290570444)
XLA Ops:
  0.7 1.0 copy_bitcast_fusion.2
  1.7 0.7 copy.39
  2.3 8.7 %all-to-all-start = ((bf16[32,2,8,128]{3,2,1,0:T(8,128)(2,1)}), bf16[32,2,8,128]{3,2,1,0:T(8,128)(2,1)S(1)}, u32[]{:S(2)}, u32[]{:S(2)}) async-start(bf16[32,2,8,128]{3,2,1,0:T(8,128)(2,1)} %bitcast.59), calls=%async_computation | async-start | bytes 262144 | tf_op jit(solution)/shard_map/all_to_all | solution.py:203
  11.1 0.1 copy.25
  11.2 0.9 copy.26
  12.2 0.2 select_reduce_fusion.1
  12.5 0.1 select_n.85.table_ref
  12.6 6.1 %all-to-all-done.pieces_ref = bf16[32,2,8,128]{3,2,1,0:T(8,128)(2,1)S(1)} async-done(((bf16[32,2,8,128]{3,2,1,0:T(8,128)(2,1)}), bf16[32,2,8,128]{3,2,1,0:T(8,128)(2,1)S(1)}, u32[]{:S(2)}, u32[]{:S(2)}) %all-to-all-start) | async-done | bytes 131104 | tf_op jit(solution)/shard_map/all_to_all | solution.py:203
  18.7 1.4 %shard_map.95 = bf16[32,8,8,128]{3,2,1,0:T(8,128)(2,1)} custom-call(s32[1,128]{1,0:T(1,128)S(1)} %select_n.85.table_ref, bf16[32,2,8,128]{3,2,1,0:T(8,128)(2,1)S(1)} %all-to-all-done.pieces_ref), custom_call_target="tpu_custom_call" | custom-call | tf_op jit(solution)/shard_map/pallas_call | solution.py:261
  20.1 10.8 %all-to-all-start.1 = ((bf16[256,8,128]{2,1,0:T(8,128)(2,1)}), bf16[256,8,128]{2,1,0:T(8,128)(2,1)S(1)}, u32[]{:S(2)}, u32[]{:S(2)}) async-start(bf16[256,8,128]{2,1,0:T(8,128)(2,1)} %bitcast.20), calls=%async_computation.1 | async-start | bytes 1048576 | tf_op jit(solution)/shard_map/all_to_all | solution.py:203
  31.1 0.9 dynamic-slice_bitcast_fusion
  32.0 1.5 %collective-permute-start = (bf16[2304,128]{1,0:T(8,128)(2,1)}, bf16[2304,128]{1,0:T(8,128)(2,1)S(1)}, u32[]{:S(2)}, u32[]{:S(2)}) collective-permute-start(bf16[2304,128]{1,0:T(8,128)(2,1)} %get-tuple-element.17), channel_id=1, source_target_pairs={{0,16},{16,0},{32,48},{48,32},{64,80},{80,64},{96,112},{112,96},{1... | collective-permute-start | bytes 1769480 | tf_op jit(solution)/shard_map/ppermute | solution.py:199
  33.5 0.4 shard_map.94
  33.9 0.3 collective-permute-start.1
  34.2 0.1 copy.24
  34.3 0.1 reduce-window.8
  34.4 0.1 reduce
  34.5 0.6 dynamic_slice.17
  35.8 0.2 select_reduce_fusion
  36.0 0.1 reshape.122
  36.2 19.2 %collective-permute-done.1.refs_4_ = f32[2,512]{1,0:T(2,128)S(1)} collective-permute-done((f32[2,512]{1,0:T(2,128)S(1)}, f32[2,512]{1,0:T(2,128)S(1)}, u32[]{:S(2)}, u32[]{:S(2)}) %collective-permute-start.1) | collective-permute-done | bytes 4128 | tf_op jit(solution)/shard_map/ppermute | solution.py:199
  55.4 5.2 %shard_map.96 = (bf16[1024,128]{1,0:T(8,128)(2,1)S(1)}, bf16[1280,128]{1,0:T(8,128)(2,1)S(1)}, f32[256,128]{1,0:T(8,128)S(1)}, bf16[2,2,512,128]{3,2,1,0:T(8,128)(2,1)}) custom-call(s32[3,512]{1,0:T(4,128)S(1)} %concatenate.7.refs_0_, bf16[2304,128]{1,0:T(8,128)(2,1)S(1)} %get-tuple-element.18.refs_1_, bf16[2304,128]{1,0:T(8,128)(2,1)S(1)} %collective-permute-done.refs_2_, ...), custom_call_target="tpu_custom_call" | custom-call | tf_op jit(solution)/shard_map/pallas_call | solution.py:275
  60.6 13.4 %all-to-all-start.2 = ((bf16[256,8,128]{2,1,0:T(8,128)(2,1)}), bf16[256,8,128]{2,1,0:T(8,128)(2,1)S(1)}, u32[]{:S(2)}, u32[]{:S(2)}) async-start(bf16[256,8,128]{2,1,0:T(8,128)(2,1)} %bitcast.22), calls=%async_computation.2 | async-start | bytes 1048576 | tf_op jit(solution)/shard_map/all_to_all | solution.py:203
  74.0 1.6 %collective-permute-start.2 = (bf16[1280,128]{1,0:T(8,128)(2,1)S(1)}, bf16[1280,128]{1,0:T(8,128)(2,1)S(1)}, u32[]{:S(2)}, u32[]{:S(2)}) collective-permute-start(bf16[1280,128]{1,0:T(8,128)(2,1)S(1)} %get-tuple-element.11), channel_id=1, source_target_pairs={{0,16},{16,0},{32,48},{48,32},{64,80},{80,64},{96,112},{112,96},{1... | collective-permute-start | bytes 983048 | tf_op jit(solution)/shard_map/ppermute | solution.py:199
  75.5 17.2 %collective-permute-done.2 = bf16[1280,128]{1,0:T(8,128)(2,1)S(1)} collective-permute-done((bf16[1280,128]{1,0:T(8,128)(2,1)S(1)}, bf16[1280,128]{1,0:T(8,128)(2,1)S(1)}, u32[]{:S(2)}, u32[]{:S(2)}) %collective-permute-start.2) | collective-permute-done | bytes 327712 | tf_op jit(solution)/shard_map/ppermute | solution.py:199
  92.8 2.4 %all-to-all-done.2 = bf16[256,8,128]{2,1,0:T(8,128)(2,1)S(1)} async-done(((bf16[256,8,128]{2,1,0:T(8,128)(2,1)}), bf16[256,8,128]{2,1,0:T(8,128)(2,1)S(1)}, u32[]{:S(2)}, u32[]{:S(2)}) %all-to-all-start.2) | async-done | bytes 524320 | tf_op jit(solution)/shard_map/all_to_all | solution.py:203
  95.2 1.2 %shard_map.97 = bf16[32,2,8,128]{3,2,1,0:T(8,128)(2,1)} custom-call(s32[1,128]{1,0:T(1,128)S(1)} %select_n.85.table_ref, bf16[32,8,8,128]{3,2,1,0:T(8,128)(2,1)S(1)} %bitcast.62), custom_call_target="tpu_custom_call" | custom-call | tf_op jit(solution)/shard_map/pallas_call | solution.py:304
  96.5 5.5 %all-to-all-start.3 = ((bf16[32,2,8,128]{3,2,1,0:T(8,128)(2,1)}), bf16[32,2,8,128]{3,2,1,0:T(8,128)(2,1)S(1)}, u32[]{:S(2)}, u32[]{:S(2)}) async-start(bf16[32,2,8,128]{3,2,1,0:T(8,128)(2,1)} %shard_map.97), calls=%async_computation.3 | async-start | bytes 262144 | tf_op jit(solution)/shard_map/all_to_all | solution.py:203
  102.0 0.9 copy.30
  102.9 6.7 %all-to-all-done.3 = bf16[32,2,8,128]{3,2,1,0:T(8,128)(2,1)S(1)} async-done(((bf16[32,2,8,128]{3,2,1,0:T(8,128)(2,1)}), bf16[32,2,8,128]{3,2,1,0:T(8,128)(2,1)S(1)}, u32[]{:S(2)}, u32[]{:S(2)}) %all-to-all-start.3) | async-done | bytes 131104 | tf_op jit(solution)/shard_map/all_to_all | solution.py:203
  109.7 0.1 copy.38
  109.8 0.7 slice_bitcast_fusion
  (33 shorter events, 0.6 us)
Async XLA Ops:
  0.6 10.5 %copy-start.3 = (bf16[64,32,128]{2,1,0:T(8,128)(2,1)S(1)}, bf16[64,32,128]{2,1,0:T(8,128)(2,1)}, u32[]{:S(2)}) copy-start(bf16[64,32,128]{2,1,0:T(8,128)(2,1)} %param.7) | copy-start | bytes 1572868
  0.6 10.6 %copy-start = (bf16[64,32,128]{2,1,0:T(8,128)(2,1)S(1)}, bf16[64,32,128]{2,1,0:T(8,128)(2,1)}, u32[]{:S(2)}) copy-start(bf16[64,32,128]{2,1,0:T(8,128)(2,1)} %grad_ref.1) | copy-start | bytes 1572868
  2.3 9.8 %copy-start.5 = (s32[16,2]{0,1:T(2,128)S(1)}, s32[16,2]{0,1:T(2,128)}, u32[]{:S(2)}) copy-start(s32[16,2]{0,1:T(2,128)} %param.12) | copy-start | bytes 388
  2.3 16.4 %all-to-all-start = ((bf16[32,2,8,128]{3,2,1,0:T(8,128)(2,1)}), bf16[32,2,8,128]{3,2,1,0:T(8,128)(2,1)S(1)}, u32[]{:S(2)}, u32[]{:S(2)}) async-start(bf16[32,2,8,128]{3,2,1,0:T(8,128)(2,1)} %bitcast.59), calls=%async_computation | async-start | bytes 262144 | tf_op jit(solution)/shard_map/all_to_all | solution.py:203
  20.1 10.8 %copy-start.2 = (bf16[2,2,64,8,128]{4,3,2,1,0:T(8,128)(2,1)S(1)}, bf16[2,2,64,8,128]{4,3,2,1,0:T(8,128)(2,1)}, u32[]{:S(2)}) copy-start(bf16[2,2,64,8,128]{4,3,2,1,0:T(8,128)(2,1)} %copy.26) | copy-start | bytes 1572868
  20.1 35.2 %all-to-all-start.1 = ((bf16[256,8,128]{2,1,0:T(8,128)(2,1)}), bf16[256,8,128]{2,1,0:T(8,128)(2,1)S(1)}, u32[]{:S(2)}, u32[]{:S(2)}) async-start(bf16[256,8,128]{2,1,0:T(8,128)(2,1)} %bitcast.20), calls=%async_computation.1 | async-start | bytes 1048576 | tf_op jit(solution)/shard_map/all_to_all | solution.py:203
  31.0 2.4 %copy-start.1 = (bf16[64,32,128]{2,1,0:T(8,128)(2,1)S(1)}, bf16[64,32,128]{2,1,0:T(8,128)(2,1)}, u32[]{:S(2)}) copy-start(bf16[64,32,128]{2,1,0:T(8,128)(2,1)} %out_ref.1) | copy-start | bytes 1572868
  31.1 3.1 %copy-start.4 = (s32[64]{0:T(128)S(1)}, s32[64]{0:T(128)}, u32[]{:S(2)}) copy-start(s32[64]{0:T(128)} %param.13) | copy-start | bytes 772
  32.0 23.4 %collective-permute-start = (bf16[2304,128]{1,0:T(8,128)(2,1)}, bf16[2304,128]{1,0:T(8,128)(2,1)S(1)}, u32[]{:S(2)}, u32[]{:S(2)}) collective-permute-start(bf16[2304,128]{1,0:T(8,128)(2,1)} %get-tuple-element.17), channel_id=1, source_target_pairs={{0,16},{16,0},{32,48},{48,32},{64,80},{80,64},{96,112},{112,96},{1... | collective-permute-start | bytes 1769480 | tf_op jit(solution)/shard_map/ppermute | solution.py:199
  33.9 21.5 %collective-permute-start.1 = (f32[2,512]{1,0:T(2,128)S(1)}, f32[2,512]{1,0:T(2,128)S(1)}, u32[]{:S(2)}, u32[]{:S(2)}) collective-permute-start(f32[2,512]{1,0:T(2,128)S(1)} %get-tuple-element.25), channel_id=1, source_target_pairs={{0,16},{16,0},{32,48},{48,32},{64,80},{80,64},{96,112},{112,96},{1... | collective-permute-start | bytes 12296 | tf_op jit(solution)/shard_map/ppermute | solution.py:199
  60.6 34.6 %all-to-all-start.2 = ((bf16[256,8,128]{2,1,0:T(8,128)(2,1)}), bf16[256,8,128]{2,1,0:T(8,128)(2,1)S(1)}, u32[]{:S(2)}, u32[]{:S(2)}) async-start(bf16[256,8,128]{2,1,0:T(8,128)(2,1)} %bitcast.22), calls=%async_computation.2 | async-start | bytes 1048576 | tf_op jit(solution)/shard_map/all_to_all | solution.py:203
  74.0 18.7 %collective-permute-start.2 = (bf16[1280,128]{1,0:T(8,128)(2,1)S(1)}, bf16[1280,128]{1,0:T(8,128)(2,1)S(1)}, u32[]{:S(2)}, u32[]{:S(2)}) collective-permute-start(bf16[1280,128]{1,0:T(8,128)(2,1)S(1)} %get-tuple-element.11), channel_id=1, source_target_pairs={{0,16},{16,0},{32,48},{48,32},{64,80},{80,64},{96,112},{112,96},{1... | collective-permute-start | bytes 983048 | tf_op jit(solution)/shard_map/ppermute | solution.py:199
  96.5 13.2 %all-to-all-start.3 = ((bf16[32,2,8,128]{3,2,1,0:T(8,128)(2,1)}), bf16[32,2,8,128]{3,2,1,0:T(8,128)(2,1)S(1)}, u32[]{:S(2)}, u32[]{:S(2)}) async-start(bf16[32,2,8,128]{3,2,1,0:T(8,128)(2,1)} %shard_map.97), calls=%async_computation.3 | async-start | bytes 262144 | tf_op jit(solution)/shard_map/all_to_all | solution.py:203
